TPU v7x, 128 devices: a whole 4x4x4 slice. The times are simulated.
128 devices in a mesh: gy: 2 (over y_hi), gx: 64 (over x, y_lo, z, core).
Axes of the slice: x: 4, y: 4 (y_hi: 2, y_lo: 2; y = y_hi * 2 + y_lo), z: 4, core: 2. Of those that a mesh axis runs over, the one named last changes fastest.
Arguments:
- radar_frame: bfloat16 [256, 1024, 128], P('gy', 'gx'), may hold values from -6 to 6
- lstm_state: bfloat16 [256, 1024, 128], P('gy', 'gx'), may hold values from -6 to 6
- w_conv: bfloat16 [3, 3, 192, 256], replicated, may hold values from -0.15625 to 0.15625
- b_gates: float32 [256], replicated, may hold values from -6 to 6
- norm_gain: float32 [64], replicated, may hold values from 0.5 to 2
- w_qkv: bfloat16 [64, 384], replicated, may hold values from -1 to 1
- w_out: bfloat16 [128, 64], replicated, may hold values from -1.25 to 1.25
- state_grad: bfloat16 [256, 1024, 128], P('gy', 'gx'), may hold values from -6 to 6
Outputs:
- new_state: bfloat16 [256, 1024, 128], P('gy', 'gx')
- grad_frame: bfloat16 [256, 1024, 128], P('gy', 'gx')
- grad_state: bfloat16 [256, 1024, 128], P('gy', 'gx')
All inputs are finite; a program needn't handle non-finite values.
Results may differ from a plain program's by a relative error of at most 0.014.
The roundings to bfloat16 on the way count: a program that leaves them out, or rounds other values in their place, can miss the bound.
Values may be sent and summed in bfloat16 or wider, within the bound.
No kernel may reach another device: no remote copies, remote signals or barrier semaphores. Data moves between devices by JAX's collectives and lax.ppermute only.
A program may use at most 128 MiB of HBM per device.

v0:
```python
import jax
import jax.numpy as jnp
from jax import lax
from jax.sharding import PartitionSpec as P

HEADS = 8


EPS = 1e-05


def with_halo(block, sides, width):
    for axis, dim in sides:
        count = lax.axis_size(axis)
        forward = [(i, i + 1) for i in range(count - 1)]
        backward = [(target, source) for source, target in forward]
        low = lax.ppermute(
            lax.slice_in_dim(block, block.shape[dim] - width, None, axis=dim), axis, forward
        )
        high = lax.ppermute(lax.slice_in_dim(block, 0, width, axis=dim), axis, backward)
        block = jnp.concatenate([low, block, high], axis=dim)
    return block


def conv_forward(padded, w_conv, row_count, col_count):
    channels = padded.shape[2]
    total = jnp.zeros((row_count * col_count, w_conv.shape[3]), jnp.float32)
    for row_tap in range(3):
        for col_tap in range(3):
            window = padded[row_tap : row_tap + row_count, col_tap : col_tap + col_count].reshape(
                -1, channels
            )
            total = total + jnp.dot(
                window, w_conv[row_tap, col_tap], preferred_element_type=jnp.float32
            )
    return total.reshape(row_count, col_count, -1)


def conv_backward(padded_grad, w_conv, row_count, col_count):
    gate_dim = padded_grad.shape[2]
    total = jnp.zeros((row_count * col_count, w_conv.shape[2]), jnp.float32)
    for row_tap in range(3):
        for col_tap in range(3):
            window = padded_grad[
                2 - row_tap : 2 - row_tap + row_count, 2 - col_tap : 2 - col_tap + col_count
            ].reshape(-1, gate_dim)
            total = total + jnp.dot(
                window, w_conv[row_tap, col_tap].T, preferred_element_type=jnp.float32
            )
    return total.reshape(row_count, col_count, -1)


def to_items(tensor):
    count, length, width = tensor.shape
    head_size = width // HEADS
    return (
        tensor.reshape(count, length, HEADS, head_size)
        .transpose(0, 2, 1, 3)
        .reshape(count * HEADS, length, head_size)
    )


def from_items(tensor, count):
    length, head_size = (tensor.shape[1], tensor.shape[2])
    return (
        tensor.reshape(count, HEADS, length, head_size)
        .transpose(0, 2, 1, 3)
        .reshape(count, length, HEADS * head_size)
    )


def grouped(func, arrays):
    total = arrays[0].shape[0]
    group_size = 4
    shaped = tuple(
        (member.reshape((total // group_size, group_size) + member.shape[1:]) for member in arrays)
    )
    result = lax.map(func, shaped)
    return tuple((answer.reshape((total,) + answer.shape[2:]) for answer in result))


def item_probs(queries, key_items):
    scores = jnp.einsum(
        "gqd,gkd->gqk", queries, key_items, preferred_element_type=jnp.float32
    ) * queries.shape[-1] ** (-0.5)
    exp_scores = jnp.exp(scores)
    return exp_scores / jnp.sum(exp_scores, axis=-1, keepdims=True)


def attend_forward(pieces):
    queries, key_items, value_items = pieces
    probs = item_probs(queries, key_items)
    attended = jnp.einsum(
        "gqk,gkd->gqd", probs.astype(jnp.bfloat16), value_items, preferred_element_type=jnp.float32
    )
    return (attended.astype(jnp.bfloat16),)


def attend_backward(pieces):
    queries, key_items, value_items, grad_items = pieces
    scale = queries.shape[-1] ** (-0.5)
    probs = item_probs(queries, key_items)
    grad_value = jnp.einsum(
        "gqk,gqd->gkd", probs.astype(jnp.bfloat16), grad_items, preferred_element_type=jnp.float32
    )
    grad_prob = jnp.einsum(
        "gqd,gkd->gqk", grad_items, value_items, preferred_element_type=jnp.float32
    )
    inner = jnp.sum(probs * grad_prob, axis=-1, keepdims=True)
    grad_score = (probs * (grad_prob - inner)).astype(jnp.bfloat16)
    grad_query = (
        jnp.einsum("gqk,gkd->gqd", grad_score, key_items, preferred_element_type=jnp.float32)
        * scale
    )
    grad_key = (
        jnp.einsum("gqk,gqd->gkd", grad_score, queries, preferred_element_type=jnp.float32) * scale
    )
    return (
        grad_query.astype(jnp.bfloat16),
        grad_key.astype(jnp.bfloat16),
        grad_value.astype(jnp.bfloat16),
    )


def on_device(radar_frame, lstm_state, w_conv, b_gates, norm_gain, w_qkv, w_out, state_grad):
    row_count, col_count, in_channels = radar_frame.shape
    hidden_dim = lstm_state.shape[2] // 2
    attn_dim = w_out.shape[0]
    qkv_width = w_qkv.shape[1]
    h_prev = lstm_state[..., :hidden_dim]
    c_prev = lstm_state[..., hidden_dim:].astype(jnp.float32)
    inputs = jnp.concatenate([radar_frame, h_prev], axis=-1)
    padded = with_halo(inputs, (("gy", 0), ("gx", 1)), 1)
    gates = conv_forward(padded, w_conv, row_count, col_count) + b_gates
    in_gate = jax.nn.sigmoid(gates[..., :hidden_dim])
    forget = jax.nn.sigmoid(gates[..., hidden_dim : 2 * hidden_dim])
    out_gate = jax.nn.sigmoid(gates[..., 2 * hidden_dim : 3 * hidden_dim])
    update = jnp.tanh(gates[..., 3 * hidden_dim :])
    c_new = forget * c_prev + in_gate * update
    cell_tanh = jnp.tanh(c_new)
    h_new = out_gate * cell_tanh
    inv_rms = lax.rsqrt(jnp.mean(h_new * h_new, axis=-1, keepdims=True) + EPS)
    normed = (h_new * inv_rms * norm_gain).astype(jnp.bfloat16)
    qkv_local = jnp.dot(
        normed.reshape(-1, hidden_dim), w_qkv, preferred_element_type=jnp.float32
    ).astype(jnp.bfloat16)
    qkv_rows = lax.all_to_all(
        qkv_local.reshape(row_count, col_count * qkv_width),
        "gx",
        split_axis=0,
        concat_axis=1,
        tiled=True,
    )
    qkv_rows = qkv_rows.reshape(qkv_rows.shape[0], -1, qkv_width)
    line_count = qkv_rows.shape[0]
    query_items = to_items(qkv_rows[..., :attn_dim])
    key_items = to_items(qkv_rows[..., attn_dim : 2 * attn_dim])
    value_items = to_items(qkv_rows[..., 2 * attn_dim :])
    (attended_items,) = grouped(attend_forward, (query_items, key_items, value_items))
    attended_rows = from_items(attended_items, line_count)
    attended = lax.all_to_all(
        attended_rows.reshape(line_count, -1), "gx", split_axis=1, concat_axis=0, tiled=True
    )
    attended = attended.reshape(row_count * col_count, attn_dim)
    mixed = h_new + jnp.dot(attended, w_out, preferred_element_type=jnp.float32).reshape(
        row_count, col_count, hidden_dim
    )
    new_state = jnp.concatenate([mixed, c_new], axis=-1).astype(jnp.bfloat16)
    grad_mixed = state_grad[..., :hidden_dim]
    grad_attended = jnp.dot(
        grad_mixed.reshape(-1, hidden_dim), w_out.T, preferred_element_type=jnp.float32
    ).astype(jnp.bfloat16)
    grad_rows = lax.all_to_all(
        grad_attended.reshape(row_count, col_count * attn_dim),
        "gx",
        split_axis=0,
        concat_axis=1,
        tiled=True,
    )
    grad_rows = grad_rows.reshape(line_count, -1, attn_dim)
    grad_query, grad_key, grad_value = grouped(
        attend_backward, (query_items, key_items, value_items, to_items(grad_rows))
    )
    grad_qkv_rows = jnp.concatenate(
        [
            from_items(grad_query, line_count),
            from_items(grad_key, line_count),
            from_items(grad_value, line_count),
        ],
        axis=-1,
    )
    grad_qkv = lax.all_to_all(
        grad_qkv_rows.reshape(line_count, -1), "gx", split_axis=1, concat_axis=0, tiled=True
    )
    grad_normed = jnp.dot(
        grad_qkv.reshape(-1, qkv_width), w_qkv.T, preferred_element_type=jnp.float32
    )
    grad_normed = grad_normed.reshape(row_count, col_count, hidden_dim)
    scaled = grad_normed * norm_gain
    grad_hidden = (
        grad_mixed.astype(jnp.float32)
        + inv_rms * scaled
        - h_new * inv_rms**3 * jnp.mean(scaled * h_new, axis=-1, keepdims=True)
    )
    grad_cell = state_grad[..., hidden_dim:].astype(jnp.float32) + grad_hidden * out_gate * (
        1.0 - cell_tanh * cell_tanh
    )
    grad_gates = jnp.concatenate(
        [
            grad_cell * update * in_gate * (1.0 - in_gate),
            grad_cell * c_prev * forget * (1.0 - forget),
            grad_hidden * cell_tanh * out_gate * (1.0 - out_gate),
            grad_cell * in_gate * (1.0 - update * update),
        ],
        axis=-1,
    ).astype(jnp.bfloat16)
    padded_grad = with_halo(grad_gates, (("gy", 0), ("gx", 1)), 1)
    grad_inputs = conv_backward(padded_grad, w_conv, row_count, col_count)
    grad_frame = grad_inputs[..., :in_channels].astype(jnp.bfloat16)
    grad_state = jnp.concatenate(
        [grad_inputs[..., in_channels:], grad_cell * forget], axis=-1
    ).astype(jnp.bfloat16)
    return (new_state, grad_frame, grad_state)


def solution(mesh):
    in_specs = (
        P("gy", "gx", None),
        P("gy", "gx", None),
        P(),
        P(),
        P(),
        P(),
        P(),
        P("gy", "gx", None),
    )
    out_specs = (P("gy", "gx", None), P("gy", "gx", None), P("gy", "gx", None))
    return jax.shard_map(
        on_device, mesh=mesh, in_specs=in_specs, out_specs=out_specs, check_vma=False
    )
```

profile of v0, /device:TPU:2, one launch (start us, length us, event | category | flops | bytes accessed | tf_op | source)
XLA Modules:
  0.0 403.9 jit_solution(1212646908281484311)
XLA Ops:
  12.0 9.0 %all-to-all-start.2 = ((bf16[64,2,2048]{2,1,0:T(2,128)(2,1)}), bf16[64,2,2048]{2,1,0:T(2,128)(2,1)S(1)}, u32[]{:S(2)}, u32[]{:S(2)}) async-start(bf16[64,2,2048]{2,1,0:T(2,128)(2,1)} %all_to_all.54), calls=%async_computation.2 | async-start | bytes 1048576 | tf_op jit(solution)/shard_map/all_to_all | solution.py:173
  24.2 6.7 %collective-permute-start.3 = (bf16[130,1,192]{2,0,1:T(8,128)(2,1)S(1)}, bf16[130,1,192]{2,0,1:T(8,128)(2,1)S(1)}, u32[]{:S(2)}, u32[]{:S(2)}) collective-permute-start(bf16[130,1,192]{2,0,1:T(8,128)(2,1)S(1)} %get-tuple-element.154), channel_id=1, source_target_pairs={{1,0},{2,1},{3,2},{4,3},{5,4},{6,5},{7,6},{8,7},{9,8},{10,9},{11,1... | collective-permute-start | bytes 149768 | tf_op jit(solution)/shard_map/ppermute | solution.py:20
  51.2 9.4 %all-to-all-start = ((bf16[64,2,6144]{2,1,0:T(2,128)(2,1)}), bf16[64,2,6144]{2,1,0:T(2,128)(2,1)S(1)}, u32[]{:S(2)}, u32[]{:S(2)}) async-start(bf16[64,2,6144]{2,1,0:T(2,128)(2,1)} %all_to_all.48), calls=%async_computation | async-start | bytes 3145728 | tf_op jit(solution)/shard_map/all_to_all | solution.py:147
  70.5 12.5 %all-to-all-done = bf16[64,2,6144]{2,1,0:T(2,128)(2,1)S(1)} async-done(((bf16[64,2,6144]{2,1,0:T(2,128)(2,1)}), bf16[64,2,6144]{2,1,0:T(2,128)(2,1)S(1)}, u32[]{:S(2)}, u32[]{:S(2)}) %all-to-all-start) | async-done | bytes 1572896 | tf_op jit(solution)/shard_map/all_to_all | solution.py:147
  85.2 22.1 %while.24 = (s32[]{:T(128)}, bf16[4,4,1024,16]{2,3,1,0:T(8,128)(2,1)S(1)}, bf16[4,4,1024,16]{2,3,1,0:T(8,128)(2,1)S(1)}, bf16[4,4,1024,16]{2,3,1,0:T(8,128)(2,1)...) while((s32[]{:T(128)}, bf16[4,4,1024,16]{2,3,1,0:T(8,128)(2,1)S(1)}, ...), condition=%wide.region_3.4_spmd, body=%wide.region_1.3_spmd.sunk | while | flops 289468416 | bytes 34113604 | solution.py:78
  111.5 8.2 %all_to_all.51 = bf16[2,64,2048]{2,1,0:T(8,128)(2,1)S(1)} reshape(bf16[2,1024,8,16]{3,2,1,0:T(8,128)(2,1)} %bitcast.228) | data formatting | bytes 1048576 | tf_op jit(solution)/shard_map/all_to_all | solution.py:161
  121.0 6.7 %all-to-all-start.1 = ((bf16[2,64,2048]{2,0,1:T(2,128)(2,1)}), bf16[2,64,2048]{2,0,1:T(2,128)(2,1)}, u32[]{:S(2)}, u32[]{:S(2)}) async-start(bf16[2,64,2048]{2,0,1:T(2,128)(2,1)} %copy.168), calls=%async_computation.1 | async-start | bytes 1048576 | tf_op jit(solution)/shard_map/all_to_all | solution.py:161
  127.8 153.3 %while.25 = (s32[]{:T(128)}, bf16[4,4,1024,16]{2,3,1,0:T(8,128)(2,1)S(1)}, bf16[4,4,1024,16]{2,3,1,0:T(8,128)(2,1)S(1)}, bf16[4,4,1024,16]{2,3,1,0:T(8,128)(2,1)...) while((s32[]{:T(128)}, ...), condition=%wide.region_7.8_spmd, body=%wide.region_4.7_spmd.sunk | while | flops 730128384 | bytes 230003888 | solution.py:78
  130.7 9.7 %multiply_reduce_fusion.4 = (f32[4,1024]{1,0:T(4,128)S(1)}, f32[4,1024,1024]{1,2,0:T(8,128)}) fusion(f32[4,1024]{1,0:T(4,128)S(1)} %get-tuple-element.262, f32[4,1024,1024]{1,2,0:T(8,128)S(1)} %get-tuple-element.263, bf16[4,4,1024,16]{2,3,1,0:T(8,128)(2,1)} %get-tuple-element.291, s32[]{:T(128)} %get-tuple-element.275, ...), kind=kOutput, calls=%fused_computation.18.clone.1 | convolution fusion | flops 150990848 | bytes 33850368 | tf_op jit(solution)/shard_map/while/body/eval_jaxpr/gqd,gkd->gqk/dot_general | solution.py:106
  141.6 10.4 %multiply_convert_fusion.7 = bf16[4,1024,1024]{1,2,0:T(8,128)(2,1)} fusion(f32[4,1024,1024]{1,2,0:T(8,128)} %get-tuple-element.264, f32[4,1024]{1,0:T(4,128)S(1)} %get-tuple-element.265, f32[4,1024]{1,0:T(4,128)S(1)} %get-tuple-element.262, f32[4,1024,1024]{1,2,0:T(8,128)S(1)} %get-tuple-element.263), kind=kLoop, calls=%fused_computation.17.clone.1 | loop fusion | flops 20971520 | bytes 41975808 | tf_op jit(solution)/shard_map/while/body/eval_jaxpr/convert_element_type | solution.py:110
  159.0 7.2 %fusion.180 = bf16[4,4,1024,16]{2,3,1,0:T(8,128)(2,1)S(1)} fusion(bf16[4,4,1024,16]{2,3,1,0:T(8,128)(2,1)S(1)} %get-tuple-element.278, s32[]{:T(128)} %get-tuple-element.275, bf16[4,4,1024,16]{2,3,1,0:T(8,128)(2,1)S(1)} %copy-done.29, f32[4,1024,1024]{1,2,0:T(8,128)} %copy-done.1, f32[4,1024]{1,0:T(4,128)S(1)} %get-tuple-element.262), kind=kOutput, calls=%fused_computation.30.clone.1 | convolution fusion | flops 146866176 | bytes 17056768 | tf_op jit(solution)/shard_map/while/body/eval_jaxpr/gqk,gqd->gkd/dot_general | solution.py:103
  169.0 9.7 %multiply_reduce_fusion.4 = (f32[4,1024]{1,0:T(4,128)S(1)}, f32[4,1024,1024]{1,2,0:T(8,128)}) fusion(f32[4,1024]{1,0:T(4,128)S(1)} %get-tuple-element.262, f32[4,1024,1024]{1,2,0:T(8,128)S(1)} %get-tuple-element.263, bf16[4,4,1024,16]{2,3,1,0:T(8,128)(2,1)} %get-tuple-element.291, s32[]{:T(128)} %get-tuple-element.275, ...), kind=kOutput, calls=%fused_computation.18.clone.1 | convolution fusion | flops 150990848 | bytes 33850368 | tf_op jit(solution)/shard_map/while/body/eval_jaxpr/gqd,gkd->gqk/dot_general | solution.py:106
  179.9 10.4 %multiply_convert_fusion.7 = bf16[4,1024,1024]{1,2,0:T(8,128)(2,1)} fusion(f32[4,1024,1024]{1,2,0:T(8,128)} %get-tuple-element.264, f32[4,1024]{1,0:T(4,128)S(1)} %get-tuple-element.265, f32[4,1024]{1,0:T(4,128)S(1)} %get-tuple-element.262, f32[4,1024,1024]{1,2,0:T(8,128)S(1)} %get-tuple-element.263), kind=kLoop, calls=%fused_computation.17.clone.1 | loop fusion | flops 20971520 | bytes 41975808 | tf_op jit(solution)/shard_map/while/body/eval_jaxpr/convert_element_type | solution.py:110
  197.3 7.2 %fusion.180 = bf16[4,4,1024,16]{2,3,1,0:T(8,128)(2,1)S(1)} fusion(bf16[4,4,1024,16]{2,3,1,0:T(8,128)(2,1)S(1)} %get-tuple-element.278, s32[]{:T(128)} %get-tuple-element.275, bf16[4,4,1024,16]{2,3,1,0:T(8,128)(2,1)S(1)} %copy-done.29, f32[4,1024,1024]{1,2,0:T(8,128)} %copy-done.1, f32[4,1024]{1,0:T(4,128)S(1)} %get-tuple-element.262), kind=kOutput, calls=%fused_computation.30.clone.1 | convolution fusion | flops 146866176 | bytes 17056768 | tf_op jit(solution)/shard_map/while/body/eval_jaxpr/gqk,gqd->gkd/dot_general | solution.py:103
  207.4 9.7 %multiply_reduce_fusion.4 = (f32[4,1024]{1,0:T(4,128)S(1)}, f32[4,1024,1024]{1,2,0:T(8,128)}) fusion(f32[4,1024]{1,0:T(4,128)S(1)} %get-tuple-element.262, f32[4,1024,1024]{1,2,0:T(8,128)S(1)} %get-tuple-element.263, bf16[4,4,1024,16]{2,3,1,0:T(8,128)(2,1)} %get-tuple-element.291, s32[]{:T(128)} %get-tuple-element.275, ...), kind=kOutput, calls=%fused_computation.18.clone.1 | convolution fusion | flops 150990848 | bytes 33850368 | tf_op jit(solution)/shard_map/while/body/eval_jaxpr/gqd,gkd->gqk/dot_general | solution.py:106
  218.2 10.4 %multiply_convert_fusion.7 = bf16[4,1024,1024]{1,2,0:T(8,128)(2,1)} fusion(f32[4,1024,1024]{1,2,0:T(8,128)} %get-tuple-element.264, f32[4,1024]{1,0:T(4,128)S(1)} %get-tuple-element.265, f32[4,1024]{1,0:T(4,128)S(1)} %get-tuple-element.262, f32[4,1024,1024]{1,2,0:T(8,128)S(1)} %get-tuple-element.263), kind=kLoop, calls=%fused_computation.17.clone.1 | loop fusion | flops 20971520 | bytes 41975808 | tf_op jit(solution)/shard_map/while/body/eval_jaxpr/convert_element_type | solution.py:110
  235.7 7.2 %fusion.180 = bf16[4,4,1024,16]{2,3,1,0:T(8,128)(2,1)S(1)} fusion(bf16[4,4,1024,16]{2,3,1,0:T(8,128)(2,1)S(1)} %get-tuple-element.278, s32[]{:T(128)} %get-tuple-element.275, bf16[4,4,1024,16]{2,3,1,0:T(8,128)(2,1)S(1)} %copy-done.29, f32[4,1024,1024]{1,2,0:T(8,128)} %copy-done.1, f32[4,1024]{1,0:T(4,128)S(1)} %get-tuple-element.262), kind=kOutput, calls=%fused_computation.30.clone.1 | convolution fusion | flops 146866176 | bytes 17056768 | tf_op jit(solution)/shard_map/while/body/eval_jaxpr/gqk,gqd->gkd/dot_general | solution.py:103
  245.7 9.7 %multiply_reduce_fusion.4 = (f32[4,1024]{1,0:T(4,128)S(1)}, f32[4,1024,1024]{1,2,0:T(8,128)}) fusion(f32[4,1024]{1,0:T(4,128)S(1)} %get-tuple-element.262, f32[4,1024,1024]{1,2,0:T(8,128)S(1)} %get-tuple-element.263, bf16[4,4,1024,16]{2,3,1,0:T(8,128)(2,1)} %get-tuple-element.291, s32[]{:T(128)} %get-tuple-element.275, ...), kind=kOutput, calls=%fused_computation.18.clone.1 | convolution fusion | flops 150990848 | bytes 33850368 | tf_op jit(solution)/shard_map/while/body/eval_jaxpr/gqd,gkd->gqk/dot_general | solution.py:106
  256.6 10.4 %multiply_convert_fusion.7 = bf16[4,1024,1024]{1,2,0:T(8,128)(2,1)} fusion(f32[4,1024,1024]{1,2,0:T(8,128)} %get-tuple-element.264, f32[4,1024]{1,0:T(4,128)S(1)} %get-tuple-element.265, f32[4,1024]{1,0:T(4,128)S(1)} %get-tuple-element.262, f32[4,1024,1024]{1,2,0:T(8,128)S(1)} %get-tuple-element.263), kind=kLoop, calls=%fused_computation.17.clone.1 | loop fusion | flops 20971520 | bytes 41975808 | tf_op jit(solution)/shard_map/while/body/eval_jaxpr/convert_element_type | solution.py:110
  274.0 7.2 %fusion.180 = bf16[4,4,1024,16]{2,3,1,0:T(8,128)(2,1)S(1)} fusion(bf16[4,4,1024,16]{2,3,1,0:T(8,128)(2,1)S(1)} %get-tuple-element.278, s32[]{:T(128)} %get-tuple-element.275, bf16[4,4,1024,16]{2,3,1,0:T(8,128)(2,1)S(1)} %copy-done.29, f32[4,1024,1024]{1,2,0:T(8,128)} %copy-done.1, f32[4,1024]{1,0:T(4,128)S(1)} %get-tuple-element.262), kind=kOutput, calls=%fused_computation.30.clone.1 | convolution fusion | flops 146866176 | bytes 17056768 | tf_op jit(solution)/shard_map/while/body/eval_jaxpr/gqk,gqd->gkd/dot_general | solution.py:103
  285.7 9.2 %all-to-all-start.3 = ((bf16[2,64,6144]{2,0,1:T(2,128)(2,1)}), bf16[2,64,6144]{2,0,1:T(2,128)(2,1)}, u32[]{:S(2)}, u32[]{:S(2)}) async-start(bf16[2,64,6144]{2,0,1:T(2,128)(2,1)} %copy.176), calls=%async_computation.3 | async-start | bytes 3145728 | tf_op jit(solution)/shard_map/all_to_all | solution.py:192
  300.7 16.5 %all-to-all-done.3 = bf16[2,64,6144]{2,0,1:T(2,128)(2,1)} async-done(((bf16[2,64,6144]{2,0,1:T(2,128)(2,1)}), bf16[2,64,6144]{2,0,1:T(2,128)(2,1)}, u32[]{:S(2)}, u32[]{:S(2)}) %all-to-all-start.3) | async-done | bytes 1572896 | tf_op jit(solution)/shard_map/all_to_all | solution.py:192
  330.9 6.6 %collective-permute-start.4 = (bf16[1,16,256]{2,1,0:T(8,128)(2,1)S(1)}, bf16[1,16,256]{2,1,0:T(8,128)(2,1)S(1)}, u32[]{:S(2)}, u32[]{:S(2)}) collective-permute-start(bf16[1,16,256]{2,1,0:T(8,128)(2,1)S(1)} %copy.178), channel_id=1, source_target_pairs={{0,64},{1,65},{2,66},{3,67},{4,68},{5,69},{6,70},{7,71},{8,72},{9,... | collective-permute-start | bytes 24584 | tf_op jit(solution)/shard_map/ppermute | solution.py:17
  361.2 7.7 %maximum_maximum_fusion = (bf16[130,17,256]{0,2,1:T(8,128)(2,1)}, bf16[130,17,256]{0,2,1:T(8,128)(2,1)S(1)}) fusion(bf16[1,16,256]{0,2,1:T(8,128)(2,1)S(1)} %copy.181, bf16[128,16,64]{0,2,1:T(8,128)(2,1)S(1)} %get-tuple-element.135, bf16[128,16,64]{0,2,1:T(8,128)(2,1)S(1)} %get-tuple-element.129, bf16[128,16,64]{0,2,1:T(8,128)(2,1)S(1)} %get-tuple-element.136, ...), kind=kLoop, calls=%fused_computation.76 | loop fusion | flops 15841280 | bytes 3461120 | tf_op jit(solution)/shard_map/concatenate | solution.py:21
  (241 shorter events, 200.2 us)
Async XLA Ops:
  0.6 48.7 %copy-start = (bf16[64,384]{1,0:T(8,128)(2,1)S(1)}, bf16[64,384]{1,0:T(8,128)(2,1)}, u32[]{:S(2)}) copy-start(bf16[64,384]{1,0:T(8,128)(2,1)} %param.17) | copy-start | bytes 147460
  0.7 8.4 %copy-start.22 = (bf16[128,16,128]{2,1,0:T(8,128)(2,1)S(1)}, bf16[128,16,128]{2,1,0:T(8,128)(2,1)}, u32[]{:S(2)}) copy-start(bf16[128,16,128]{2,1,0:T(8,128)(2,1)} %param.19) | copy-start | bytes 1572868
  2.2 8.6 %copy-start.35 = (bf16[128,64]{0,1:T(8,128)(2,1)S(1)}, bf16[128,64]{0,1:T(8,128)(2,1)}, u32[]{:S(2)}) copy-start(bf16[128,64]{0,1:T(8,128)(2,1)} %param.18) | copy-start | bytes 49156
  2.6 19.5 %collective-permute-start = (bf16[1,16,192]{2,0,1:T(2,128)(2,1)S(1)}, bf16[1,16,192]{2,0,1:T(2,128)(2,1)S(1)}, u32[]{:S(2)}, u32[]{:S(2)}) collective-permute-start(bf16[1,16,192]{2,0,1:T(2,128)(2,1)S(1)} %get-tuple-element.162), channel_id=1, source_target_pairs={{0,64},{1,65},{2,66},{3,67},{4,68},{5,69},{6,70},{7,71},{8,72},{9,... | collective-permute-start | bytes 18440 | tf_op jit(solution)/shard_map/ppermute | solution.py:17
  7.7 14.4 %collective-permute-start.1 = (bf16[1,16,192]{2,0,1:T(2,128)(2,1)S(1)}, bf16[1,16,192]{2,0,1:T(2,128)(2,1)S(1)}, u32[]{:S(2)}, u32[]{:S(2)}) collective-permute-start(bf16[1,16,192]{2,0,1:T(2,128)(2,1)S(1)} %get-tuple-element.163), channel_id=1, source_target_pairs={{64,0},{65,1},{66,2},{67,3},{68,4},{69,5},{70,6},{71,7},{72,8},{73... | collective-permute-start | bytes 18440 | tf_op jit(solution)/shard_map/ppermute | solution.py:20
  12.0 39.2 %all-to-all-start.2 = ((bf16[64,2,2048]{2,1,0:T(2,128)(2,1)}), bf16[64,2,2048]{2,1,0:T(2,128)(2,1)S(1)}, u32[]{:S(2)}, u32[]{:S(2)}) async-start(bf16[64,2,2048]{2,1,0:T(2,128)(2,1)} %all_to_all.54), calls=%async_computation.2 | async-start | bytes 1048576 | tf_op jit(solution)/shard_map/all_to_all | solution.py:173
  22.1 24.6 %copy-start.20 = (bf16[128,16,64]{0,2,1:T(8,128)(2,1)}, bf16[128,16,64]{0,2,1:T(8,128)(2,1)S(1)}, u32[]{:S(2)}) copy-start(bf16[128,16,64]{0,2,1:T(8,128)(2,1)S(1)} %copy.205) | copy-start | bytes 786436
  22.1 10.6 %collective-permute-start.2 = (bf16[130,1,192]{2,0,1:T(8,128)(2,1)S(1)}, bf16[130,1,192]{2,0,1:T(8,128)(2,1)S(1)}, u32[]{:S(2)}, u32[]{:S(2)}) collective-permute-start(bf16[130,1,192]{2,0,1:T(8,128)(2,1)S(1)} %get-tuple-element.155), channel_id=1, source_target_pairs={{0,1},{1,2},{2,3},{3,4},{4,5},{5,6},{6,7},{7,8},{8,9},{9,10},{10,1... | collective-permute-start | bytes 149768 | tf_op jit(solution)/shard_map/ppermute | solution.py:17
  24.2 8.6 %collective-permute-start.3 = (bf16[130,1,192]{2,0,1:T(8,128)(2,1)S(1)}, bf16[130,1,192]{2,0,1:T(8,128)(2,1)S(1)}, u32[]{:S(2)}, u32[]{:S(2)}) collective-permute-start(bf16[130,1,192]{2,0,1:T(8,128)(2,1)S(1)} %get-tuple-element.154), channel_id=1, source_target_pairs={{1,0},{2,1},{3,2},{4,3},{5,4},{6,5},{7,6},{8,7},{9,8},{10,9},{11,1... | collective-permute-start | bytes 149768 | tf_op jit(solution)/shard_map/ppermute | solution.py:20
  51.2 31.7 %all-to-all-start = ((bf16[64,2,6144]{2,1,0:T(2,128)(2,1)}), bf16[64,2,6144]{2,1,0:T(2,128)(2,1)S(1)}, u32[]{:S(2)}, u32[]{:S(2)}) async-start(bf16[64,2,6144]{2,1,0:T(2,128)(2,1)} %all_to_all.48), calls=%async_computation | async-start | bytes 3145728 | tf_op jit(solution)/shard_map/all_to_all | solution.py:147
  121.0 164.7 %all-to-all-start.1 = ((bf16[2,64,2048]{2,0,1:T(2,128)(2,1)}), bf16[2,64,2048]{2,0,1:T(2,128)(2,1)}, u32[]{:S(2)}, u32[]{:S(2)}) async-start(bf16[2,64,2048]{2,0,1:T(2,128)(2,1)} %copy.168), calls=%async_computation.1 | async-start | bytes 1048576 | tf_op jit(solution)/shard_map/all_to_all | solution.py:161
  130.7 10.9 %copy-start.1 = (f32[4,1024,1024]{1,2,0:T(8,128)}, f32[4,1024,1024]{1,2,0:T(8,128)S(1)}, u32[]{:S(2)}) copy-start(f32[4,1024,1024]{1,2,0:T(8,128)S(1)} %get-tuple-element.263) | copy-start | bytes 50331652 | tf_op jit(solution)/shard_map/while
  152.0 5.8 %copy-start.2 = (bf16[4,1024,1024]{1,2,0:T(8,128)(2,1)S(1)}, bf16[4,1024,1024]{1,2,0:T(8,128)(2,1)}, u32[]{:S(2)}) copy-start(bf16[4,1024,1024]{1,2,0:T(8,128)(2,1)} %multiply_convert_fusion.7) | copy-start | bytes 25165828 | tf_op jit(solution)/shard_map/while
  169.0 10.9 %copy-start.1 = (f32[4,1024,1024]{1,2,0:T(8,128)}, f32[4,1024,1024]{1,2,0:T(8,128)S(1)}, u32[]{:S(2)}) copy-start(f32[4,1024,1024]{1,2,0:T(8,128)S(1)} %get-tuple-element.263) | copy-start | bytes 50331652 | tf_op jit(solution)/shard_map/while
  207.4 10.9 %copy-start.1 = (f32[4,1024,1024]{1,2,0:T(8,128)}, f32[4,1024,1024]{1,2,0:T(8,128)S(1)}, u32[]{:S(2)}) copy-start(f32[4,1024,1024]{1,2,0:T(8,128)S(1)} %get-tuple-element.263) | copy-start | bytes 50331652 | tf_op jit(solution)/shard_map/while
  245.7 10.9 %copy-start.1 = (f32[4,1024,1024]{1,2,0:T(8,128)}, f32[4,1024,1024]{1,2,0:T(8,128)S(1)}, u32[]{:S(2)}) copy-start(f32[4,1024,1024]{1,2,0:T(8,128)S(1)} %get-tuple-element.263) | copy-start | bytes 50331652 | tf_op jit(solution)/shard_map/while
  285.7 9.2 %copy-start.10 = (bf16[128,16,64]{2,1,0:T(8,128)(2,1)S(1)}, bf16[128,16,64]{2,1,0:T(8,128)(2,1)}, u32[]{:S(2)}) copy-start(bf16[128,16,64]{2,1,0:T(8,128)(2,1)} %copy-done.9) | copy-start | bytes 786436
  285.7 13.9 %copy-start.36 = (bf16[128,64]{0,1:T(8,128)(2,1)S(1)}, bf16[128,64]{0,1:T(8,128)(2,1)}, u32[]{:S(2)}) copy-start(bf16[128,64]{0,1:T(8,128)(2,1)} %param.18) | copy-start | bytes 49156
  285.7 31.4 %all-to-all-start.3 = ((bf16[2,64,6144]{2,0,1:T(2,128)(2,1)}), bf16[2,64,6144]{2,0,1:T(2,128)(2,1)}, u32[]{:S(2)}, u32[]{:S(2)}) async-start(bf16[2,64,6144]{2,0,1:T(2,128)(2,1)} %copy.176), calls=%async_computation.3 | async-start | bytes 3145728 | tf_op jit(solution)/shard_map/all_to_all | solution.py:192
  330.5 8.7 %copy-start.28 = (bf16[128,16,64]{0,2,1:T(8,128)(2,1)S(1)}, bf16[128,16,64]{0,2,1:T(8,128)(2,1)}, u32[]{:S(2)}) copy-start(bf16[128,16,64]{0,2,1:T(8,128)(2,1)} %get-tuple-element.164) | copy-start | bytes 786436
  330.9 15.3 %collective-permute-start.4 = (bf16[1,16,256]{2,1,0:T(8,128)(2,1)S(1)}, bf16[1,16,256]{2,1,0:T(8,128)(2,1)S(1)}, u32[]{:S(2)}, u32[]{:S(2)}) collective-permute-start(bf16[1,16,256]{2,1,0:T(8,128)(2,1)S(1)} %copy.178), channel_id=1, source_target_pairs={{0,64},{1,65},{2,66},{3,67},{4,68},{5,69},{6,70},{7,71},{8,72},{9,... | collective-permute-start | bytes 24584 | tf_op jit(solution)/shard_map/ppermute | solution.py:17
  337.9 8.8 %collective-permute-start.5 = (bf16[1,16,256]{2,1,0:T(8,128)(2,1)S(1)}, bf16[1,16,256]{2,1,0:T(8,128)(2,1)S(1)}, u32[]{:S(2)}, u32[]{:S(2)}) collective-permute-start(bf16[1,16,256]{2,1,0:T(8,128)(2,1)S(1)} %copy.179), channel_id=1, source_target_pairs={{64,0},{65,1},{66,2},{67,3},{68,4},{69,5},{70,6},{71,7},{72,8},{73... | collective-permute-start | bytes 24584 | tf_op jit(solution)/shard_map/ppermute | solution.py:20
  348.1 13.1 %collective-permute-start.6 = (bf16[130,1,256]{0,2,1:T(8,128)(2,1)}, bf16[130,1,256]{0,2,1:T(8,128)(2,1)S(1)}, u32[]{:S(2)}, u32[]{:S(2)}) collective-permute-start(bf16[130,1,256]{0,2,1:T(8,128)(2,1)} %get-tuple-element.133), channel_id=1, source_target_pairs={{1,0},{2,1},{3,2},{4,3},{5,4},{6,5},{7,6},{8,7},{9,8},{10,9},{11,1... | collective-permute-start | bytes 199688 | tf_op jit(solution)/shard_map/ppermute | solution.py:20
  350.8 10.4 %collective-permute-start.7 = (bf16[130,1,256]{0,2,1:T(8,128)(2,1)}, bf16[130,1,256]{0,2,1:T(8,128)(2,1)S(1)}, u32[]{:S(2)}, u32[]{:S(2)}) collective-permute-start(bf16[130,1,256]{0,2,1:T(8,128)(2,1)} %get-tuple-element.132), channel_id=1, source_target_pairs={{0,1},{1,2},{2,3},{3,4},{4,5},{5,6},{6,7},{7,8},{8,9},{9,10},{10,1... | collective-permute-start | bytes 199688 | tf_op jit(solution)/shard_map/ppermute | solution.py:17
  (37 other events, 97.4 us)
where the time goes:
time: 411 us; the launch traced here: 404 us
  matrix products  149 us (36%)
  local copies, waits for them, and re-layouts  102 us (25%)
  starting transfers between devices  62.1 us (15%)
  other arithmetic  60.6 us (15%)
  waiting for transfers between devices  29.1 us (7%)
    convert_element_type x4, other arithmetic, attend_backward(): grad_score = (probs * (grad_prob - inner)).astype(jnp.bfloat16)  41.6 us
    dot_general x4, matrix products, attend_backward(): jnp.einsum('gqd,gkd->gqk', grad_items, value_items, preferred_element_typ...  38.8 us
    dot_general x4, matrix products, attend_backward(): jnp.einsum('gqk,gqd->gkd', probs.astype(jnp.bfloat16), grad_items, prefer...  28.7 us
    dot_general x4, matrix products, attend_backward(): jnp.einsum('gqk,gqd->gkd', grad_score, queries, preferred_element_type=jn...  23.2 us
    slice x10, local copies, waits for them, and re-layouts, conv_backward(): padded_grad[2 - row_tap:2 - row_tap + row_count, 2 - col_tap:2 - col_tap...  22.6 us
    dot_general x8, matrix products, item_probs(): jnp.einsum('gqd,gkd->gqk', queries, key_items, preferred_element_type=jnp...  22.4 us
    all_to_all x1, waiting for transfers between devices, on_device(): lax.all_to_all(grad_qkv_rows.reshape(line_count, -1), 'gx', split_axis=1,...  16.5 us
    ppermute x4, starting transfers between devices, with_halo(): lax.ppermute(lax.slice_in_dim(block, block.shape[dim] - width, None, axis...  16 us
  transfers between devices with their start and end apart: 12, of which 2 were waited for; matrix products, arithmetic and copies ran while one was open for 51% of the time, Pallas kernels for 0%

commit v1 on v0

v1 whole, which is shorter than its diff:
```python
import jax
import jax.numpy as jnp
from jax import lax
from jax.experimental import pallas as pl
from jax.experimental.pallas import tpu as pltpu
from jax.sharding import PartitionSpec as P

HEADS = 8
EPS = 1e-05
LOG2E = 1.4426950408889634
F32 = jnp.float32
BF16 = jnp.bfloat16


def matmul(lhs, rhs, lhs_dim=1, rhs_dim=0):
    return lax.dot_general(
        lhs, rhs, (((lhs_dim,), (rhs_dim,)), ((), ())), preferred_element_type=F32
    )


def call(body, out_shape, scratch=(), vmem=48):
    return pl.pallas_call(
        body,
        out_shape=out_shape,
        scratch_shapes=list(scratch),
        compiler_params=pltpu.CompilerParams(vmem_limit_bytes=vmem << 20),
    )


def low_half(shape):
    return lax.broadcasted_iota(jnp.int32, shape, 1) < shape[1] // 2


def swap_halves(value):
    return pltpu.roll(value, value.shape[1] // 2, axis=1)


def column_of(shape, cols):
    return lax.rem(lax.broadcasted_iota(jnp.int32, shape, 0), cols)


def spread(edge, cols, at):
    rows = edge.shape[0]
    shape = (rows * cols, rows)
    position = lax.broadcasted_iota(jnp.int32, shape, 0)
    row = lax.broadcasted_iota(jnp.int32, shape, 1)
    pick = jnp.where(position == row * cols + at, 1.0, 0.0).astype(BF16)
    return matmul(pick, edge)


def pick_column(flat, cols, at):
    rows = flat.shape[0] // cols
    shape = (rows, rows * cols)
    row = lax.broadcasted_iota(jnp.int32, shape, 0)
    position = lax.broadcasted_iota(jnp.int32, shape, 1)
    pick = jnp.where(position == row * cols + at, 1.0, 0.0).astype(BF16)
    return matmul(pick, flat).astype(BF16)


def fill_taps(taps, parts, row_halo, left, right, corners, rows, cols, chunk):
    width = taps.shape[1] // 3
    upper = lax.axis_index("gy") == 0
    for start in range(0, rows, chunk):
        count = chunk * cols
        begin = start * cols
        column = 0
        for part in parts:
            part_width = part.shape[1]
            value = part[pl.ds(begin, count), :]
            wide = value.astype(F32)
            where = column_of(wide.shape, cols)
            lanes = pl.ds(column, part_width)
            left_edge = spread(left[pl.ds(start, chunk), lanes], cols, 0)
            right_edge = spread(right[pl.ds(start, chunk), lanes], cols, cols - 1)
            before = jnp.where(where == 0, left_edge, pltpu.roll(wide, 1, axis=0))
            after = jnp.where(where == cols - 1, right_edge, pltpu.roll(wide, count - 1, axis=0))
            target = pl.ds(cols + begin, count)
            taps[target, pl.ds(column, part_width)] = before.astype(BF16)
            taps[target, pl.ds(width + column, part_width)] = value
            taps[target, pl.ds(2 * width + column, part_width)] = after.astype(BF16)
            column += part_width
    halo = row_halo[...].astype(F32)
    where = column_of(halo.shape, cols)
    first = jnp.broadcast_to(corners[pl.ds(0, 1), :].astype(F32), halo.shape)
    last = jnp.broadcast_to(corners[pl.ds(1, 1), :].astype(F32), halo.shape)
    before = jnp.where(where == 0, first, pltpu.roll(halo, 1, axis=0))
    after = jnp.where(where == cols - 1, last, pltpu.roll(halo, cols - 1, axis=0))
    for index, piece in enumerate((before, halo, after)):
        lanes = pl.ds(index * width, width)
        taps[pl.ds(0, cols), lanes] = jnp.where(upper, 0.0, piece).astype(BF16)
        taps[pl.ds((rows + 1) * cols, cols), lanes] = jnp.where(upper, piece, 0.0).astype(BF16)


def conv_chunk(taps, weights, begin, count, cols):
    total = matmul(taps[pl.ds(begin, count), :], weights[0])
    total = total + matmul(taps[pl.ds(begin + cols, count), :], weights[1])
    return total + matmul(taps[pl.ds(begin + 2 * cols, count), :], weights[2])


def lane_mean(value, low, size):
    return jnp.sum(jnp.where(low, value, 0.0), axis=-1, keepdims=True) / size


def step_forward(rows, cols, chunk):
    def body(radar, state, row_halo, left, right, corners, weights, bias, gain, state_grad,
             payload, sig_ref, mix_ref, cell_ref, taps):
        fill_taps(taps, (radar, state), row_halo, left, right, corners, rows, cols, chunk)
        count = chunk * cols
        half = state.shape[1] // 2
        for start in range(0, rows, chunk):
            begin = start * cols
            part = pl.ds(begin, count)
            gates = conv_chunk(taps, weights, begin, count, cols) + bias[...]
            low = low_half((count, 2 * half))
            sig = jax.nn.sigmoid(gates[:, : 2 * half])
            other = gates[:, 2 * half :]
            mix = jnp.where(low, jax.nn.sigmoid(other), jnp.tanh(other))
            held = state[part, :].astype(F32)
            terms = sig * jnp.where(low, swap_halves(mix), held)
            c_new = terms + swap_halves(terms)
            h_new = mix * jnp.tanh(c_new)
            inv_rms = lax.rsqrt(lane_mean(h_new * h_new, low, half) + EPS)
            normed = h_new * inv_rms * gain[...]
            grad = swap_halves(state_grad[part, :].astype(F32))
            payload[part, :] = jnp.where(low, normed, grad).astype(BF16)
            sig_ref[part, :] = sig
            mix_ref[part, :] = mix
            cell_ref[part, :] = jnp.where(low, h_new, c_new)

    return body


def attention(lines, length, block):
    def body(cells, w_rows, w_cols, w_mixed, w_q_back, w_kv_back, out,
             rows, grad_rows, cols, key_mask, value_mask, exps, probs, scores, mixed, grad_q, grad_kv):
        head = pl.program_id(1)
        size = w_rows.shape[1] // 4
        dim = size // HEADS
        scale = dim ** (-0.5)

        @pl.when(head == 0)
        def _():
            line = cells[...].reshape(length, cells.shape[-1])
            flat = matmul(line, w_rows[...]).astype(BF16)
            rows[:, pl.ds(0, 3 * size)] = flat[:, : 3 * size]
            rows[:, pl.ds(3 * size, size)] = jnp.ones((length, size), BF16)
            grad_rows[...] = flat[:, 3 * size :]
            cols[...] = matmul(w_cols[...], line, 1, 1).astype(BF16)
            mixed[...] = jnp.zeros_like(mixed)
            grad_q[...] = jnp.zeros_like(grad_q)

        key_mask[...] = jnp.zeros_like(key_mask)
        value_mask[...] = jnp.zeros_like(value_mask)
        at = pl.multiple_of(head * dim, dim)
        key_mask[pl.ds(at, dim), :] = cols[pl.ds(size + at, dim), :]
        value_mask[pl.ds(at, dim), :] = cols[pl.ds(2 * size + at, dim), :]
        lane = lax.broadcasted_iota(jnp.int32, (block, size), 1)
        mine = jnp.logical_and(lane >= at, lane < at + dim)
        total_v = jnp.zeros((dim, length), F32)
        total_k = jnp.zeros((dim, length), F32)
        for begin in range(0, length, block):
            part = pl.ds(begin, block)
            exps[part, :] = jnp.exp2(
                matmul(rows[part, pl.ds(0, size)], key_mask[...]) * (scale * LOG2E)
            ).astype(BF16)
            sums = matmul(exps[part, :], rows[:, pl.ds(2 * size, 2 * size)])
            inverse = 1.0 / sums[:, size:]
            attended = jnp.where(mine, sums[:, :size] * inverse, 0.0)
            mixed[part, :] += attended
            grads = grad_rows[part, :]
            inner = jnp.sum(attended * grads.astype(F32), axis=-1, keepdims=True)
            prob = exps[part, :].astype(F32) * inverse[:, :1]
            probs[part, :] = prob.astype(BF16)
            scores[part, :] = (
                prob * (matmul(grads, value_mask[...]) - inner)
            ).astype(BF16)
            grad_q[part, :] += jnp.where(
                mine, matmul(scores[part, :], rows[:, pl.ds(size, size)]), 0.0
            )
            total_v = total_v + matmul(
                cols[pl.ds(3 * size + at, dim), part], probs[part, :]
            )
            total_k = total_k + matmul(cols[pl.ds(at, dim), part], scores[part, :])
        grad_kv[pl.ds(at, dim), :] = (total_k * scale).astype(BF16)
        grad_kv[pl.ds(size + at, dim), :] = total_v.astype(BF16)

        @pl.when(head == HEADS - 1)
        def _():
            result = (
                matmul(mixed[...].astype(BF16), w_mixed[...])
                + matmul((grad_q[...] * scale).astype(BF16), w_q_back[...])
                + matmul(grad_kv[...], w_kv_back[...], 0, 0)
            )
            out[...] = result.astype(BF16).reshape(out.shape)

    return body


def attend(cells, w_rows, w_cols, w_mixed, w_q_back, w_kv_back):
    peers, lines, cols, width = cells.shape
    length = peers * cols
    size = w_mixed.shape[0]
    block = min(256, length)
    whole = lambda array: pl.BlockSpec(array.shape, lambda i, j: (0,) * array.ndim)
    line_spec = pl.BlockSpec((peers, None, cols, width), lambda i, j: (0, i, 0, 0))

    return pl.pallas_call(
        attention(lines, length, block),
        out_shape=jax.ShapeDtypeStruct(cells.shape, BF16),
        grid=(lines, HEADS),
        in_specs=[line_spec] + [whole(w) for w in (w_rows, w_cols, w_mixed, w_q_back, w_kv_back)],
        out_specs=line_spec,
        scratch_shapes=[
            pltpu.VMEM((length, 4 * size), BF16),
            pltpu.VMEM((length, size), BF16),
            pltpu.VMEM((4 * size, length), BF16),
            pltpu.VMEM((size, length), BF16),
            pltpu.VMEM((size, length), BF16),
            pltpu.VMEM((length, length), BF16),
            pltpu.VMEM((length, length), BF16),
            pltpu.VMEM((length, length), BF16),
            pltpu.VMEM((length, size), F32),
            pltpu.VMEM((length, size), F32),
            pltpu.VMEM((2 * size, length), BF16),
        ],
        compiler_params=pltpu.CompilerParams(
            dimension_semantics=("arbitrary", "arbitrary"), vmem_limit_bytes=48 << 20
        ),
    )(cells, w_rows, w_cols, w_mixed, w_q_back, w_kv_back)


def gate_grads(rows, cols, chunk):
    def body(back, state, state_grad, gain, sig_ref, mix_ref, cell_ref,
             new_state, grads, left, right, first, last, c_grad):
        count = chunk * cols
        half = state.shape[1] // 2
        for start in range(0, rows, chunk):
            part = pl.ds(start * cols, count)
            low = low_half((count, 2 * half))
            sig, mix, cell = sig_ref[part, :], mix_ref[part, :], cell_ref[part, :]
            arrived = back[part, :].astype(F32)
            new_state[part, :] = (cell + jnp.where(low, arrived, 0.0)).astype(BF16)
            held = state[part, :].astype(F32)
            given = state_grad[part, :].astype(F32)
            inv_rms = lax.rsqrt(lane_mean(cell * cell, low, half) + EPS)
            scaled = swap_halves(arrived) * gain[...]
            along = lane_mean(scaled * cell, low, half)
            hidden = given + inv_rms * scaled - cell * (inv_rms * inv_rms * inv_rms * along)
            hidden = jnp.where(low, hidden, swap_halves(hidden))
            c_new = jnp.where(low, swap_halves(cell), cell)
            c_tanh = jnp.tanh(c_new)
            mix_swapped = swap_halves(mix)
            out_gate = jnp.where(low, mix, mix_swapped)
            given_cell = jnp.where(low, swap_halves(given), given)
            cell_grad = given_cell + hidden * out_gate * (1.0 - c_tanh * c_tanh)
            one = cell_grad * jnp.where(low, mix_swapped, held) * sig * (1.0 - sig)
            two = jnp.where(
                low,
                hidden * c_tanh * mix * (1.0 - mix),
                cell_grad * swap_halves(sig) * (1.0 - mix * mix),
            )
            one, two = one.astype(BF16), two.astype(BF16)
            grads[part, pl.ds(0, 2 * half)] = one
            grads[part, pl.ds(2 * half, 2 * half)] = two
            c_grad[part, :] = (cell_grad * sig).astype(BF16)
            for lanes, value in ((pl.ds(0, 2 * half), one), (pl.ds(2 * half, 2 * half), two)):
                left[pl.ds(start, chunk), lanes] = pick_column(value, cols, 0)
                right[pl.ds(start, chunk), lanes] = pick_column(value, cols, cols - 1)
        first[...] = grads[pl.ds(0, cols), :]
        last[...] = grads[pl.ds((rows - 1) * cols, cols), :]

    return body


def step_backward(rows, cols, chunk):
    def body(grads, row_halo, left, right, corners, weights, c_grad, grad_frame, grad_state, taps):
        fill_taps(taps, (grads,), row_halo, left, right, corners, rows, cols, chunk)
        count = chunk * cols
        wide = grad_frame.shape[1]
        for start in range(0, rows, chunk):
            begin = start * cols
            part = pl.ds(begin, count)
            total = conv_chunk(taps, weights, begin, count, cols)
            grad_frame[part, :] = total[:, :wide].astype(BF16)
            rest = total[:, wide:].astype(BF16)
            grad_state[part, :] = jnp.where(low_half(rest.shape), rest, c_grad[part, :])

    return body


def exchange(first_col, last_col, first_row, last_row):
    count = lax.axis_size("gx")
    forward = [(i, i + 1) for i in range(count - 1)]
    backward = [(target, source) for source, target in forward]
    left = lax.ppermute(last_col, "gx", forward)
    right = lax.ppermute(first_col, "gx", backward)
    border = jnp.where(lax.axis_index("gy") == 0, last_row, first_row)
    row_halo = lax.ppermute(border, "gy", [(0, 1), (1, 0)])
    across = lambda pairs: [
        (y * count + source, (1 - y) * count + target) for y in (0, 1) for source, target in pairs
    ]
    low = lax.ppermute(border[-1:], ("gy", "gx"), across(forward))
    high = lax.ppermute(border[:1], ("gy", "gx"), across(backward))
    return row_halo, left, right, jnp.concatenate([low, high], axis=0)


def on_device(radar_frame, lstm_state, w_conv, b_gates, norm_gain, w_qkv, w_out, state_grad):
    row_count, col_count, in_channels = radar_frame.shape
    hidden = lstm_state.shape[2] // 2
    gate_dim = w_conv.shape[3]
    attn_dim = w_out.shape[0]
    cells = row_count * col_count
    chunk = min(32, row_count)
    lines = row_count // lax.axis_size("gx")
    shape = lambda *dims: jax.ShapeDtypeStruct(dims, BF16)
    wide = lambda *dims: jax.ShapeDtypeStruct(dims, F32)
    vmem = pltpu.VMEM

    radar = radar_frame.reshape(cells, in_channels)
    state = lstm_state.reshape(cells, 2 * hidden)
    given = state_grad.reshape(cells, 2 * hidden)
    both = lambda a, b: jnp.concatenate([a, b], axis=-1)
    halo = exchange(
        both(radar_frame[:, 0], lstm_state[:, 0]),
        both(radar_frame[:, -1], lstm_state[:, -1]),
        both(radar_frame[0], lstm_state[0]),
        both(radar_frame[-1], lstm_state[-1]),
    )
    in_pad = 2 * hidden + in_channels - w_conv.shape[2]
    padded = jnp.pad(w_conv, ((0, 0), (0, 0), (0, in_pad), (0, 0)))
    w_forward = padded.reshape(3, -1, gate_dim)
    w_backward = padded[::-1, ::-1].transpose(0, 1, 3, 2).reshape(3, 3 * gate_dim, -1)
    gain = jnp.tile(norm_gain, 2)[None]

    payload, sig, mix, cell = call(
        step_forward(row_count, col_count, chunk),
        (shape(cells, 2 * hidden),) + (wide(cells, 2 * hidden),) * 3,
        [vmem(((row_count + 2) * col_count, 3 * (in_channels + 2 * hidden)), BF16)],
    )(radar, state, *halo, w_forward, b_gates[None], gain, given)

    peers = lax.axis_size("gx")
    send = payload.reshape(peers, lines, col_count, 2 * hidden)
    lines_in = lax.all_to_all(send, "gx", split_axis=0, concat_axis=0, tiled=True)
    none = jnp.zeros((hidden, attn_dim), BF16)
    w_qkv_down = jnp.concatenate([w_qkv, jnp.zeros_like(w_qkv)], axis=0)
    w_grad_down = jnp.concatenate([none, w_out.T], axis=0)
    w_all = jnp.concatenate([w_qkv_down, w_grad_down], axis=1)
    w_mixed = jnp.concatenate([w_out, jnp.zeros_like(w_out)], axis=1)
    w_back = jnp.concatenate([jnp.zeros_like(w_qkv), w_qkv], axis=0).T
    lines_out = attend(
        lines_in, w_all, w_all.T, w_mixed, w_back[:attn_dim], w_back[attn_dim:]
    )
    back = lax.all_to_all(lines_out, "gx", split_axis=0, concat_axis=0, tiled=True)

    new_state, grads, left, right, first, last, c_grad = call(
        gate_grads(row_count, col_count, chunk),
        (
            shape(cells, 2 * hidden),
            shape(cells, gate_dim),
            shape(row_count, gate_dim),
            shape(row_count, gate_dim),
            shape(col_count, gate_dim),
            shape(col_count, gate_dim),
            shape(cells, 2 * hidden),
        ),
    )(back.reshape(cells, 2 * hidden), state, given, gain, sig, mix, cell)
    halo = exchange(left, right, first, last)
    grad_frame, grad_state = call(
        step_backward(row_count, col_count, chunk),
        (shape(cells, in_channels), shape(cells, 2 * hidden)),
        [vmem(((row_count + 2) * col_count, 3 * gate_dim), BF16)],
    )(grads, *halo, w_backward, c_grad)
    whole = lambda array: array.reshape(row_count, col_count, -1)
    return whole(new_state), whole(grad_frame), whole(grad_state)


def solution(mesh):
    spec = P("gy", "gx", None)
    return jax.shard_map(
        on_device,
        mesh=mesh,
        in_specs=(spec, spec, P(), P(), P(), P(), P(), spec),
        out_specs=(spec, spec, spec),
        check_vma=False,
    )
```

time: 411 us -> 189 us (0.46); the launches traced: 404 us -> 188 us
  matrix products: 149 us -> 0 us
  Pallas kernels: 0 us -> 96.3 us
  local copies, waits for them, and re-layouts: 102 us -> 10.6 us
  other arithmetic: 60.6 us -> 0.14 us
  blocking collectives: 0 us -> 16.9 us
  waiting for transfers between devices: 29.1 us -> 13.4 us
  starting transfers between devices: 62.1 us -> 49.7 us
    dot_general x50 -> x0, matrix products: 149 us -> none  [the longest x4 38.8 us: attend_backward(): jnp.einsum('gqd,gkd->gqk', grad_items, value_items, preferred_element_typ...]
    pallas_call x0 -> x4, Pallas kernels: none -> 96.3 us  [the longest x1 81 us: attend(): pl.pallas_call(attention(lines, length, block), out_shape=jax.ShapeDtypeS...]
    convert_element_type x5 -> x0, other arithmetic: 41.8 us -> none  [the longest x4 41.6 us: attend_backward(): grad_score = (probs * (grad_prob - inner)).astype(jnp.bfloat16)]
    slice x31 -> x6, local copies, waits for them, and re-layouts: 34.7 us -> 2.3 us  [the longest x1 1.14 us: on_device(): radar_frame[:, 0]]
    all_to_all x4 -> x1, starting transfers between devices: 34.2 us -> 9.5 us  [on_device(): lax.all_to_all(send, 'gx', split_axis=0, concat_axis=0, tiled=True)]
    all_to_all x4 -> x1, waiting for transfers between devices: 29 us -> 10.9 us  [on_device(): lax.all_to_all(send, 'gx', split_axis=0, concat_axis=0, tiled=True)]
    all_to_all x0 -> x1, blocking collectives: none -> 16.9 us  [on_device(): lax.all_to_all(lines_out, 'gx', split_axis=0, concat_axis=0, tiled=True)]
    all_to_all x8 -> x0, local copies, waits for them, and re-layouts: 16 us -> none  [the longest x2 9.51 us: on_device(): lax.all_to_all(attended_rows.reshape(line_count, -1), 'gx', split_axis=1,...]
  transfers between devices with their start and end apart: 12 -> 11, of which waited for: 2 -> 3; matrix products, arithmetic and copies ran while one was open for 51% -> 4% of each run, Pallas kernels for 0% -> 0%
where the time goes in v1:
time: 189 us; the launch traced here: 188 us
  Pallas kernels  96.3 us (51%)
  starting transfers between devices  49.7 us (26%)
  blocking collectives  16.9 us (9%)
  waiting for transfers between devices  13.4 us (7%)
  local copies, waits for them, and re-layouts  10.6 us (6%)
    pallas_call x1, Pallas kernels, attend(): pl.pallas_call(attention(lines, length, block), out_shape=jax.ShapeDtypeS...  81 us
    all_to_all x1, blocking collectives, on_device(): lax.all_to_all(lines_out, 'gx', split_axis=0, concat_axis=0, tiled=True)  16.9 us
    ppermute x2, starting transfers between devices, exchange(): high = lax.ppermute(border[:1], ('gy', 'gx'), across(backward))  15.7 us
    ppermute x2, starting transfers between devices, exchange(): right = lax.ppermute(first_col, 'gx', backward)  13.4 us
    all_to_all x1, waiting for transfers between devices, on_device(): lax.all_to_all(send, 'gx', split_axis=0, concat_axis=0, tiled=True)  10.9 us
    all_to_all x1, starting transfers between devices, on_device(): lax.all_to_all(send, 'gx', split_axis=0, concat_axis=0, tiled=True)  9.5 us
    pallas_call x1, Pallas kernels, on_device(): call(step_forward(row_count, col_count, chunk), (shape(cells, 2 * hidden)...  6.41 us
    pallas_call x1, Pallas kernels, on_device(): call(gate_grads(row_count, col_count, chunk), (shape(cells, 2 * hidden),...  4.83 us
  transfers between devices with their start and end apart: 11, of which 3 were waited for; matrix products, arithmetic and copies ran while one was open for 4% of the time, Pallas kernels for 0%

profile of v1, /device:TPU:2, one launch (start us, length us, event | category | flops | bytes accessed | tf_op | source)
XLA Modules:
  0.0 188.0 jit_solution(10658784537911664861)
XLA Ops:
  1.5 3.3 %collective-permute-start = (bf16[16,256]{1,0:T(8,128)(2,1)S(1)}, bf16[16,256]{1,0:T(8,128)(2,1)S(1)}, u32[]{:S(2)}, u32[]{:S(2)}) collective-permute-start(bf16[16,256]{1,0:T(8,128)(2,1)S(1)} %maximum_select_fusion), channel_id=1, source_target_pairs={{0,64},{64,0},{1,65},{65,1},{2,66},{66,2},{3,67},{67,3},{4,68},{68... | collective-permute-start | bytes 24584 | tf_op jit(solution)/shard_map/ppermute | solution.py:298
  4.8 1.9 %collective-permute-start.3 = (bf16[1,256]{1,0:T(2,128)(2,1)S(1)}, bf16[1,256]{1,0:T(2,128)(2,1)S(1)}, u32[]{:S(2)}, u32[]{:S(2)}) collective-permute-start(bf16[1,256]{1,0:T(2,128)(2,1)S(1)} %get-tuple-element.41), channel_id=1, source_target_pairs={{0,65},{1,66},{2,67},{3,68},{4,69},{5,70},{6,71},{7,72},{8,73},{9,... | collective-permute-start | bytes 1544 | tf_op jit(solution)/shard_map/ppermute | solution.py:302
  6.7 7.9 %collective-permute-start.4 = (bf16[1,256]{1,0:T(2,128)(2,1)S(1)}, bf16[1,256]{1,0:T(2,128)(2,1)S(1)}, u32[]{:S(2)}, u32[]{:S(2)}) collective-permute-start(bf16[1,256]{1,0:T(2,128)(2,1)S(1)} %get-tuple-element.42), channel_id=1, source_target_pairs={{1,64},{2,65},{3,66},{4,67},{5,68},{6,69},{7,70},{8,71},{9,72},{10... | collective-permute-start | bytes 1544 | tf_op jit(solution)/shard_map/ppermute | solution.py:303
  14.5 1.1 fusion.4
  15.7 1.1 fusion.5
  16.9 1.9 %collective-permute-start.1 = (bf16[128,256]{1,0:T(8,128)(2,1)S(1)}, bf16[128,256]{1,0:T(8,128)(2,1)S(1)}, u32[]{:S(2)}, u32[]{:S(2)}) collective-permute-start(bf16[128,256]{1,0:T(8,128)(2,1)S(1)} %pad_maximum_fusion), channel_id=1, source_target_pairs={{0,1},{1,2},{2,3},{3,4},{4,5},{5,6},{6,7},{7,8},{8,9},{9,10},{10,1... | collective-permute-start | bytes 196616 | tf_op jit(solution)/shard_map/ppermute | solution.py:295
  18.9 6.8 %collective-permute-start.2 = (bf16[128,256]{1,0:T(8,128)(2,1)S(1)}, bf16[128,256]{1,0:T(8,128)(2,1)S(1)}, u32[]{:S(2)}, u32[]{:S(2)}) collective-permute-start(bf16[128,256]{1,0:T(8,128)(2,1)S(1)} %pad_maximum_fusion.1), channel_id=1, source_target_pairs={{1,0},{2,1},{3,2},{4,3},{5,4},{6,5},{7,6},{8,7},{9,8},{10,9},{11,1... | collective-permute-start | bytes 196616 | tf_op jit(solution)/shard_map/ppermute | solution.py:296
  25.8 1.1 pad.8
  27.6 6.4 %shard_map.103 = (bf16[2048,128]{1,0:T(8,128)(2,1)}, f32[2048,128]{1,0:T(8,128)S(1)}, f32[2048,128]{1,0:T(8,128)S(1)}, f32[2048,128]{1,0:T(8,128)S(1)}) custom-call(bf16[2048,128]{1,0:T(8,128)(2,1)S(1)} %bitcast.40, bf16[2048,128]{1,0:T(8,128)(2,1)S(1)} %bitcast.35, bf16[16,256]{1,0:T(8,128)(2,1)S(1)} %collective-permute-done.row_halo, ...), custom_call_target="tpu_custom_call" | custom-call | tf_op jit(solution)/shard_map/pallas_call | solution.py:335
  34.0 1.0 copy-done.2
  36.0 9.5 %all-to-all-start = ((bf16[64,2,16,128]{3,2,1,0:T(8,128)(2,1)}), bf16[64,2,16,128]{3,2,1,0:T(8,128)(2,1)S(1)}, u32[]{:S(2)}, u32[]{:S(2)}) async-start(bf16[64,2,16,128]{3,2,1,0:T(8,128)(2,1)} %bitcast.13), calls=%async_computation | async-start | bytes 1048576 | tf_op jit(solution)/shard_map/all_to_all | solution.py:343
  46.1 10.9 %all-to-all-done.cells = bf16[64,2,16,128]{3,2,1,0:T(8,128)(2,1)S(1)} async-done(((bf16[64,2,16,128]{3,2,1,0:T(8,128)(2,1)}), bf16[64,2,16,128]{3,2,1,0:T(8,128)(2,1)S(1)}, u32[]{:S(2)}, u32[]{:S(2)}) %all-to-all-start) | async-done | bytes 524320 | tf_op jit(solution)/shard_map/all_to_all | solution.py:343
  57.0 81.0 %shard_map.104 = bf16[64,2,16,128]{3,2,1,0:T(8,128)(2,1)S(1)} custom-call(bf16[64,2,16,128]{3,2,1,0:T(8,128)(2,1)S(1)} %all-to-all-done.cells, bf16[128,512]{1,0:T(8,128)(2,1)S(1)} %copy.19.w_rows, bf16[512,128]{1,0:T(8,128)(2,1)S(1)} %get-tuple-element.37.w_cols, bf16[128,128]{1,0:T(8,128)(2,1)S(1)} %concatenate.41.w_mixed, ...), custom_call_target="tpu_custom_call" | custom-call | tf_op jit(solution)/shard_map/pallas_call | solution.py:207
  137.9 16.9 %all_to_all.10 = bf16[64,2,16,128]{3,2,1,0:T(8,128)(2,1)S(1)} all-to-all(bf16[64,2,16,128]{3,2,1,0:T(8,128)(2,1)S(1)} %shard_map.104), channel_id=1, replica_groups=mesh['gy'=2,'gx'=64] {'gx'}, dimensions={0} | all-to-all | bytes 1048576 | tf_op jit(solution)/shard_map/all_to_all | solution.py:353
  154.8 4.8 %shard_map.105 = (bf16[2048,128]{1,0:T(8,128)(2,1)}, bf16[2048,256]{1,0:T(8,128)(2,1)S(1)}, bf16[128,256]{1,0:T(8,128)(2,1)S(1)}, bf16[128,256]{1,0:T(8,128)(2,1...) custom-call(bf16[2048,128]{1,0:T(8,128)(2,1)S(1)} %bitcast.37, ...), custom_call_target="tpu_custom_call" | custom-call | tf_op jit(solution)/shard_map/pallas_call | solution.py:355
  159.7 1.0 copy-done.5
  160.7 1.9 %collective-permute-start.8 = (bf16[1,256]{1,0:T(2,128)(2,1)S(1)}, bf16[1,256]{1,0:T(2,128)(2,1)S(1)}, u32[]{:S(2)}, u32[]{:S(2)}) collective-permute-start(bf16[1,256]{1,0:T(2,128)(2,1)S(1)} %get-tuple-element.39), channel_id=1, source_target_pairs={{0,65},{1,66},{2,67},{3,68},{4,69},{5,70},{6,71},{7,72},{8,73},{9,... | collective-permute-start | bytes 1544 | tf_op jit(solution)/shard_map/ppermute | solution.py:302
  162.6 7.9 %collective-permute-start.9 = (bf16[1,256]{1,0:T(2,128)(2,1)S(1)}, bf16[1,256]{1,0:T(2,128)(2,1)S(1)}, u32[]{:S(2)}, u32[]{:S(2)}) collective-permute-start(bf16[1,256]{1,0:T(2,128)(2,1)S(1)} %get-tuple-element.40), channel_id=1, source_target_pairs={{1,64},{2,65},{3,66},{4,67},{5,68},{6,69},{7,70},{8,71},{9,72},{10... | collective-permute-start | bytes 1544 | tf_op jit(solution)/shard_map/ppermute | solution.py:303
  170.5 1.1 reverse_bitcast_fusion
  171.6 1.7 copy.20
  173.3 1.9 %collective-permute-start.6 = (bf16[128,256]{1,0:T(8,128)(2,1)S(1)}, bf16[128,256]{1,0:T(8,128)(2,1)S(1)}, u32[]{:S(2)}, u32[]{:S(2)}) collective-permute-start(bf16[128,256]{1,0:T(8,128)(2,1)S(1)} %get-tuple-element.24), channel_id=1, source_target_pairs={{0,1},{1,2},{2,3},{3,4},{4,5},{5,6},{6,7},{7,8},{8,9},{9,10},{10,1... | collective-permute-start | bytes 196616 | tf_op jit(solution)/shard_map/ppermute | solution.py:295
  175.3 6.7 %collective-permute-start.7 = (bf16[128,256]{1,0:T(8,128)(2,1)S(1)}, bf16[128,256]{1,0:T(8,128)(2,1)S(1)}, u32[]{:S(2)}, u32[]{:S(2)}) collective-permute-start(bf16[128,256]{1,0:T(8,128)(2,1)S(1)} %get-tuple-element.25), channel_id=1, source_target_pairs={{1,0},{2,1},{3,2},{4,3},{5,4},{6,5},{7,6},{8,7},{9,8},{10,9},{11,1... | collective-permute-start | bytes 196616 | tf_op jit(solution)/shard_map/ppermute | solution.py:296
  182.0 1.8 collective-permute-done.7.right
  183.8 4.2 %shard_map.106 = (bf16[2048,128]{1,0:T(8,128)(2,1)}, bf16[2048,128]{1,0:T(8,128)(2,1)}) custom-call(bf16[2048,256]{1,0:T(8,128)(2,1)S(1)} %copy-done.6, bf16[16,256]{1,0:T(8,128)(2,1)S(1)} %collective-permute-done.5.row_halo, bf16[128,256]{1,0:T(8,128)(2,1)S(1)} %collective-permute-done.6.left, bf16[128,256]{1,0:T(8,128)(2,1)S(1)} %collective-permute-done.7.right, ...), custom_call_target="tpu_custom_call" | custom-call | tf_op jit(solution)/shard_map/pallas_call | solution.py:368
  (57 shorter events, 3.3 us)
Async XLA Ops:
  0.6 25.0 %copy-start.13 = (f32[64]{0:T(128)S(1)}, f32[64]{0:T(128)}, u32[]{:S(2)}) copy-start(f32[64]{0:T(128)} %param.12) | copy-start | bytes 772
  0.6 25.1 %copy-start.10 = (bf16[3,3,192,256]{3,2,1,0:T(8,128)(2,1)S(1)}, bf16[3,3,192,256]{3,2,1,0:T(8,128)(2,1)}, u32[]{:S(2)}) copy-start(bf16[3,3,192,256]{3,2,1,0:T(8,128)(2,1)} %param.10) | copy-start | bytes 2654212
  1.5 25.4 %collective-permute-start = (bf16[16,256]{1,0:T(8,128)(2,1)S(1)}, bf16[16,256]{1,0:T(8,128)(2,1)S(1)}, u32[]{:S(2)}, u32[]{:S(2)}) collective-permute-start(bf16[16,256]{1,0:T(8,128)(2,1)S(1)} %maximum_select_fusion), channel_id=1, source_target_pairs={{0,64},{64,0},{1,65},{65,1},{2,66},{66,2},{3,67},{67,3},{4,68},{68... | collective-permute-start | bytes 24584 | tf_op jit(solution)/shard_map/ppermute | solution.py:298
  4.8 22.1 %collective-permute-start.3 = (bf16[1,256]{1,0:T(2,128)(2,1)S(1)}, bf16[1,256]{1,0:T(2,128)(2,1)S(1)}, u32[]{:S(2)}, u32[]{:S(2)}) collective-permute-start(bf16[1,256]{1,0:T(2,128)(2,1)S(1)} %get-tuple-element.41), channel_id=1, source_target_pairs={{0,65},{1,66},{2,67},{3,68},{4,69},{5,70},{6,71},{7,72},{8,73},{9,... | collective-permute-start | bytes 1544 | tf_op jit(solution)/shard_map/ppermute | solution.py:302
  6.7 20.2 %collective-permute-start.4 = (bf16[1,256]{1,0:T(2,128)(2,1)S(1)}, bf16[1,256]{1,0:T(2,128)(2,1)S(1)}, u32[]{:S(2)}, u32[]{:S(2)}) collective-permute-start(bf16[1,256]{1,0:T(2,128)(2,1)S(1)} %get-tuple-element.42), channel_id=1, source_target_pairs={{1,64},{2,65},{3,66},{4,67},{5,68},{6,69},{7,70},{8,71},{9,72},{10... | collective-permute-start | bytes 1544 | tf_op jit(solution)/shard_map/ppermute | solution.py:303
  16.9 10.1 %collective-permute-start.1 = (bf16[128,256]{1,0:T(8,128)(2,1)S(1)}, bf16[128,256]{1,0:T(8,128)(2,1)S(1)}, u32[]{:S(2)}, u32[]{:S(2)}) collective-permute-start(bf16[128,256]{1,0:T(8,128)(2,1)S(1)} %pad_maximum_fusion), channel_id=1, source_target_pairs={{0,1},{1,2},{2,3},{3,4},{4,5},{5,6},{6,7},{7,8},{8,9},{9,10},{10,1... | collective-permute-start | bytes 196616 | tf_op jit(solution)/shard_map/ppermute | solution.py:295
  18.8 8.8 %copy-start = (bf16[128,16,128]{2,1,0:T(8,128)(2,1)S(1)}, bf16[128,16,128]{2,1,0:T(8,128)(2,1)}, u32[]{:S(2)}) copy-start(bf16[128,16,128]{2,1,0:T(8,128)(2,1)} %param.9) | copy-start | bytes 1572868
  18.8 8.8 %copy-start.1 = (bf16[128,16,128]{2,1,0:T(8,128)(2,1)S(1)}, bf16[128,16,128]{2,1,0:T(8,128)(2,1)}, u32[]{:S(2)}) copy-start(bf16[128,16,128]{2,1,0:T(8,128)(2,1)} %param.15) | copy-start | bytes 1572868
  18.8 8.7 %copy-start.7 = (bf16[128,16,128]{2,1,0:T(8,128)(2,1)S(1)}, bf16[128,16,128]{2,1,0:T(8,128)(2,1)}, u32[]{:S(2)}) copy-start(bf16[128,16,128]{2,1,0:T(8,128)(2,1)} %param.8) | copy-start | bytes 1572868
  18.8 8.7 %copy-start.8 = (f32[256]{0:T(256)S(1)}, f32[256]{0:T(256)}, u32[]{:S(2)}) copy-start(f32[256]{0:T(256)} %param.11) | copy-start | bytes 3076
  18.9 8.7 %collective-permute-start.2 = (bf16[128,256]{1,0:T(8,128)(2,1)S(1)}, bf16[128,256]{1,0:T(8,128)(2,1)S(1)}, u32[]{:S(2)}, u32[]{:S(2)}) collective-permute-start(bf16[128,256]{1,0:T(8,128)(2,1)S(1)} %pad_maximum_fusion.1), channel_id=1, source_target_pairs={{1,0},{2,1},{3,2},{4,3},{5,4},{6,5},{7,6},{8,7},{9,8},{10,9},{11,1... | collective-permute-start | bytes 196616 | tf_op jit(solution)/shard_map/ppermute | solution.py:296
  27.6 17.9 %copy-start.11 = (bf16[64,384]{1,0:T(8,128)(2,1)S(1)}, bf16[64,384]{1,0:T(8,128)(2,1)}, u32[]{:S(2)}) copy-start(bf16[64,384]{1,0:T(8,128)(2,1)} %param.13) | copy-start | bytes 147460
  34.0 1.0 copy-start.2
  36.0 9.8 %copy-start.12 = (bf16[128,64]{0,1:T(8,128)(2,1)S(1)}, bf16[128,64]{0,1:T(8,128)(2,1)}, u32[]{:S(2)}) copy-start(bf16[128,64]{0,1:T(8,128)(2,1)} %param.14) | copy-start | bytes 49156
  36.0 21.0 %all-to-all-start = ((bf16[64,2,16,128]{3,2,1,0:T(8,128)(2,1)}), bf16[64,2,16,128]{3,2,1,0:T(8,128)(2,1)S(1)}, u32[]{:S(2)}, u32[]{:S(2)}) async-start(bf16[64,2,16,128]{3,2,1,0:T(8,128)(2,1)} %bitcast.13), calls=%async_computation | async-start | bytes 1048576 | tf_op jit(solution)/shard_map/all_to_all | solution.py:343
  57.0 97.9 %copy-start.3 = (f32[2048,128]{1,0:T(8,128)S(1)}, f32[2048,128]{1,0:T(8,128)}, u32[]{:S(2)}) copy-start(f32[2048,128]{1,0:T(8,128)} %copy-done.2) | copy-start | bytes 3145732
  154.8 15.6 %copy-start.9 = (bf16[3,3,256,256]{3,2,1,0:T(8,128)(2,1)S(1)}, bf16[3,3,256,256]{3,2,1,0:T(8,128)(2,1)}, u32[]{:S(2)}) copy-start(bf16[3,3,256,256]{3,2,1,0:T(8,128)(2,1)} %pad.8) | copy-start | bytes 3538948
  159.7 1.0 copy-start.5
  160.7 21.3 %collective-permute-start.8 = (bf16[1,256]{1,0:T(2,128)(2,1)S(1)}, bf16[1,256]{1,0:T(2,128)(2,1)S(1)}, u32[]{:S(2)}, u32[]{:S(2)}) collective-permute-start(bf16[1,256]{1,0:T(2,128)(2,1)S(1)} %get-tuple-element.39), channel_id=1, source_target_pairs={{0,65},{1,66},{2,67},{3,68},{4,69},{5,70},{6,71},{7,72},{8,73},{9,... | collective-permute-start | bytes 1544 | tf_op jit(solution)/shard_map/ppermute | solution.py:302
  162.6 19.3 %collective-permute-start.9 = (bf16[1,256]{1,0:T(2,128)(2,1)S(1)}, bf16[1,256]{1,0:T(2,128)(2,1)S(1)}, u32[]{:S(2)}, u32[]{:S(2)}) collective-permute-start(bf16[1,256]{1,0:T(2,128)(2,1)S(1)} %get-tuple-element.40), channel_id=1, source_target_pairs={{1,64},{2,65},{3,66},{4,67},{5,68},{6,69},{7,70},{8,71},{9,72},{10... | collective-permute-start | bytes 1544 | tf_op jit(solution)/shard_map/ppermute | solution.py:303
  171.6 12.2 %copy-start.6 = (bf16[2048,256]{1,0:T(8,128)(2,1)S(1)}, bf16[2048,256]{1,0:T(8,128)(2,1)}, u32[]{:S(2)}) copy-start(bf16[2048,256]{1,0:T(8,128)(2,1)} %copy-done.5) | copy-start | bytes 3145732
  173.2 8.7 %collective-permute-start.5 = (bf16[16,256]{1,0:T(8,128)(2,1)S(1)}, bf16[16,256]{1,0:T(8,128)(2,1)S(1)}, u32[]{:S(2)}, u32[]{:S(2)}) collective-permute-start(bf16[16,256]{1,0:T(8,128)(2,1)S(1)} %broadcast_select_fusion), channel_id=1, source_target_pairs={{0,64},{64,0},{1,65},{65,1},{2,66},{66,2},{3,67},{67,3},{4,68},{68... | collective-permute-start | bytes 24584 | tf_op jit(solution)/shard_map/ppermute | solution.py:298
  173.3 8.6 %collective-permute-start.6 = (bf16[128,256]{1,0:T(8,128)(2,1)S(1)}, bf16[128,256]{1,0:T(8,128)(2,1)S(1)}, u32[]{:S(2)}, u32[]{:S(2)}) collective-permute-start(bf16[128,256]{1,0:T(8,128)(2,1)S(1)} %get-tuple-element.24), channel_id=1, source_target_pairs={{0,1},{1,2},{2,3},{3,4},{4,5},{5,6},{6,7},{7,8},{8,9},{9,10},{10,1... | collective-permute-start | bytes 196616 | tf_op jit(solution)/shard_map/ppermute | solution.py:295
  175.3 8.5 %collective-permute-start.7 = (bf16[128,256]{1,0:T(8,128)(2,1)S(1)}, bf16[128,256]{1,0:T(8,128)(2,1)S(1)}, u32[]{:S(2)}, u32[]{:S(2)}) collective-permute-start(bf16[128,256]{1,0:T(8,128)(2,1)S(1)} %get-tuple-element.25), channel_id=1, source_target_pairs={{1,0},{2,1},{3,2},{4,3},{5,4},{6,5},{7,6},{8,7},{9,8},{10,9},{11,1... | collective-permute-start | bytes 196616 | tf_op jit(solution)/shard_map/ppermute | solution.py:296
  (1 other events, 1.0 us)

commit v2 on v1

v2 whole, which is shorter than its diff:
```python
import jax
import jax.numpy as jnp
from jax import lax
from jax.experimental import pallas as pl
from jax.experimental.pallas import tpu as pltpu
from jax.sharding import PartitionSpec as P

HEADS = 8
EPS = 1e-05
LOG2E = 1.4426950408889634
VMEM_ATTEND = 28
F32 = jnp.float32
BF16 = jnp.bfloat16


def matmul(lhs, rhs, lhs_dim=1, rhs_dim=0):
    return lax.dot_general(
        lhs, rhs, (((lhs_dim,), (rhs_dim,)), ((), ())), preferred_element_type=F32
    )


def call(body, out_shape, scratch=(), vmem=24):
    return pl.pallas_call(
        body,
        out_shape=out_shape,
        scratch_shapes=list(scratch),
        compiler_params=pltpu.CompilerParams(vmem_limit_bytes=vmem << 20),
    )


def low_half(shape):
    return lax.broadcasted_iota(jnp.int32, shape, 1) < shape[1] // 2


def swap_halves(value):
    return pltpu.roll(value, value.shape[1] // 2, axis=1)


def column_of(shape, cols):
    return lax.rem(lax.broadcasted_iota(jnp.int32, shape, 0), cols)


def spread(edge, cols, at):
    rows = edge.shape[0]
    shape = (rows * cols, rows)
    position = lax.broadcasted_iota(jnp.int32, shape, 0)
    row = lax.broadcasted_iota(jnp.int32, shape, 1)
    pick = jnp.where(position == row * cols + at, 1.0, 0.0).astype(BF16)
    return matmul(pick, edge)


def pick_column(flat, cols, at):
    rows = flat.shape[0] // cols
    shape = (rows, rows * cols)
    row = lax.broadcasted_iota(jnp.int32, shape, 0)
    position = lax.broadcasted_iota(jnp.int32, shape, 1)
    pick = jnp.where(position == row * cols + at, 1.0, 0.0).astype(BF16)
    return matmul(pick, flat).astype(BF16)


def fill_taps(taps, parts, row_halo, left, right, rows, cols, chunk):
    width = taps.shape[1] // 3
    upper = lax.axis_index("gy") == 0
    for start in range(0, rows, chunk):
        count = chunk * cols
        begin = start * cols
        column = 0
        for part in parts:
            part_width = part.shape[1]
            value = part[pl.ds(begin, count), :]
            wide = value.astype(F32)
            where = column_of(wide.shape, cols)
            lanes = pl.ds(column, part_width)
            left_edge = spread(left[pl.ds(start, chunk), lanes], cols, 0)
            right_edge = spread(right[pl.ds(start, chunk), lanes], cols, cols - 1)
            before = jnp.where(where == 0, left_edge, pltpu.roll(wide, 1, axis=0))
            after = jnp.where(where == cols - 1, right_edge, pltpu.roll(wide, count - 1, axis=0))
            target = pl.ds(cols + begin, count)
            taps[target, pl.ds(column, part_width)] = before.astype(BF16)
            taps[target, pl.ds(width + column, part_width)] = value
            taps[target, pl.ds(2 * width + column, part_width)] = after.astype(BF16)
            column += part_width
    halo = row_halo[pl.ds(0, cols), :].astype(F32)
    where = column_of(halo.shape, cols)
    first = jnp.broadcast_to(row_halo[pl.ds(cols, 1), :].astype(F32), halo.shape)
    last = jnp.broadcast_to(row_halo[pl.ds(cols + 1, 1), :].astype(F32), halo.shape)
    before = jnp.where(where == 0, first, pltpu.roll(halo, 1, axis=0))
    after = jnp.where(where == cols - 1, last, pltpu.roll(halo, cols - 1, axis=0))
    for index, piece in enumerate((before, halo, after)):
        lanes = pl.ds(index * width, width)
        taps[pl.ds(0, cols), lanes] = jnp.where(upper, 0.0, piece).astype(BF16)
        taps[pl.ds((rows + 1) * cols, cols), lanes] = jnp.where(upper, piece, 0.0).astype(BF16)


def conv_forward(taps, w_conv, begin, count, cols):
    depth = w_conv.shape[2]
    width = taps.shape[1] // 3
    total = None
    for row_tap in range(3):
        for col_tap in range(3):
            window = taps[pl.ds(begin + row_tap * cols, count), pl.ds(col_tap * width, depth)]
            term = matmul(window, w_conv[row_tap, col_tap])
            total = term if total is None else total + term
    return total


def conv_backward(taps, w_conv, begin, count, cols):
    width = taps.shape[1] // 3
    total = None
    for row_tap in range(3):
        for col_tap in range(3):
            window = taps[pl.ds(begin + row_tap * cols, count), pl.ds(col_tap * width, width)]
            term = matmul(window, w_conv[2 - row_tap, 2 - col_tap], 1, 1)
            total = term if total is None else total + term
    return total


def lane_mean(value, low, size):
    return jnp.sum(jnp.where(low, value, 0.0), axis=-1, keepdims=True) / size


def edges(rows, cols, chunk):
    def body(radar, state, left, right, first, last):
        width = radar.shape[1]
        for part, lanes in ((radar, pl.ds(0, width)), (state, pl.ds(width, state.shape[1]))):
            for start in range(0, rows, chunk):
                value = part[pl.ds(start * cols, chunk * cols), :]
                left[pl.ds(start, chunk), lanes] = pick_column(value, cols, 0)
                right[pl.ds(start, chunk), lanes] = pick_column(value, cols, cols - 1)
            first[:, lanes] = part[pl.ds(0, cols), :]
            last[:, lanes] = part[pl.ds((rows - 1) * cols, cols), :]

    return body


def step_forward(rows, cols, chunk):
    def body(radar, state, row_halo, left, right, weights, bias, gain, state_grad,
             payload, sig_ref, mix_ref, cell_ref, taps):
        fill_taps(taps, (radar, state), row_halo, left, right, rows, cols, chunk)
        count = chunk * cols
        half = state.shape[1] // 2
        for start in range(0, rows, chunk):
            begin = start * cols
            part = pl.ds(begin, count)
            gates = conv_forward(taps, weights, begin, count, cols) + bias[...]
            low = low_half((count, 2 * half))
            sig = jax.nn.sigmoid(gates[:, : 2 * half])
            other = gates[:, 2 * half :]
            mix = jnp.where(low, jax.nn.sigmoid(other), jnp.tanh(other))
            held = state[part, :].astype(F32)
            terms = sig * jnp.where(low, swap_halves(mix), held)
            c_new = terms + swap_halves(terms)
            h_new = mix * jnp.tanh(c_new)
            inv_rms = lax.rsqrt(lane_mean(h_new * h_new, low, half) + EPS)
            normed = h_new * inv_rms * jnp.concatenate([gain[...], gain[...]], axis=1)
            grad = swap_halves(state_grad[part, :].astype(F32))
            payload[part, :] = jnp.where(low, normed, grad).astype(BF16)
            sig_ref[part, :] = sig
            mix_ref[part, :] = mix
            cell_ref[part, :] = jnp.where(low, h_new, c_new)

    return body


def attention(length, block):
    def body(cells, w_qkv, w_out_t, out, w_qkv_t, rows, cols, query_mask, grad_mask, values, exps, probs,
             scores, mixed, grad_q, grad_k, grad_v):
        head = pl.program_id(1)
        size = w_out_t.shape[1]
        dim = size // HEADS
        scale = dim ** (-0.5)

        @pl.when(head == 0)
        def _():
            line = cells[...].reshape(length, cells.shape[-1]).astype(F32)
            half = line.shape[1] // 2
            normed = line[:, :half].astype(BF16)
            given = swap_halves(line)[:, :half].astype(BF16)
            w_qkv_t[...] = w_qkv[...].astype(F32).T.astype(BF16)
            w_out = w_out_t[...].astype(F32).T.astype(BF16)
            rows[...] = matmul(normed, w_qkv[:, pl.ds(size, 2 * size)]).astype(BF16)
            cols[pl.ds(0, 3 * size), :] = matmul(w_qkv_t[...], normed, 1, 1).astype(BF16)
            cols[pl.ds(3 * size, size), :] = matmul(w_out, given, 1, 1).astype(BF16)
            values[pl.ds(dim, dim), :] = jnp.ones((dim, length), BF16)

        at = pl.multiple_of(head * dim, dim)
        mine = pl.ds(at, dim)
        query_cols = cols[mine, :]
        key_cols = cols[pl.ds(size + at, dim), :]
        grad_cols = cols[pl.ds(3 * size + at, dim), :]
        query_mask[...] = jnp.zeros_like(query_mask)
        grad_mask[...] = jnp.zeros_like(grad_mask)
        query_mask[mine, :] = query_cols
        grad_mask[mine, :] = grad_cols
        values[pl.ds(0, dim), :] = cols[pl.ds(2 * size + at, dim), :]
        for begin in range(0, length, block):
            part = pl.ds(begin, block)
            exps[:, part] = jnp.exp2(
                matmul(rows[:, pl.ds(0, size)], query_mask[:, part]) * (scale * LOG2E)
            ).astype(BF16)
            sums = matmul(values[...], exps[:, part])
            inverse = 1.0 / sums[dim : dim + 1]
            attended = sums[:dim] * inverse
            mixed[mine, part] = attended.astype(BF16)
            grads = cols[pl.ds(3 * size + at, dim), part].astype(F32)
            inner = jnp.sum(attended * grads, axis=0, keepdims=True)
            prob = exps[:, part].astype(F32) * inverse
            probs[:, part] = prob.astype(BF16)
            grad_prob = matmul(rows[:, pl.ds(size, size)], grad_mask[:, part])
            scores[:, part] = (prob * (grad_prob - inner)).astype(BF16)
            grad_q[mine, part] = (matmul(key_cols, scores[:, part]) * scale).astype(BF16)
        grad_k[mine, :] = (matmul(query_cols, scores[...], 1, 1) * scale).astype(BF16)
        grad_v[mine, :] = matmul(grad_cols, probs[...], 1, 1).astype(BF16)

        @pl.when(head == HEADS - 1)
        def _():
            w_out = w_out_t[...].astype(F32).T.astype(BF16)
            back = (
                matmul(grad_q[...], w_qkv_t[pl.ds(0, size), :], 0, 0)
                + matmul(grad_k[...], w_qkv_t[pl.ds(size, size), :], 0, 0)
                + matmul(grad_v[...], w_qkv_t[pl.ds(2 * size, size), :], 0, 0)
            )
            result = jnp.concatenate([matmul(mixed[...], w_out, 0, 0), back], axis=1)
            out[...] = result.astype(BF16).reshape(out.shape)

    return body


def attend(cells, w_qkv, w_out_t):
    peers, lines, cols, width = cells.shape
    length = peers * cols
    size = w_out_t.shape[1]
    block = min(512, length)
    whole = lambda array: pl.BlockSpec(array.shape, lambda i, j: (0,) * array.ndim)
    line_spec = pl.BlockSpec((peers, None, cols, width), lambda i, j: (0, i, 0, 0))
    tall = pltpu.VMEM((size, length), BF16)
    square = pltpu.VMEM((length, length), BF16)
    return pl.pallas_call(
        attention(length, block),
        out_shape=jax.ShapeDtypeStruct(cells.shape, BF16),
        grid=(lines, HEADS),
        in_specs=[line_spec, whole(w_qkv), whole(w_out_t)],
        out_specs=line_spec,
        scratch_shapes=[
            pltpu.VMEM(w_qkv.shape[::-1], BF16),
            pltpu.VMEM((length, 2 * size), BF16),
            pltpu.VMEM((4 * size, length), BF16),
            tall,
            tall,
            pltpu.VMEM((2 * size // HEADS, length), BF16),
            square,
            square,
            square,
            tall,
            tall,
            tall,
            tall,
        ],
        compiler_params=pltpu.CompilerParams(
            dimension_semantics=("arbitrary", "arbitrary"), vmem_limit_bytes=VMEM_ATTEND << 20
        ),
    )(cells, w_qkv, w_out_t)


def gate_grads(rows, cols, chunk):
    def body(back, state, state_grad, gain, sig_ref, mix_ref, cell_ref,
             new_state, grads, left, right, first, last, c_grad):
        count = chunk * cols
        half = state.shape[1] // 2
        for start in range(0, rows, chunk):
            part = pl.ds(start * cols, count)
            low = low_half((count, 2 * half))
            sig, mix, cell = sig_ref[part, :], mix_ref[part, :], cell_ref[part, :]
            arrived = back[part, :].astype(F32)
            new_state[part, :] = (cell + jnp.where(low, arrived, 0.0)).astype(BF16)
            held = state[part, :].astype(F32)
            given = state_grad[part, :].astype(F32)
            inv_rms = lax.rsqrt(lane_mean(cell * cell, low, half) + EPS)
            scaled = swap_halves(arrived) * jnp.concatenate([gain[...], gain[...]], axis=1)
            along = lane_mean(scaled * cell, low, half)
            hidden = given + inv_rms * scaled - cell * (inv_rms * inv_rms * inv_rms * along)
            hidden = jnp.where(low, hidden, swap_halves(hidden))
            c_new = jnp.where(low, swap_halves(cell), cell)
            c_tanh = jnp.tanh(c_new)
            mix_swapped = swap_halves(mix)
            out_gate = jnp.where(low, mix, mix_swapped)
            given_cell = jnp.where(low, swap_halves(given), given)
            cell_grad = given_cell + hidden * out_gate * (1.0 - c_tanh * c_tanh)
            one = cell_grad * jnp.where(low, mix_swapped, held) * sig * (1.0 - sig)
            two = jnp.where(
                low,
                hidden * c_tanh * mix * (1.0 - mix),
                cell_grad * swap_halves(sig) * (1.0 - mix * mix),
            )
            one, two = one.astype(BF16), two.astype(BF16)
            grads[part, pl.ds(0, 2 * half)] = one
            grads[part, pl.ds(2 * half, 2 * half)] = two
            c_grad[part, :] = (cell_grad * sig).astype(BF16)
            for lanes, value in ((pl.ds(0, 2 * half), one), (pl.ds(2 * half, 2 * half), two)):
                left[pl.ds(start, chunk), lanes] = pick_column(value, cols, 0)
                right[pl.ds(start, chunk), lanes] = pick_column(value, cols, cols - 1)
        first[...] = grads[pl.ds(0, cols), :]
        last[...] = grads[pl.ds((rows - 1) * cols, cols), :]

    return body


def step_backward(rows, cols, chunk):
    def body(grads, row_halo, left, right, weights, c_grad, grad_frame, grad_state, taps):
        fill_taps(taps, (grads,), row_halo, left, right, rows, cols, chunk)
        count = chunk * cols
        wide = grad_frame.shape[1]
        for start in range(0, rows, chunk):
            begin = start * cols
            part = pl.ds(begin, count)
            total = conv_backward(taps, weights, begin, count, cols).astype(BF16)
            rest = total.shape[1] - wide
            grad_frame[part, :] = total[:, :wide]
            grad_state[part, pl.ds(0, rest)] = total[:, wide:]
            grad_state[part, pl.ds(rest, rest)] = c_grad[part, pl.ds(rest, rest)]

    return body


def exchange(first_col, last_col, first_row, last_row):
    count = lax.axis_size("gx")
    forward = [(i, i + 1) for i in range(count - 1)]
    backward = [(target, source) for source, target in forward]
    left = lax.ppermute(last_col, "gx", forward)
    right = lax.ppermute(first_col, "gx", backward)
    upper = lax.axis_index("gy") == 0
    border = jnp.where(upper, last_row, first_row)
    edge = lambda column: jnp.where(upper, column[-1:], column[:1])
    sent = jnp.concatenate([border, edge(left), edge(right)], axis=0)
    received = lax.ppermute(sent, "gy", [(0, 1), (1, 0)])
    return received, left, right


def on_device(radar_frame, lstm_state, w_conv, b_gates, norm_gain, w_qkv, w_out, state_grad):
    row_count, col_count, in_channels = radar_frame.shape
    hidden = lstm_state.shape[2] // 2
    gate_dim = w_conv.shape[3]
    attn_dim = w_out.shape[0]
    cells = row_count * col_count
    chunk = min(32, row_count)
    lines = row_count // lax.axis_size("gx")
    shape = lambda *dims: jax.ShapeDtypeStruct(dims, BF16)
    wide = lambda *dims: jax.ShapeDtypeStruct(dims, F32)
    vmem = pltpu.VMEM

    radar = radar_frame.reshape(cells, in_channels)
    state = lstm_state.reshape(cells, 2 * hidden)
    given = state_grad.reshape(cells, 2 * hidden)
    depth = in_channels + 2 * hidden
    sides = call(
        edges(row_count, col_count, chunk),
        (shape(row_count, depth),) * 2 + (shape(col_count, depth),) * 2,
    )(radar, state)
    halo = exchange(*sides)
    gain = norm_gain[None]

    payload, sig, mix, cell = call(
        step_forward(row_count, col_count, chunk),
        (shape(cells, 2 * hidden),) + (wide(cells, 2 * hidden),) * 3,
        [vmem(((row_count + 2) * col_count, 3 * (in_channels + 2 * hidden)), BF16)],
    )(radar, state, *halo, w_conv, b_gates[None], gain, given)

    peers = lax.axis_size("gx")
    send = payload.reshape(peers, lines, col_count, 2 * hidden)
    lines_in = lax.all_to_all(send, "gx", split_axis=0, concat_axis=0, tiled=True)
    lines_out = attend(lines_in, w_qkv, w_out.T)
    back = lax.all_to_all(lines_out, "gx", split_axis=0, concat_axis=0, tiled=True)

    new_state, grads, left, right, first, last, c_grad = call(
        gate_grads(row_count, col_count, chunk),
        (
            shape(cells, 2 * hidden),
            shape(cells, gate_dim),
            shape(row_count, gate_dim),
            shape(row_count, gate_dim),
            shape(col_count, gate_dim),
            shape(col_count, gate_dim),
            shape(cells, 2 * hidden),
        ),
    )(back.reshape(cells, 2 * hidden), state, given, gain, sig, mix, cell)
    halo = exchange(left, right, first, last)
    grad_frame, grad_state = call(
        step_backward(row_count, col_count, chunk),
        (shape(cells, in_channels), shape(cells, 2 * hidden)),
        [vmem(((row_count + 2) * col_count, 3 * gate_dim), BF16)],
    )(grads, *halo, w_conv, c_grad)
    whole = lambda array: array.reshape(row_count, col_count, -1)
    return whole(new_state), whole(grad_frame), whole(grad_state)


def solution(mesh):
    spec = P("gy", "gx", None)
    return jax.shard_map(
        on_device,
        mesh=mesh,
        in_specs=(spec, spec, P(), P(), P(), P(), P(), spec),
        out_specs=(spec, spec, spec),
        check_vma=False,
    )
```

time: 189 us -> 140 us (0.74)
  Pallas kernels: 96.3 us -> 65.8 us
  starting transfers between devices: 49.7 us -> 23.7 us
  blocking collectives: 16.9 us -> 36.6 us
  waiting for transfers between devices: 13.4 us -> 7.71 us
  local copies, waits for them, and re-layouts: 10.6 us -> 4.99 us
    pallas_call x1 -> x2, Pallas kernels: 81 us -> 53.6 us  [the longest x1 53.2 us: attend(): pl.pallas_call(attention(length, block), out_shape=jax.ShapeDtypeStruct(c...]
    all_to_all x0 -> x1, blocking collectives: none -> 19.7 us  [on_device(): lax.all_to_all(send, 'gx', split_axis=0, concat_axis=0, tiled=True)]
    ppermute x6 -> x2, starting transfers between devices: 22.9 us -> 6.53 us  [exchange(): received = lax.ppermute(sent, 'gy', [(0, 1), (1, 0)])]
    all_to_all x1 -> x0, waiting for transfers between devices: 10.9 us -> none  [on_device(): lax.all_to_all(send, 'gx', split_axis=0, concat_axis=0, tiled=True)]
    all_to_all x1 -> x0, starting transfers between devices: 9.5 us -> none  [on_device(): lax.all_to_all(send, 'gx', split_axis=0, concat_axis=0, tiled=True)]
    ppermute x6 -> x2, waiting for transfers between devices: 0.02 us -> 4.02 us  [exchange(): received = lax.ppermute(sent, 'gy', [(0, 1), (1, 0)])]
    transpose x3 -> x0, local copies, waits for them, and re-layouts: 2.86 us -> none  [the longest x2 2.76 us: on_device(): padded[::-1, ::-1].transpose(0, 1, 3, 2).reshape(3, 3 * gate_dim, -1)]
    slice x6 -> x0, local copies, waits for them, and re-layouts: 2.3 us -> none  [the longest x1 1.14 us: on_device(): radar_frame[:, 0]]
  transfers between devices with their start and end apart: 11 -> 6, of which waited for: 3 -> 4; matrix products, arithmetic and copies ran while one was open for 4% -> 0% of each run, Pallas kernels for 0% -> 0%
where the time goes in v2:
time: 140 us
  Pallas kernels  65.8 us (47%)
  blocking collectives  36.6 us (26%)
  starting transfers between devices  23.7 us (17%)
  waiting for transfers between devices  7.71 us (6%)
  local copies, waits for them, and re-layouts  4.99 us (4%)
    pallas_call x1, Pallas kernels, attend(): pl.pallas_call(attention(length, block), out_shape=jax.ShapeDtypeStruct(c...  53.2 us
    all_to_all x1, blocking collectives, on_device(): lax.all_to_all(send, 'gx', split_axis=0, concat_axis=0, tiled=True)  19.7 us
    all_to_all x1, blocking collectives, on_device(): lax.all_to_all(lines_out, 'gx', split_axis=0, concat_axis=0, tiled=True)  16.9 us
    ppermute x2, starting transfers between devices, exchange(): right = lax.ppermute(first_col, 'gx', backward)  13.2 us
    ppermute x2, starting transfers between devices, exchange(): received = lax.ppermute(sent, 'gy', [(0, 1), (1, 0)])  6.53 us
    unnamed x22, local copies, waits for them, and re-layouts  4.99 us
    pallas_call x1, Pallas kernels, on_device(): call(step_forward(row_count, col_count, chunk), (shape(cells, 2 * hidden)...  4.15 us
    pallas_call x1, Pallas kernels, on_device(): call(step_backward(row_count, col_count, chunk), (shape(cells, in_channel...  4.14 us
  transfers between devices with their start and end apart: 6, of which 4 were waited for; matrix products, arithmetic and copies ran while one was open for 0% of the time, Pallas kernels for 0%

profile of v2, /device:TPU:2, one launch (start us, length us, event | category | flops | bytes accessed | tf_op | source)
XLA Modules:
  0.0 139.5 jit_solution(11543048593719145795)
XLA Ops:
  0.6 1.0 copy-done
  1.7 1.0 copy-done.5
  2.7 0.4 shard_map.103
  3.1 1.9 %collective-permute-start = (bf16[128,256]{1,0:T(8,128)(2,1)S(1)}, bf16[128,256]{1,0:T(8,128)(2,1)S(1)}, u32[]{:S(2)}, u32[]{:S(2)}) collective-permute-start(bf16[128,256]{1,0:T(8,128)(2,1)S(1)} %get-tuple-element.22), channel_id=1, source_target_pairs={{0,1},{1,2},{2,3},{3,4},{4,5},{5,6},{6,7},{7,8},{8,9},{9,10},{10,1... | collective-permute-start | bytes 196616 | tf_op jit(solution)/shard_map/ppermute | solution.py:329
  5.1 6.7 %collective-permute-start.1 = (bf16[128,256]{1,0:T(8,128)(2,1)S(1)}, bf16[128,256]{1,0:T(8,128)(2,1)S(1)}, u32[]{:S(2)}, u32[]{:S(2)}) collective-permute-start(bf16[128,256]{1,0:T(8,128)(2,1)S(1)} %get-tuple-element.23), channel_id=1, source_target_pairs={{1,0},{2,1},{3,2},{4,3},{5,4},{6,5},{7,6},{8,7},{9,8},{10,9},{11,1... | collective-permute-start | bytes 196616 | tf_op jit(solution)/shard_map/ppermute | solution.py:330
  11.8 1.8 %collective-permute-done.1.right = bf16[128,256]{1,0:T(8,128)(2,1)S(1)} collective-permute-done((bf16[128,256]{1,0:T(8,128)(2,1)S(1)}, bf16[128,256]{1,0:T(8,128)(2,1)S(1)}, u32[]{:S(2)}, u32[]{:S(2)}) %collective-permute-start.1) | collective-permute-done | bytes 65568 | tf_op jit(solution)/shard_map/ppermute | solution.py:330
  13.6 3.3 %collective-permute-start.2 = (bf16[18,256]{1,0:T(8,128)(2,1)S(1)}, bf16[18,256]{1,0:T(8,128)(2,1)S(1)}, u32[]{:S(2)}, u32[]{:S(2)}) collective-permute-start(bf16[18,256]{1,0:T(8,128)(2,1)S(1)} %pad_maximum_fusion), channel_id=1, source_target_pairs={{0,64},{64,0},{1,65},{65,1},{2,66},{66,2},{3,67},{67,3},{4,68},{68... | collective-permute-start | bytes 27656 | tf_op jit(solution)/shard_map/ppermute | solution.py:335
  16.9 2.0 %collective-permute-done.2.row_halo = bf16[18,256]{1,0:T(8,128)(2,1)S(1)} collective-permute-done((bf16[18,256]{1,0:T(8,128)(2,1)S(1)}, bf16[18,256]{1,0:T(8,128)(2,1)S(1)}, u32[]{:S(2)}, u32[]{:S(2)}) %collective-permute-start.2) | collective-permute-done | bytes 9248 | tf_op jit(solution)/shard_map/ppermute | solution.py:335
  18.9 0.6 copy-done.9
  19.6 0.0 copy-done.10
  19.6 1.2 copy-done.2
  20.8 1.0 copy-done.6
  21.8 4.1 %shard_map.104 = (bf16[2048,128]{1,0:T(8,128)(2,1)S(1)}, f32[2048,128]{1,0:T(8,128)S(1)}, f32[2048,128]{1,0:T(8,128)S(1)}, f32[2048,128]{1,0:T(8,128)S(1)}) custom-call(bf16[2048,128]{1,0:T(8,128)(2,1)S(1)} %bitcast.18, bf16[2048,128]{1,0:T(8,128)(2,1)S(1)} %bitcast.12, bf16[18,256]{1,0:T(8,128)(2,1)S(1)} %collective-permute-done.2.row_halo, ...), custom_call_target="tpu_custom_call" | custom-call | tf_op jit(solution)/shard_map/pallas_call | solution.py:362
  26.0 0.0 copy-start.7
  26.0 19.7 %all_to_all.10.cells = bf16[64,2,16,128]{3,2,1,0:T(8,128)(2,1)S(1)} all-to-all(bf16[64,2,16,128]{3,2,1,0:T(8,128)(2,1)S(1)} %bitcast.19), channel_id=1, replica_groups=mesh['gy'=2,'gx'=64] {'gx'}, dimensions={0} | all-to-all | bytes 1048576 | tf_op jit(solution)/shard_map/all_to_all | solution.py:370
  45.6 53.2 %shard_map.105 = bf16[64,2,16,128]{3,2,1,0:T(8,128)(2,1)S(1)} custom-call(bf16[64,2,16,128]{3,2,1,0:T(8,128)(2,1)S(1)} %all_to_all.10.cells, bf16[64,384]{1,0:T(8,128)(2,1)S(1)} %copy-done.7, bf16[64,128]{1,0:T(8,128)(2,1)S(1)} %bitcast.20), custom_call_target="tpu_custom_call" | custom-call | tf_op jit(solution)/shard_map/pallas_call | solution.py:238
  98.9 16.9 %all_to_all.11 = bf16[64,2,16,128]{3,2,1,0:T(8,128)(2,1)S(1)} all-to-all(bf16[64,2,16,128]{3,2,1,0:T(8,128)(2,1)S(1)} %shard_map.105), channel_id=1, replica_groups=mesh['gy'=2,'gx'=64] {'gx'}, dimensions={0} | all-to-all | bytes 1048576 | tf_op jit(solution)/shard_map/all_to_all | solution.py:372
  115.8 3.9 %shard_map.106 = (bf16[2048,128]{1,0:T(8,128)(2,1)}, bf16[2048,256]{1,0:T(8,128)(2,1)S(1)}, bf16[128,256]{1,0:T(8,128)(2,1)S(1)}, bf16[128,256]{1,0:T(8,128)(2,1...) custom-call(bf16[2048,128]{1,0:T(8,128)(2,1)S(1)} %bitcast.14, ...), custom_call_target="tpu_custom_call" | custom-call | tf_op jit(solution)/shard_map/pallas_call | solution.py:374
  119.6 2.0 %collective-permute-start.3 = (bf16[128,256]{1,0:T(8,128)(2,1)S(1)}, bf16[128,256]{1,0:T(8,128)(2,1)S(1)}, u32[]{:S(2)}, u32[]{:S(2)}) collective-permute-start(bf16[128,256]{1,0:T(8,128)(2,1)S(1)} %get-tuple-element.32), channel_id=1, source_target_pairs={{0,1},{1,2},{2,3},{3,4},{4,5},{5,6},{6,7},{7,8},{8,9},{9,10},{10,1... | collective-permute-start | bytes 196616 | tf_op jit(solution)/shard_map/ppermute | solution.py:329
  121.6 6.6 %collective-permute-start.4 = (bf16[128,256]{1,0:T(8,128)(2,1)S(1)}, bf16[128,256]{1,0:T(8,128)(2,1)S(1)}, u32[]{:S(2)}, u32[]{:S(2)}) collective-permute-start(bf16[128,256]{1,0:T(8,128)(2,1)S(1)} %get-tuple-element.33), channel_id=1, source_target_pairs={{1,0},{2,1},{3,2},{4,3},{5,4},{6,5},{7,6},{8,7},{9,8},{10,9},{11,1... | collective-permute-start | bytes 196616 | tf_op jit(solution)/shard_map/ppermute | solution.py:330
  128.2 1.8 %collective-permute-done.4.right = bf16[128,256]{1,0:T(8,128)(2,1)S(1)} collective-permute-done((bf16[128,256]{1,0:T(8,128)(2,1)S(1)}, bf16[128,256]{1,0:T(8,128)(2,1)S(1)}, u32[]{:S(2)}, u32[]{:S(2)}) %collective-permute-start.4) | collective-permute-done | bytes 65568 | tf_op jit(solution)/shard_map/ppermute | solution.py:330
  130.1 3.3 %collective-permute-start.5 = (bf16[18,256]{1,0:T(8,128)(2,1)S(1)}, bf16[18,256]{1,0:T(8,128)(2,1)S(1)}, u32[]{:S(2)}, u32[]{:S(2)}) collective-permute-start(bf16[18,256]{1,0:T(8,128)(2,1)S(1)} %pad_maximum_fusion.1), channel_id=1, source_target_pairs={{0,64},{64,0},{1,65},{65,1},{2,66},{66,2},{3,67},{67,3},{4,68},{68... | collective-permute-start | bytes 27656 | tf_op jit(solution)/shard_map/ppermute | solution.py:335
  133.4 2.0 %collective-permute-done.5.row_halo = bf16[18,256]{1,0:T(8,128)(2,1)S(1)} collective-permute-done((bf16[18,256]{1,0:T(8,128)(2,1)S(1)}, bf16[18,256]{1,0:T(8,128)(2,1)S(1)}, u32[]{:S(2)}, u32[]{:S(2)}) %collective-permute-start.5) | collective-permute-done | bytes 9248 | tf_op jit(solution)/shard_map/ppermute | solution.py:335
  135.4 4.1 %shard_map.107 = (bf16[2048,128]{1,0:T(8,128)(2,1)}, bf16[2048,128]{1,0:T(8,128)(2,1)}) custom-call(bf16[2048,256]{1,0:T(8,128)(2,1)S(1)} %get-tuple-element.29.grads, bf16[18,256]{1,0:T(8,128)(2,1)S(1)} %collective-permute-done.5.row_halo, bf16[128,256]{1,0:T(8,128)(2,1)S(1)} %collective-permute-done.3.left, ...), custom_call_target="tpu_custom_call" | custom-call | tf_op jit(solution)/shard_map/pallas_call | solution.py:387
  (25 shorter events, 0.1 us)
Async XLA Ops:
  0.6 1.0 copy-start
  1.7 1.0 copy-start.5
  2.7 16.2 %copy-start.1 = (bf16[128,16,128]{2,1,0:T(8,128)(2,1)S(1)}, bf16[128,16,128]{2,1,0:T(8,128)(2,1)}, u32[]{:S(2)}) copy-start(bf16[128,16,128]{2,1,0:T(8,128)(2,1)} %param.9) | copy-start | bytes 1572868
  2.7 16.2 %copy-start.4 = (bf16[128,16,128]{2,1,0:T(8,128)(2,1)S(1)}, bf16[128,16,128]{2,1,0:T(8,128)(2,1)}, u32[]{:S(2)}) copy-start(bf16[128,16,128]{2,1,0:T(8,128)(2,1)} %param.15) | copy-start | bytes 1572868
  3.1 8.6 %collective-permute-start = (bf16[128,256]{1,0:T(8,128)(2,1)S(1)}, bf16[128,256]{1,0:T(8,128)(2,1)S(1)}, u32[]{:S(2)}, u32[]{:S(2)}) collective-permute-start(bf16[128,256]{1,0:T(8,128)(2,1)S(1)} %get-tuple-element.22), channel_id=1, source_target_pairs={{0,1},{1,2},{2,3},{3,4},{4,5},{5,6},{6,7},{7,8},{8,9},{9,10},{10,1... | collective-permute-start | bytes 196616 | tf_op jit(solution)/shard_map/ppermute | solution.py:329
  5.1 8.5 %collective-permute-start.1 = (bf16[128,256]{1,0:T(8,128)(2,1)S(1)}, bf16[128,256]{1,0:T(8,128)(2,1)S(1)}, u32[]{:S(2)}, u32[]{:S(2)}) collective-permute-start(bf16[128,256]{1,0:T(8,128)(2,1)S(1)} %get-tuple-element.23), channel_id=1, source_target_pairs={{1,0},{2,1},{3,2},{4,3},{5,4},{6,5},{7,6},{8,7},{9,8},{10,9},{11,1... | collective-permute-start | bytes 196616 | tf_op jit(solution)/shard_map/ppermute | solution.py:330
  13.6 5.3 %collective-permute-start.2 = (bf16[18,256]{1,0:T(8,128)(2,1)S(1)}, bf16[18,256]{1,0:T(8,128)(2,1)S(1)}, u32[]{:S(2)}, u32[]{:S(2)}) collective-permute-start(bf16[18,256]{1,0:T(8,128)(2,1)S(1)} %pad_maximum_fusion), channel_id=1, source_target_pairs={{0,64},{64,0},{1,65},{65,1},{2,66},{66,2},{3,67},{67,3},{4,68},{68... | collective-permute-start | bytes 27656 | tf_op jit(solution)/shard_map/ppermute | solution.py:335
  18.9 0.7 copy-start.9
  18.9 0.7 copy-start.10
  19.6 1.2 copy-start.2
  20.8 1.0 copy-start.6
  26.0 19.7 %copy-start.7 = (bf16[64,384]{1,0:T(8,128)(2,1)S(1)}, bf16[64,384]{1,0:T(8,128)(2,1)}, u32[]{:S(2)}) copy-start(bf16[64,384]{1,0:T(8,128)(2,1)} %w_qkv.1) | copy-start | bytes 147460
  26.0 19.7 %copy-start.8 = (bf16[128,64]{0,1:T(8,128)(2,1)S(1)}, bf16[128,64]{0,1:T(8,128)(2,1)}, u32[]{:S(2)}) copy-start(bf16[128,64]{0,1:T(8,128)(2,1)} %param.14) | copy-start | bytes 49156
  115.8 19.6 %copy-start.3 = (bf16[3,3,192,256]{3,2,1,0:T(8,128)(2,1)S(1)}, bf16[3,3,192,256]{3,2,1,0:T(8,128)(2,1)}, u32[]{:S(2)}) copy-start(bf16[3,3,192,256]{3,2,1,0:T(8,128)(2,1)} %weights.3) | copy-start | bytes 2654212
  119.6 8.6 %collective-permute-start.3 = (bf16[128,256]{1,0:T(8,128)(2,1)S(1)}, bf16[128,256]{1,0:T(8,128)(2,1)S(1)}, u32[]{:S(2)}, u32[]{:S(2)}) collective-permute-start(bf16[128,256]{1,0:T(8,128)(2,1)S(1)} %get-tuple-element.32), channel_id=1, source_target_pairs={{0,1},{1,2},{2,3},{3,4},{4,5},{5,6},{6,7},{7,8},{8,9},{9,10},{10,1... | collective-permute-start | bytes 196616 | tf_op jit(solution)/shard_map/ppermute | solution.py:329
  121.6 8.5 %collective-permute-start.4 = (bf16[128,256]{1,0:T(8,128)(2,1)S(1)}, bf16[128,256]{1,0:T(8,128)(2,1)S(1)}, u32[]{:S(2)}, u32[]{:S(2)}) collective-permute-start(bf16[128,256]{1,0:T(8,128)(2,1)S(1)} %get-tuple-element.33), channel_id=1, source_target_pairs={{1,0},{2,1},{3,2},{4,3},{5,4},{6,5},{7,6},{8,7},{9,8},{10,9},{11,1... | collective-permute-start | bytes 196616 | tf_op jit(solution)/shard_map/ppermute | solution.py:330
  130.1 5.3 %collective-permute-start.5 = (bf16[18,256]{1,0:T(8,128)(2,1)S(1)}, bf16[18,256]{1,0:T(8,128)(2,1)S(1)}, u32[]{:S(2)}, u32[]{:S(2)}) collective-permute-start(bf16[18,256]{1,0:T(8,128)(2,1)S(1)} %pad_maximum_fusion.1), channel_id=1, source_target_pairs={{0,64},{64,0},{1,65},{65,1},{2,66},{66,2},{3,67},{67,3},{4,68},{68... | collective-permute-start | bytes 27656 | tf_op jit(solution)/shard_map/ppermute | solution.py:335

commit v3 on v2

--- a/solution.py
+++ b/solution.py
@@ -19,10 +19,12 @@
     )
 
 
-def call(body, out_shape, scratch=(), vmem=24):
+def call(body, out_shape, scratch=(), in_place=(), count=0, vmem=24):
+    spaces = [pltpu.HBM if index in in_place else pltpu.VMEM for index in range(count)]
     return pl.pallas_call(
         body,
         out_shape=out_shape,
+        in_specs=[pl.BlockSpec(memory_space=space) for space in spaces],
         scratch_shapes=list(scratch),
         compiler_params=pltpu.CompilerParams(vmem_limit_bytes=vmem << 20),
     )
@@ -80,10 +82,10 @@
             taps[target, pl.ds(width + column, part_width)] = value
             taps[target, pl.ds(2 * width + column, part_width)] = after.astype(BF16)
             column += part_width
-    halo = row_halo[pl.ds(0, cols), :].astype(F32)
+    halo = row_halo[...].astype(F32)
     where = column_of(halo.shape, cols)
-    first = jnp.broadcast_to(row_halo[pl.ds(cols, 1), :].astype(F32), halo.shape)
-    last = jnp.broadcast_to(row_halo[pl.ds(cols + 1, 1), :].astype(F32), halo.shape)
+    first = jnp.broadcast_to(left[pl.ds(rows, 1), :].astype(F32), halo.shape)
+    last = jnp.broadcast_to(right[pl.ds(rows, 1), :].astype(F32), halo.shape)
     before = jnp.where(where == 0, first, pltpu.roll(halo, 1, axis=0))
     after = jnp.where(where == cols - 1, last, pltpu.roll(halo, cols - 1, axis=0))
     for index, piece in enumerate((before, halo, after)):
@@ -119,24 +121,57 @@
     return jnp.sum(jnp.where(low, value, 0.0), axis=-1, keepdims=True) / size
 
 
+def fetch(source, target, sems, pieces):
+    size = source.shape[0] // pieces
+    copies = [
+        pltpu.make_async_copy(
+            source.at[pl.ds(index * size, size)], target.at[pl.ds(index * size, size)], sems.at[index]
+        )
+        for index in range(pieces)
+    ]
+    for copy in copies:
+        copy.start()
+    return copies
+
+
 def edges(rows, cols, chunk):
-    def body(radar, state, left, right, first, last):
+    pieces = rows // chunk
+
+    def body(radar, state, bias_in, gain_in, left, right, radar_here, state_here, bias, gain,
+             radar_sems, state_sems, sems):
+        small = (
+            pltpu.make_async_copy(bias_in, bias, sems.at[0]),
+            pltpu.make_async_copy(gain_in, gain, sems.at[1]),
+        )
+        ready = (
+            fetch(radar, radar_here, radar_sems, pieces),
+            fetch(state, state_here, state_sems, pieces),
+        )
+        for copy in small:
+            copy.start()
         width = radar.shape[1]
-        for part, lanes in ((radar, pl.ds(0, width)), (state, pl.ds(width, state.shape[1]))):
-            for start in range(0, rows, chunk):
-                value = part[pl.ds(start * cols, chunk * cols), :]
-                left[pl.ds(start, chunk), lanes] = pick_column(value, cols, 0)
-                right[pl.ds(start, chunk), lanes] = pick_column(value, cols, cols - 1)
-            first[:, lanes] = part[pl.ds(0, cols), :]
-            last[:, lanes] = part[pl.ds((rows - 1) * cols, cols), :]
+        for index in range(pieces):
+            for part, copies, lanes in (
+                (radar_here, ready[0], pl.ds(0, width)),
+                (state_here, ready[1], pl.ds(width, state.shape[1])),
+            ):
+                copies[index].wait()
+                value = part[pl.ds(index * chunk * cols, chunk * cols), :]
+                left[pl.ds(index * chunk, chunk), lanes] = pick_column(value, cols, 0)
+                right[pl.ds(index * chunk, chunk), lanes] = pick_column(value, cols, cols - 1)
+        for copy in small:
+            copy.wait()
 
     return body
 
 
 def step_forward(rows, cols, chunk):
-    def body(radar, state, row_halo, left, right, weights, bias, gain, state_grad,
-             payload, sig_ref, mix_ref, cell_ref, taps):
+    def body(radar, state, row_halo, left, right, weights_out, bias, gain, grad_out,
+             payload, sig_ref, mix_ref, cell_ref, taps, weights, state_grad, sems, grad_sems):
+        later = fetch(weights_out, weights, sems, 3) + fetch(grad_out, state_grad, grad_sems, 1)
         fill_taps(taps, (radar, state), row_halo, left, right, rows, cols, chunk)
+        for copy in later:
+            copy.wait()
         count = chunk * cols
         half = state.shape[1] // 2
         for start in range(0, rows, chunk):
@@ -204,10 +239,10 @@
             mixed[mine, part] = attended.astype(BF16)
             grads = cols[pl.ds(3 * size + at, dim), part].astype(F32)
             inner = jnp.sum(attended * grads, axis=0, keepdims=True)
-            prob = exps[:, part].astype(F32) * inverse
-            probs[:, part] = prob.astype(BF16)
+            prob = exps[:, part] * inverse.astype(BF16)
+            probs[:, part] = prob
             grad_prob = matmul(rows[:, pl.ds(size, size)], grad_mask[:, part])
-            scores[:, part] = (prob * (grad_prob - inner)).astype(BF16)
+            scores[:, part] = prob * (grad_prob - inner).astype(BF16)
             grad_q[mine, part] = (matmul(key_cols, scores[:, part]) * scale).astype(BF16)
         grad_k[mine, :] = (matmul(query_cols, scores[...], 1, 1) * scale).astype(BF16)
         grad_v[mine, :] = matmul(grad_cols, probs[...], 1, 1).astype(BF16)
@@ -262,45 +297,61 @@
     )(cells, w_qkv, w_out_t)
 
 
-def gate_grads(rows, cols, chunk):
+def gate_grads(part, count, back, state, state_grad, gain, sig_ref, mix_ref, cell_ref):
+    half = state.shape[1] // 2
+    low = low_half((count, 2 * half))
+    sig, mix, cell = sig_ref[part, :], mix_ref[part, :], cell_ref[part, :]
+    arrived = back[part, :].astype(F32)
+    new_state = cell + jnp.where(low, arrived, 0.0)
+    held = state[part, :].astype(F32)
+    given = state_grad[part, :].astype(F32)
+    inv_rms = lax.rsqrt(lane_mean(cell * cell, low, half) + EPS)
+    scaled = swap_halves(arrived) * jnp.concatenate([gain[...], gain[...]], axis=1)
+    along = lane_mean(scaled * cell, low, half)
+    hidden = given + inv_rms * scaled - cell * (inv_rms * inv_rms * inv_rms * along)
+    hidden = jnp.where(low, hidden, swap_halves(hidden))
+    c_new = jnp.where(low, swap_halves(cell), cell)
+    c_tanh = jnp.tanh(c_new)
+    mix_swapped = swap_halves(mix)
+    out_gate = jnp.where(low, mix, mix_swapped)
+    given_cell = jnp.where(low, swap_halves(given), given)
+    cell_grad = given_cell + hidden * out_gate * (1.0 - c_tanh * c_tanh)
+    one = cell_grad * jnp.where(low, mix_swapped, held) * sig * (1.0 - sig)
+    two = jnp.where(
+        low,
+        hidden * c_tanh * mix * (1.0 - mix),
+        cell_grad * swap_halves(sig) * (1.0 - mix * mix),
+    )
+    return one.astype(BF16), two.astype(BF16), cell_grad * sig, new_state
+
+
+def border_grads(rows, cols):
+    def body(*refs):
+        out = refs[-1]
+        begin = jnp.where(lax.axis_index("gy") == 0, (rows - 1) * cols, 0)
+        part = pl.ds(pl.multiple_of(begin, cols), cols)
+        one, two, _, _ = gate_grads(part, cols, *refs[:-1])
+        out[...] = jnp.concatenate([one, two], axis=1)
+
+    return body
+
+
+def all_grads(rows, cols, chunk):
     def body(back, state, state_grad, gain, sig_ref, mix_ref, cell_ref,
-             new_state, grads, left, right, first, last, c_grad):
+             new_state, grads, left, right, c_grad):
         count = chunk * cols
-        half = state.shape[1] // 2
+        width = state.shape[1]
         for start in range(0, rows, chunk):
             part = pl.ds(start * cols, count)
-            low = low_half((count, 2 * half))
-            sig, mix, cell = sig_ref[part, :], mix_ref[part, :], cell_ref[part, :]
-            arrived = back[part, :].astype(F32)
-            new_state[part, :] = (cell + jnp.where(low, arrived, 0.0)).astype(BF16)
-            held = state[part, :].astype(F32)
-            given = state_grad[part, :].astype(F32)
-            inv_rms = lax.rsqrt(lane_mean(cell * cell, low, half) + EPS)
-            scaled = swap_halves(arrived) * jnp.concatenate([gain[...], gain[...]], axis=1)
-            along = lane_mean(scaled * cell, low, half)
-            hidden = given + inv_rms * scaled - cell * (inv_rms * inv_rms * inv_rms * along)
-            hidden = jnp.where(low, hidden, swap_halves(hidden))
-            c_new = jnp.where(low, swap_halves(cell), cell)
-            c_tanh = jnp.tanh(c_new)
-            mix_swapped = swap_halves(mix)
-            out_gate = jnp.where(low, mix, mix_swapped)
-            given_cell = jnp.where(low, swap_halves(given), given)
-            cell_grad = given_cell + hidden * out_gate * (1.0 - c_tanh * c_tanh)
-            one = cell_grad * jnp.where(low, mix_swapped, held) * sig * (1.0 - sig)
-            two = jnp.where(
-                low,
-                hidden * c_tanh * mix * (1.0 - mix),
-                cell_grad * swap_halves(sig) * (1.0 - mix * mix),
+            one, two, cell, new = gate_grads(
+                part, count, back, state, state_grad, gain, sig_ref, mix_ref, cell_ref
             )
-            one, two = one.astype(BF16), two.astype(BF16)
-            grads[part, pl.ds(0, 2 * half)] = one
-            grads[part, pl.ds(2 * half, 2 * half)] = two
-            c_grad[part, :] = (cell_grad * sig).astype(BF16)
-            for lanes, value in ((pl.ds(0, 2 * half), one), (pl.ds(2 * half, 2 * half), two)):
+            new_state[part, :] = new.astype(BF16)
+            c_grad[part, :] = cell.astype(BF16)
+            for lanes, value in ((pl.ds(0, width), one), (pl.ds(width, width), two)):
+                grads[part, lanes] = value
                 left[pl.ds(start, chunk), lanes] = pick_column(value, cols, 0)
                 right[pl.ds(start, chunk), lanes] = pick_column(value, cols, cols - 1)
-        first[...] = grads[pl.ds(0, cols), :]
-        last[...] = grads[pl.ds((rows - 1) * cols, cols), :]
 
     return body
 
@@ -322,18 +373,18 @@
     return body
 
 
-def exchange(first_col, last_col, first_row, last_row):
+def swap_border(first_row, last_row):
+    border = jnp.where(lax.axis_index("gy") == 0, last_row, first_row)
+    return lax.ppermute(border, "gy", [(0, 1), (1, 0)])
+
+
+def exchange_columns(first_col, last_col, row_halo):
     count = lax.axis_size("gx")
     forward = [(i, i + 1) for i in range(count - 1)]
     backward = [(target, source) for source, target in forward]
-    left = lax.ppermute(last_col, "gx", forward)
-    right = lax.ppermute(first_col, "gx", backward)
-    upper = lax.axis_index("gy") == 0
-    border = jnp.where(upper, last_row, first_row)
-    edge = lambda column: jnp.where(upper, column[-1:], column[:1])
-    sent = jnp.concatenate([border, edge(left), edge(right)], axis=0)
-    received = lax.ppermute(sent, "gy", [(0, 1), (1, 0)])
-    return received, left, right
+    left = lax.ppermute(jnp.concatenate([last_col, row_halo[-1:]], axis=0), "gx", forward)
+    right = lax.ppermute(jnp.concatenate([first_col, row_halo[:1]], axis=0), "gx", backward)
+    return row_halo, left, right
 
 
 def on_device(radar_frame, lstm_state, w_conv, b_gates, norm_gain, w_qkv, w_out, state_grad):
@@ -352,18 +403,35 @@
     state = lstm_state.reshape(cells, 2 * hidden)
     given = state_grad.reshape(cells, 2 * hidden)
     depth = in_channels + 2 * hidden
-    sides = call(
+    both = lambda row: jnp.concatenate([radar_frame[row], lstm_state[row]], axis=-1)
+    row_halo = swap_border(both(0), both(-1))
+    sems = pltpu.SemaphoreType.DMA
+    pieces = row_count // chunk
+    in_hbm = lambda array: pltpu.with_memory_space_constraint(array, pltpu.HBM)
+    bias, gain = b_gates[None], norm_gain[None]
+    left, right, radar, state, bias, gain = call(
         edges(row_count, col_count, chunk),
-        (shape(row_count, depth),) * 2 + (shape(col_count, depth),) * 2,
-    )(radar, state)
-    halo = exchange(*sides)
-    gain = norm_gain[None]
+        (shape(row_count, depth),) * 2
+        + (shape(*radar.shape), shape(*state.shape), wide(*bias.shape), wide(*gain.shape)),
+        [sems((pieces,)), sems((pieces,)), sems((2,))],
+        (0, 1, 2, 3),
+        4,
+    )(in_hbm(radar), in_hbm(state), in_hbm(bias), in_hbm(gain))
+    halo = exchange_columns(left, right, row_halo)
 
     payload, sig, mix, cell = call(
         step_forward(row_count, col_count, chunk),
         (shape(cells, 2 * hidden),) + (wide(cells, 2 * hidden),) * 3,
-        [vmem(((row_count + 2) * col_count, 3 * (in_channels + 2 * hidden)), BF16)],
-    )(radar, state, *halo, w_conv, b_gates[None], gain, given)
+        [
+            vmem(((row_count + 2) * col_count, 3 * depth), BF16),
+            vmem(w_conv.shape, BF16),
+            vmem(given.shape, BF16),
+            sems((3,)),
+            sems((1,)),
+        ],
+        (5, 8),
+        9,
+    )(radar, state, *halo, in_hbm(w_conv), bias, gain, in_hbm(given))
 
     peers = lax.axis_size("gx")
     send = payload.reshape(peers, lines, col_count, 2 * hidden)
@@ -371,23 +439,27 @@
     lines_out = attend(lines_in, w_qkv, w_out.T)
     back = lax.all_to_all(lines_out, "gx", split_axis=0, concat_axis=0, tiled=True)
 
-    new_state, grads, left, right, first, last, c_grad = call(
-        gate_grads(row_count, col_count, chunk),
+    back = back.reshape(cells, 2 * hidden)
+    operands = (back, state, given, gain, sig, mix, cell)
+    border = call(border_grads(row_count, col_count), shape(col_count, gate_dim), count=7)(*operands)
+    row_halo = lax.ppermute(border, "gy", [(0, 1), (1, 0)])
+    new_state, grads, left, right, c_grad = call(
+        all_grads(row_count, col_count, chunk),
         (
             shape(cells, 2 * hidden),
             shape(cells, gate_dim),
             shape(row_count, gate_dim),
             shape(row_count, gate_dim),
-            shape(col_count, gate_dim),
-            shape(col_count, gate_dim),
             shape(cells, 2 * hidden),
         ),
-    )(back.reshape(cells, 2 * hidden), state, given, gain, sig, mix, cell)
-    halo = exchange(left, right, first, last)
+        count=7,
+    )(*operands)
+    halo = exchange_columns(left, right, row_halo)
     grad_frame, grad_state = call(
         step_backward(row_count, col_count, chunk),
         (shape(cells, in_channels), shape(cells, 2 * hidden)),
         [vmem(((row_count + 2) * col_count, 3 * gate_dim), BF16)],
+        count=6,
     )(grads, *halo, w_conv, c_grad)
     whole = lambda array: array.reshape(row_count, col_count, -1)
     return whole(new_state), whole(grad_frame), whole(grad_state)

time: 140 us -> 133 us (0.950)
  local copies, waits for them, and re-layouts: 4.99 us -> 0.78 us
  blocking collectives: 36.6 us -> 33.9 us
  starting transfers between devices: 23.7 us -> 21.7 us
    unnamed x22 -> x8, local copies, waits for them, and re-layouts: 4.99 us -> 0.02 us
    all_to_all x1, blocking collectives: 19.7 us -> 16.9 us  [on_device(): lax.all_to_all(send, 'gx', split_axis=0, concat_axis=0, tiled=True)]
    pallas_call x1, Pallas kernels: 53.2 us -> 50.9 us  [attend(): pl.pallas_call(attention(length, block), out_shape=jax.ShapeDtypeStruct(c...]
    pallas_call x1, Pallas kernels: 0.4 us -> 2.35 us  [on_device(): call(edges(row_count, col_count, chunk), (shape(row_count, depth),) * 2 +...]
    ppermute x6, starting transfers between devices: 23.7 us -> 21.7 us  [the longest x2 11.8 us: exchange_columns(): lax.ppermute(jnp.concatenate([first_col, row_halo[:1]], axis=0), 'gx', ba...]
    pallas_call x1 -> x2, Pallas kernels: 3.87 us -> 4.08 us  [the longest x1 3.85 us: on_device(): call(all_grads(row_count, col_count, chunk), (shape(cells, 2 * hidden), s...]
  transfers between devices with their start and end apart: 6 -> 6, of which waited for: 4 -> 2; matrix products, arithmetic and copies ran while one was open for 0% -> 0% of each run, Pallas kernels for 0% -> 5%
where the time goes in v3:
time: 133 us; the launch traced here: 132 us
  Pallas kernels  66.3 us (50%)
  blocking collectives  33.9 us (25%)
  starting transfers between devices  21.7 us (16%)
  waiting for transfers between devices  8.63 us (6%)
    pallas_call x1, Pallas kernels, attend(): pl.pallas_call(attention(length, block), out_shape=jax.ShapeDtypeStruct(c...  50.9 us
    all_to_all x1, blocking collectives, on_device(): lax.all_to_all(lines_out, 'gx', split_axis=0, concat_axis=0, tiled=True)  17 us
    all_to_all x1, blocking collectives, on_device(): lax.all_to_all(send, 'gx', split_axis=0, concat_axis=0, tiled=True)  16.9 us
    ppermute x2, starting transfers between devices, exchange_columns(): lax.ppermute(jnp.concatenate([first_col, row_halo[:1]], axis=0), 'gx', ba...  11.8 us
    ppermute x2, waiting for transfers between devices, exchange_columns(): lax.ppermute(jnp.concatenate([last_col, row_halo[-1:]], axis=0), 'gx', fo...  6.73 us
    pallas_call x1, Pallas kernels, on_device(): call(step_forward(row_count, col_count, chunk), (shape(cells, 2 * hidden)...  4.8 us
    pallas_call x1, Pallas kernels, on_device(): call(step_backward(row_count, col_count, chunk), (shape(cells, in_channel...  4.14 us
    pallas_call x1, Pallas kernels, on_device(): call(all_grads(row_count, col_count, chunk), (shape(cells, 2 * hidden), s...  3.85 us
  transfers between devices with their start and end apart: 6, of which 2 were waited for; matrix products, arithmetic and copies ran while one was open for 0% of the time, Pallas kernels for 5%

profile of v3, /device:TPU:2, one launch (start us, length us, event | category | flops | bytes accessed | tf_op | source)
XLA Modules:
  0.0 132.1 jit_solution(10598428577173287965)
XLA Ops:
  0.6 0.7 slice_bitcast_fusion
  1.4 3.3 %collective-permute-start = (bf16[16,256]{1,0:T(8,128)(2,1)S(1)}, bf16[16,256]{1,0:T(8,128)(2,1)S(1)}, u32[]{:S(2)}, u32[]{:S(2)}) collective-permute-start(bf16[16,256]{1,0:T(8,128)(2,1)S(1)} %maximum_select_fusion), channel_id=1, source_target_pairs={{0,64},{64,0},{1,65},{65,1},{2,66},{66,2},{3,67},{67,3},{4,68},{68... | collective-permute-start | bytes 24584 | tf_op jit(solution)/shard_map/ppermute | solution.py:378
  4.7 2.4 %shard_map.103 = (bf16[128,256]{1,0:T(8,128)(2,1)S(1)}, bf16[128,256]{1,0:T(8,128)(2,1)S(1)}, bf16[2048,128]{1,0:T(8,128)(2,1)S(1)}, bf16[2048,128]{1,0:T(8,128)...) custom-call(bf16[2048,128]{1,0:T(8,128)(2,1)} %bitcast.26, bf16[2048,128]{1,0:T(8,128)(2,1)} %bitcast.27, ...), custom_call_target="tpu_custom_call" | custom-call | tf_op jit(solution)/shard_map/pallas_call | solution.py:412
  7.0 0.0 collective-permute-done.row_halo
  7.1 5.2 %collective-permute-start.2 = (bf16[129,256]{1,0:T(8,128)(2,1)S(1)}, bf16[129,256]{1,0:T(8,128)(2,1)S(1)}, u32[]{:S(2)}, u32[]{:S(2)}) collective-permute-start(bf16[129,256]{1,0:T(8,128)(2,1)S(1)} %pad_maximum_fusion.1), channel_id=1, source_target_pairs={{1,0},{2,1},{3,2},{4,3},{5,4},{6,5},{7,6},{8,7},{9,8},{10,9},{11,1... | collective-permute-start | bytes 198152 | tf_op jit(solution)/shard_map/ppermute | solution.py:386
  12.3 1.9 %collective-permute-start.1 = (bf16[129,256]{1,0:T(8,128)(2,1)S(1)}, bf16[129,256]{1,0:T(8,128)(2,1)S(1)}, u32[]{:S(2)}, u32[]{:S(2)}) collective-permute-start(bf16[129,256]{1,0:T(8,128)(2,1)S(1)} %pad_maximum_fusion), channel_id=1, source_target_pairs={{0,1},{1,2},{2,3},{3,4},{4,5},{5,6},{6,7},{7,8},{8,9},{9,10},{10,1... | collective-permute-start | bytes 198152 | tf_op jit(solution)/shard_map/ppermute | solution.py:385
  14.2 0.0 collective-permute-done.2.right
  14.2 6.7 %collective-permute-done.1.left = bf16[129,256]{1,0:T(8,128)(2,1)S(1)} collective-permute-done((bf16[129,256]{1,0:T(8,128)(2,1)S(1)}, bf16[129,256]{1,0:T(8,128)(2,1)S(1)}, u32[]{:S(2)}, u32[]{:S(2)}) %collective-permute-start.1) | collective-permute-done | bytes 66080 | tf_op jit(solution)/shard_map/ppermute | solution.py:385
  20.9 4.8 %shard_map.104 = (bf16[2048,128]{1,0:T(8,128)(2,1)S(1)}, f32[2048,128]{1,0:T(8,128)S(1)}, f32[2048,128]{1,0:T(8,128)S(1)}, f32[2048,128]{1,0:T(8,128)S(1)}) custom-call(bf16[2048,128]{1,0:T(8,128)(2,1)S(1)} %get-tuple-element.20.radar, bf16[2048,128]{1,0:T(8,128)(2,1)S(1)} %get-tuple-element.21.state.refs_1_, ...), custom_call_target="tpu_custom_call" | custom-call | tf_op jit(solution)/shard_map/pallas_call | solution.py:422
  25.7 0.0 copy-start.2
  25.7 0.0 copy-start.3
  25.7 16.9 %all_to_all.10.cells = bf16[64,2,16,128]{3,2,1,0:T(8,128)(2,1)S(1)} all-to-all(bf16[64,2,16,128]{3,2,1,0:T(8,128)(2,1)S(1)} %bitcast.24), channel_id=1, replica_groups=mesh['gy'=2,'gx'=64] {'gx'}, dimensions={0} | all-to-all | bytes 1048576 | tf_op jit(solution)/shard_map/all_to_all | solution.py:438
  42.6 50.9 %shard_map.105 = bf16[64,2,16,128]{3,2,1,0:T(8,128)(2,1)S(1)} custom-call(bf16[64,2,16,128]{3,2,1,0:T(8,128)(2,1)S(1)} %all_to_all.10.cells, bf16[64,384]{1,0:T(8,128)(2,1)S(1)} %copy-done.2, bf16[64,128]{1,0:T(8,128)(2,1)S(1)} %bitcast.25), custom_call_target="tpu_custom_call" | custom-call | tf_op jit(solution)/shard_map/pallas_call | solution.py:273
  93.5 0.0 copy-start
  93.5 17.0 %all_to_all.11 = bf16[64,2,16,128]{3,2,1,0:T(8,128)(2,1)S(1)} all-to-all(bf16[64,2,16,128]{3,2,1,0:T(8,128)(2,1)S(1)} %shard_map.105), channel_id=1, replica_groups=mesh['gy'=2,'gx'=64] {'gx'}, dimensions={0} | all-to-all | bytes 1048576 | tf_op jit(solution)/shard_map/all_to_all | solution.py:440
  110.5 0.2 shard_map.107
  110.8 2.8 %collective-permute-start.3 = (bf16[16,256]{1,0:T(8,128)(2,1)S(1)}, bf16[16,256]{1,0:T(8,128)(2,1)S(1)}, u32[]{:S(2)}, u32[]{:S(2)}) collective-permute-start(bf16[16,256]{1,0:T(8,128)(2,1)S(1)} %shard_map.107), channel_id=1, source_target_pairs={{0,64},{64,0},{1,65},{65,1},{2,66},{66,2},{3,67},{67,3},{4,68},{68... | collective-permute-start | bytes 24584 | tf_op jit(solution)/shard_map/ppermute | solution.py:445
  113.6 3.8 %shard_map.106 = (bf16[2048,128]{1,0:T(8,128)(2,1)}, bf16[2048,256]{1,0:T(8,128)(2,1)S(1)}, bf16[128,256]{1,0:T(8,128)(2,1)S(1)}, bf16[128,256]{1,0:T(8,128)(2,1)S(1)}, bf16[2048,128]{1,0:T(8,128)(2,1)S(1)}) custom-call(bf16[2048,128]{1,0:T(8,128)(2,1)S(1)} %bitcast.20, bf16[2048,128]{1,0:T(8,128)(2,1)S(1)} %get-tuple-element.21.state.refs_1_, ...), custom_call_target="tpu_custom_call" | custom-call | tf_op jit(solution)/shard_map/pallas_call | solution.py:446
  117.4 0.0 collective-permute-done.3.row_halo
  117.4 1.9 %collective-permute-start.4 = (bf16[129,256]{1,0:T(8,128)(2,1)S(1)}, bf16[129,256]{1,0:T(8,128)(2,1)S(1)}, u32[]{:S(2)}, u32[]{:S(2)}) collective-permute-start(bf16[129,256]{1,0:T(8,128)(2,1)S(1)} %pad_maximum_fusion.2), channel_id=1, source_target_pairs={{0,1},{1,2},{2,3},{3,4},{4,5},{5,6},{6,7},{7,8},{8,9},{9,10},{10,1... | collective-permute-start | bytes 198152 | tf_op jit(solution)/shard_map/ppermute | solution.py:385
  119.4 6.7 %collective-permute-start.5 = (bf16[129,256]{1,0:T(8,128)(2,1)S(1)}, bf16[129,256]{1,0:T(8,128)(2,1)S(1)}, u32[]{:S(2)}, u32[]{:S(2)}) collective-permute-start(bf16[129,256]{1,0:T(8,128)(2,1)S(1)} %pad_maximum_fusion.3), channel_id=1, source_target_pairs={{1,0},{2,1},{3,2},{4,3},{5,4},{6,5},{7,6},{8,7},{9,8},{10,9},{11,1... | collective-permute-start | bytes 198152 | tf_op jit(solution)/shard_map/ppermute | solution.py:386
  126.0 0.0 collective-permute-done.4.left
  126.1 1.9 %collective-permute-done.5.right = bf16[129,256]{1,0:T(8,128)(2,1)S(1)} collective-permute-done((bf16[129,256]{1,0:T(8,128)(2,1)S(1)}, bf16[129,256]{1,0:T(8,128)(2,1)S(1)}, u32[]{:S(2)}, u32[]{:S(2)}) %collective-permute-start.5) | collective-permute-done | bytes 66080 | tf_op jit(solution)/shard_map/ppermute | solution.py:386
  128.0 4.1 %shard_map.108 = (bf16[2048,128]{1,0:T(8,128)(2,1)}, bf16[2048,128]{1,0:T(8,128)(2,1)}) custom-call(bf16[2048,256]{1,0:T(8,128)(2,1)S(1)} %get-tuple-element.31.grads, bf16[16,256]{1,0:T(8,128)(2,1)S(1)} %collective-permute-done.3.row_halo, bf16[129,256]{1,0:T(8,128)(2,1)S(1)} %collective-permute-done.4.left, ...), custom_call_target="tpu_custom_call" | custom-call | tf_op jit(solution)/shard_map/pallas_call | solution.py:458
  (12 shorter events, 0.1 us)
Async XLA Ops:
  1.4 5.6 %collective-permute-start = (bf16[16,256]{1,0:T(8,128)(2,1)S(1)}, bf16[16,256]{1,0:T(8,128)(2,1)S(1)}, u32[]{:S(2)}, u32[]{:S(2)}) collective-permute-start(bf16[16,256]{1,0:T(8,128)(2,1)S(1)} %maximum_select_fusion), channel_id=1, source_target_pairs={{0,64},{64,0},{1,65},{65,1},{2,66},{66,2},{3,67},{67,3},{4,68},{68... | collective-permute-start | bytes 24584 | tf_op jit(solution)/shard_map/ppermute | solution.py:378
  7.1 7.1 %collective-permute-start.2 = (bf16[129,256]{1,0:T(8,128)(2,1)S(1)}, bf16[129,256]{1,0:T(8,128)(2,1)S(1)}, u32[]{:S(2)}, u32[]{:S(2)}) collective-permute-start(bf16[129,256]{1,0:T(8,128)(2,1)S(1)} %pad_maximum_fusion.1), channel_id=1, source_target_pairs={{1,0},{2,1},{3,2},{4,3},{5,4},{6,5},{7,6},{8,7},{9,8},{10,9},{11,1... | collective-permute-start | bytes 198152 | tf_op jit(solution)/shard_map/ppermute | solution.py:386
  12.3 8.6 %collective-permute-start.1 = (bf16[129,256]{1,0:T(8,128)(2,1)S(1)}, bf16[129,256]{1,0:T(8,128)(2,1)S(1)}, u32[]{:S(2)}, u32[]{:S(2)}) collective-permute-start(bf16[129,256]{1,0:T(8,128)(2,1)S(1)} %pad_maximum_fusion), channel_id=1, source_target_pairs={{0,1},{1,2},{2,3},{3,4},{4,5},{5,6},{6,7},{7,8},{8,9},{9,10},{10,1... | collective-permute-start | bytes 198152 | tf_op jit(solution)/shard_map/ppermute | solution.py:385
  25.7 16.9 %copy-start.2 = (bf16[64,384]{1,0:T(8,128)(2,1)S(1)}, bf16[64,384]{1,0:T(8,128)(2,1)}, u32[]{:S(2)}) copy-start(bf16[64,384]{1,0:T(8,128)(2,1)} %w_qkv.1) | copy-start | bytes 147460
  25.7 16.9 %copy-start.3 = (bf16[128,64]{0,1:T(8,128)(2,1)S(1)}, bf16[128,64]{0,1:T(8,128)(2,1)}, u32[]{:S(2)}) copy-start(bf16[128,64]{0,1:T(8,128)(2,1)} %param.14) | copy-start | bytes 49156
  93.5 17.0 %copy-start = (bf16[128,16,128]{2,1,0:T(8,128)(2,1)S(1)}, bf16[128,16,128]{2,1,0:T(8,128)(2,1)}, u32[]{:S(2)}) copy-start(bf16[128,16,128]{2,1,0:T(8,128)(2,1)} %param.15) | copy-start | bytes 1572868
  110.8 6.6 %collective-permute-start.3 = (bf16[16,256]{1,0:T(8,128)(2,1)S(1)}, bf16[16,256]{1,0:T(8,128)(2,1)S(1)}, u32[]{:S(2)}, u32[]{:S(2)}) collective-permute-start(bf16[16,256]{1,0:T(8,128)(2,1)S(1)} %shard_map.107), channel_id=1, source_target_pairs={{0,64},{64,0},{1,65},{65,1},{2,66},{66,2},{3,67},{67,3},{4,68},{68... | collective-permute-start | bytes 24584 | tf_op jit(solution)/shard_map/ppermute | solution.py:445
  113.5 14.4 %copy-start.1 = (bf16[3,3,192,256]{3,2,1,0:T(8,128)(2,1)S(1)}, bf16[3,3,192,256]{3,2,1,0:T(8,128)(2,1)}, u32[]{:S(2)}) copy-start(bf16[3,3,192,256]{3,2,1,0:T(8,128)(2,1)} %weights.1) | copy-start | bytes 2654212
  117.4 8.6 %collective-permute-start.4 = (bf16[129,256]{1,0:T(8,128)(2,1)S(1)}, bf16[129,256]{1,0:T(8,128)(2,1)S(1)}, u32[]{:S(2)}, u32[]{:S(2)}) collective-permute-start(bf16[129,256]{1,0:T(8,128)(2,1)S(1)} %pad_maximum_fusion.2), channel_id=1, source_target_pairs={{0,1},{1,2},{2,3},{3,4},{4,5},{5,6},{6,7},{7,8},{8,9},{9,10},{10,1... | collective-permute-start | bytes 198152 | tf_op jit(solution)/shard_map/ppermute | solution.py:385
  119.4 8.6 %collective-permute-start.5 = (bf16[129,256]{1,0:T(8,128)(2,1)S(1)}, bf16[129,256]{1,0:T(8,128)(2,1)S(1)}, u32[]{:S(2)}, u32[]{:S(2)}) collective-permute-start(bf16[129,256]{1,0:T(8,128)(2,1)S(1)} %pad_maximum_fusion.3), channel_id=1, source_target_pairs={{1,0},{2,1},{3,2},{4,3},{5,4},{6,5},{7,6},{8,7},{9,8},{10,9},{11,1... | collective-permute-start | bytes 198152 | tf_op jit(solution)/shard_map/ppermute | solution.py:386

commit v4 on v3

--- a/solution.py
+++ b/solution.py
@@ -19,13 +19,14 @@
     )
 
 
-def call(body, out_shape, scratch=(), in_place=(), count=0, vmem=24):
+def call(body, out_shape, scratch=(), in_place=(), count=0, vmem=24, cost=None):
     spaces = [pltpu.HBM if index in in_place else pltpu.VMEM for index in range(count)]
     return pl.pallas_call(
         body,
         out_shape=out_shape,
         in_specs=[pl.BlockSpec(memory_space=space) for space in spaces],
         scratch_shapes=list(scratch),
+        cost_estimate=cost,
         compiler_params=pltpu.CompilerParams(vmem_limit_bytes=vmem << 20),
     )
 
@@ -60,7 +61,19 @@
     return matmul(pick, flat).astype(BF16)
 
 
-def fill_taps(taps, parts, row_halo, left, right, rows, cols, chunk):
+def even_place():
+    return lax.rem(lax.axis_index("gx"), 2) == 0
+
+
+def sides(cols):
+    even = even_place()
+    return jnp.where(even, cols - 1, 0), jnp.where(even, 0, cols - 1)
+
+
+def fill_taps(taps, parts, row_halo, near, far, rows, cols, chunk):
+    even = even_place()
+    left = lambda *at: jnp.where(even, far[at].astype(F32), near[at].astype(F32)).astype(BF16)
+    right = lambda *at: jnp.where(even, near[at].astype(F32), far[at].astype(F32)).astype(BF16)
     width = taps.shape[1] // 3
     upper = lax.axis_index("gy") == 0
     for start in range(0, rows, chunk):
@@ -73,8 +86,8 @@
             wide = value.astype(F32)
             where = column_of(wide.shape, cols)
             lanes = pl.ds(column, part_width)
-            left_edge = spread(left[pl.ds(start, chunk), lanes], cols, 0)
-            right_edge = spread(right[pl.ds(start, chunk), lanes], cols, cols - 1)
+            left_edge = spread(left(pl.ds(start, chunk), lanes), cols, 0)
+            right_edge = spread(right(pl.ds(start, chunk), lanes), cols, cols - 1)
             before = jnp.where(where == 0, left_edge, pltpu.roll(wide, 1, axis=0))
             after = jnp.where(where == cols - 1, right_edge, pltpu.roll(wide, count - 1, axis=0))
             target = pl.ds(cols + begin, count)
@@ -84,8 +97,8 @@
             column += part_width
     halo = row_halo[...].astype(F32)
     where = column_of(halo.shape, cols)
-    first = jnp.broadcast_to(left[pl.ds(rows, 1), :].astype(F32), halo.shape)
-    last = jnp.broadcast_to(right[pl.ds(rows, 1), :].astype(F32), halo.shape)
+    first = jnp.broadcast_to(left(pl.ds(rows, 1), slice(None)).astype(F32), halo.shape)
+    last = jnp.broadcast_to(right(pl.ds(rows, 1), slice(None)).astype(F32), halo.shape)
     before = jnp.where(where == 0, first, pltpu.roll(halo, 1, axis=0))
     after = jnp.where(where == cols - 1, last, pltpu.roll(halo, cols - 1, axis=0))
     for index, piece in enumerate((before, halo, after)):
@@ -137,7 +150,7 @@
 def edges(rows, cols, chunk):
     pieces = rows // chunk
 
-    def body(radar, state, bias_in, gain_in, left, right, radar_here, state_here, bias, gain,
+    def body(radar, state, bias_in, gain_in, near, far, radar_here, state_here, bias, gain,
              radar_sems, state_sems, sems):
         small = (
             pltpu.make_async_copy(bias_in, bias, sems.at[0]),
@@ -150,6 +163,7 @@
         for copy in small:
             copy.start()
         width = radar.shape[1]
+        near_at, far_at = sides(cols)
         for index in range(pieces):
             for part, copies, lanes in (
                 (radar_here, ready[0], pl.ds(0, width)),
@@ -157,8 +171,8 @@
             ):
                 copies[index].wait()
                 value = part[pl.ds(index * chunk * cols, chunk * cols), :]
-                left[pl.ds(index * chunk, chunk), lanes] = pick_column(value, cols, 0)
-                right[pl.ds(index * chunk, chunk), lanes] = pick_column(value, cols, cols - 1)
+                near[pl.ds(index * chunk, chunk), lanes] = pick_column(value, cols, near_at)
+                far[pl.ds(index * chunk, chunk), lanes] = pick_column(value, cols, far_at)
         for copy in small:
             copy.wait()
 
@@ -166,10 +180,10 @@
 
 
 def step_forward(rows, cols, chunk):
-    def body(radar, state, row_halo, left, right, weights_out, bias, gain, grad_out,
+    def body(radar, state, row_halo, near, far, weights_out, bias, gain, grad_out,
              payload, sig_ref, mix_ref, cell_ref, taps, weights, state_grad, sems, grad_sems):
         later = fetch(weights_out, weights, sems, 3) + fetch(grad_out, state_grad, grad_sems, 1)
-        fill_taps(taps, (radar, state), row_halo, left, right, rows, cols, chunk)
+        fill_taps(taps, (radar, state), row_halo, near, far, rows, cols, chunk)
         for copy in later:
             copy.wait()
         count = chunk * cols
@@ -197,15 +211,16 @@
     return body
 
 
-def attention(length, block):
-    def body(cells, w_qkv, w_out_t, out, w_qkv_t, rows, cols, query_mask, grad_mask, values, exps, probs,
-             scores, mixed, grad_q, grad_k, grad_v):
-        head = pl.program_id(1)
+def attention(length, block, group):
+    def body(cells, w_qkv, w_out_t, out, w_qkv_t, rows, cols, mixed, grad_q, grad_k, grad_v,
+             *per_head):
+        step = pl.program_id(1)
         size = w_out_t.shape[1]
         dim = size // HEADS
         scale = dim ** (-0.5)
-
-        @pl.when(head == 0)
+        scratches = [per_head[6 * index : 6 * index + 6] for index in range(group)]
+
+        @pl.when(step == 0)
         def _():
             line = cells[...].reshape(length, cells.shape[-1]).astype(F32)
             half = line.shape[1] // 2
@@ -216,38 +231,41 @@
             rows[...] = matmul(normed, w_qkv[:, pl.ds(size, 2 * size)]).astype(BF16)
             cols[pl.ds(0, 3 * size), :] = matmul(w_qkv_t[...], normed, 1, 1).astype(BF16)
             cols[pl.ds(3 * size, size), :] = matmul(w_out, given, 1, 1).astype(BF16)
-            values[pl.ds(dim, dim), :] = jnp.ones((dim, length), BF16)
-
-        at = pl.multiple_of(head * dim, dim)
-        mine = pl.ds(at, dim)
-        query_cols = cols[mine, :]
-        key_cols = cols[pl.ds(size + at, dim), :]
-        grad_cols = cols[pl.ds(3 * size + at, dim), :]
-        query_mask[...] = jnp.zeros_like(query_mask)
-        grad_mask[...] = jnp.zeros_like(grad_mask)
-        query_mask[mine, :] = query_cols
-        grad_mask[mine, :] = grad_cols
-        values[pl.ds(0, dim), :] = cols[pl.ds(2 * size + at, dim), :]
-        for begin in range(0, length, block):
-            part = pl.ds(begin, block)
-            exps[:, part] = jnp.exp2(
-                matmul(rows[:, pl.ds(0, size)], query_mask[:, part]) * (scale * LOG2E)
-            ).astype(BF16)
-            sums = matmul(values[...], exps[:, part])
-            inverse = 1.0 / sums[dim : dim + 1]
-            attended = sums[:dim] * inverse
-            mixed[mine, part] = attended.astype(BF16)
-            grads = cols[pl.ds(3 * size + at, dim), part].astype(F32)
-            inner = jnp.sum(attended * grads, axis=0, keepdims=True)
-            prob = exps[:, part] * inverse.astype(BF16)
-            probs[:, part] = prob
-            grad_prob = matmul(rows[:, pl.ds(size, size)], grad_mask[:, part])
-            scores[:, part] = prob * (grad_prob - inner).astype(BF16)
-            grad_q[mine, part] = (matmul(key_cols, scores[:, part]) * scale).astype(BF16)
-        grad_k[mine, :] = (matmul(query_cols, scores[...], 1, 1) * scale).astype(BF16)
-        grad_v[mine, :] = matmul(grad_cols, probs[...], 1, 1).astype(BF16)
-
-        @pl.when(head == HEADS - 1)
+            for _, _, values, _, _, _ in scratches:
+                values[pl.ds(dim, dim), :] = jnp.ones((dim, length), BF16)
+
+        for index, scratch in enumerate(scratches):
+            query_mask, grad_mask, values, exps, probs, scores = scratch
+            at = pl.multiple_of((step * group + index) * dim, dim)
+            mine = pl.ds(at, dim)
+            query_cols = cols[mine, :]
+            key_cols = cols[pl.ds(size + at, dim), :]
+            grad_cols = cols[pl.ds(3 * size + at, dim), :]
+            query_mask[...] = jnp.zeros_like(query_mask)
+            grad_mask[...] = jnp.zeros_like(grad_mask)
+            query_mask[mine, :] = query_cols
+            grad_mask[mine, :] = grad_cols
+            values[pl.ds(0, dim), :] = cols[pl.ds(2 * size + at, dim), :]
+            for begin in range(0, length, block):
+                part = pl.ds(begin, block)
+                exps[:, part] = jnp.exp2(
+                    matmul(rows[:, pl.ds(0, size)], query_mask[:, part]) * (scale * LOG2E)
+                ).astype(BF16)
+                sums = matmul(values[...], exps[:, part])
+                inverse = 1.0 / sums[dim : dim + 1]
+                attended = sums[:dim] * inverse
+                mixed[mine, part] = attended.astype(BF16)
+                grads = cols[pl.ds(3 * size + at, dim), part].astype(F32)
+                inner = jnp.sum(attended * grads, axis=0, keepdims=True)
+                prob = exps[:, part] * inverse.astype(BF16)
+                probs[:, part] = prob
+                grad_prob = matmul(rows[:, pl.ds(size, size)], grad_mask[:, part])
+                scores[:, part] = prob * (grad_prob - inner).astype(BF16)
+                grad_q[mine, part] = (matmul(key_cols, scores[:, part]) * scale).astype(BF16)
+            grad_k[mine, :] = (matmul(query_cols, scores[...], 1, 1) * scale).astype(BF16)
+            grad_v[mine, :] = matmul(grad_cols, probs[...], 1, 1).astype(BF16)
+
+        @pl.when(step == HEADS // group - 1)
         def _():
             w_out = w_out_t[...].astype(F32).T.astype(BF16)
             back = (
@@ -265,15 +283,15 @@
     peers, lines, cols, width = cells.shape
     length = peers * cols
     size = w_out_t.shape[1]
-    block = min(512, length)
+    block, group = min(512, length), 2
     whole = lambda array: pl.BlockSpec(array.shape, lambda i, j: (0,) * array.ndim)
     line_spec = pl.BlockSpec((peers, None, cols, width), lambda i, j: (0, i, 0, 0))
     tall = pltpu.VMEM((size, length), BF16)
     square = pltpu.VMEM((length, length), BF16)
     return pl.pallas_call(
-        attention(length, block),
+        attention(length, block, group),
         out_shape=jax.ShapeDtypeStruct(cells.shape, BF16),
-        grid=(lines, HEADS),
+        grid=(lines, HEADS // group),
         in_specs=[line_spec, whole(w_qkv), whole(w_out_t)],
         out_specs=line_spec,
         scratch_shapes=[
@@ -282,15 +300,18 @@
             pltpu.VMEM((4 * size, length), BF16),
             tall,
             tall,
+            tall,
+            tall,
+        ]
+        + [
+            tall,
+            tall,
             pltpu.VMEM((2 * size // HEADS, length), BF16),
             square,
             square,
             square,
-            tall,
-            tall,
-            tall,
-            tall,
-        ],
+        ]
+        * group,
         compiler_params=pltpu.CompilerParams(
             dimension_semantics=("arbitrary", "arbitrary"), vmem_limit_bytes=VMEM_ATTEND << 20
         ),
@@ -338,7 +359,8 @@
 
 def all_grads(rows, cols, chunk):
     def body(back, state, state_grad, gain, sig_ref, mix_ref, cell_ref,
-             new_state, grads, left, right, c_grad):
+             new_state, grads, near, far, c_grad):
+        near_at, far_at = sides(cols)
         count = chunk * cols
         width = state.shape[1]
         for start in range(0, rows, chunk):
@@ -350,15 +372,15 @@
             c_grad[part, :] = cell.astype(BF16)
             for lanes, value in ((pl.ds(0, width), one), (pl.ds(width, width), two)):
                 grads[part, lanes] = value
-                left[pl.ds(start, chunk), lanes] = pick_column(value, cols, 0)
-                right[pl.ds(start, chunk), lanes] = pick_column(value, cols, cols - 1)
+                near[pl.ds(start, chunk), lanes] = pick_column(value, cols, near_at)
+                far[pl.ds(start, chunk), lanes] = pick_column(value, cols, far_at)
 
     return body
 
 
 def step_backward(rows, cols, chunk):
-    def body(grads, row_halo, left, right, weights, c_grad, grad_frame, grad_state, taps):
-        fill_taps(taps, (grads,), row_halo, left, right, rows, cols, chunk)
+    def body(grads, row_halo, near, far, weights, c_grad, grad_frame, grad_state, taps):
+        fill_taps(taps, (grads,), row_halo, near, far, rows, cols, chunk)
         count = chunk * cols
         wide = grad_frame.shape[1]
         for start in range(0, rows, chunk):
@@ -378,13 +400,17 @@
     return lax.ppermute(border, "gy", [(0, 1), (1, 0)])
 
 
-def exchange_columns(first_col, last_col, row_halo):
+def exchange_columns(near, far, row_halo):
     count = lax.axis_size("gx")
-    forward = [(i, i + 1) for i in range(count - 1)]
-    backward = [(target, source) for source, target in forward]
-    left = lax.ppermute(jnp.concatenate([last_col, row_halo[-1:]], axis=0), "gx", forward)
-    right = lax.ppermute(jnp.concatenate([first_col, row_halo[:1]], axis=0), "gx", backward)
-    return row_halo, left, right
+    swaps = lambda first: [
+        pair for i in range(first, count - 1, 2) for pair in ((i, i + 1), (i + 1, i))
+    ]
+    even = even_place()
+    near_cell = jnp.where(even, row_halo[-1:], row_halo[:1])
+    far_cell = jnp.where(even, row_halo[:1], row_halo[-1:])
+    near = lax.ppermute(jnp.concatenate([near, near_cell], axis=0), "gx", swaps(0))
+    far = lax.ppermute(jnp.concatenate([far, far_cell], axis=0), "gx", swaps(1))
+    return row_halo, near, far
 
 
 def on_device(radar_frame, lstm_state, w_conv, b_gates, norm_gain, w_qkv, w_out, state_grad):
@@ -409,7 +435,7 @@
     pieces = row_count // chunk
     in_hbm = lambda array: pltpu.with_memory_space_constraint(array, pltpu.HBM)
     bias, gain = b_gates[None], norm_gain[None]
-    left, right, radar, state, bias, gain = call(
+    near, far, radar, state, bias, gain = call(
         edges(row_count, col_count, chunk),
         (shape(row_count, depth),) * 2
         + (shape(*radar.shape), shape(*state.shape), wide(*bias.shape), wide(*gain.shape)),
@@ -417,7 +443,7 @@
         (0, 1, 2, 3),
         4,
     )(in_hbm(radar), in_hbm(state), in_hbm(bias), in_hbm(gain))
-    halo = exchange_columns(left, right, row_halo)
+    halo = exchange_columns(near, far, row_halo)
 
     payload, sig, mix, cell = call(
         step_forward(row_count, col_count, chunk),
@@ -443,7 +469,7 @@
     operands = (back, state, given, gain, sig, mix, cell)
     border = call(border_grads(row_count, col_count), shape(col_count, gate_dim), count=7)(*operands)
     row_halo = lax.ppermute(border, "gy", [(0, 1), (1, 0)])
-    new_state, grads, left, right, c_grad = call(
+    new_state, grads, near, far, c_grad = call(
         all_grads(row_count, col_count, chunk),
         (
             shape(cells, 2 * hidden),
@@ -453,8 +479,11 @@
             shape(cells, 2 * hidden),
         ),
         count=7,
+        cost=pl.CostEstimate(
+            flops=64 * cells * gate_dim, transcendentals=4 * cells * hidden, bytes_accessed=24 * cells * gate_dim
+        ),
     )(*operands)
-    halo = exchange_columns(left, right, row_halo)
+    halo = exchange_columns(near, far, row_halo)
     grad_frame, grad_state = call(
         step_backward(row_count, col_count, chunk),
         (shape(cells, in_channels), shape(cells, 2 * hidden)),

time: 133 us -> 128 us (0.962)
  starting transfers between devices: 21.7 us -> 15 us
  blocking collectives: 33.9 us -> 36.6 us
    ppermute x4, starting transfers between devices: 15.7 us -> 9.11 us  [the longest x2 8.94 us: exchange_columns(): far = lax.ppermute(jnp.concatenate([far, far_cell], axis=0), 'gx', swaps(1))]
    all_to_all x1, blocking collectives: 16.9 us -> 19.6 us  [on_device(): lax.all_to_all(send, 'gx', split_axis=0, concat_axis=0, tiled=True)]
where the time goes in v4:
time: 128 us; the launch traced here: 127 us
  Pallas kernels  65.8 us (51%)
  blocking collectives  36.6 us (29%)
  starting transfers between devices  15 us (12%)
  waiting for transfers between devices  8.21 us (6%)
    pallas_call x1, Pallas kernels, attend(): pl.pallas_call(attention(length, block, group), out_shape=jax.ShapeDtypeS...  49.9 us
    all_to_all x1, blocking collectives, on_device(): lax.all_to_all(send, 'gx', split_axis=0, concat_axis=0, tiled=True)  19.6 us
    all_to_all x1, blocking collectives, on_device(): lax.all_to_all(lines_out, 'gx', split_axis=0, concat_axis=0, tiled=True)  17 us
    ppermute x2, starting transfers between devices, exchange_columns(): far = lax.ppermute(jnp.concatenate([far, far_cell], axis=0), 'gx', swaps(1))  8.94 us
    ppermute x2, waiting for transfers between devices, exchange_columns(): far = lax.ppermute(jnp.concatenate([far, far_cell], axis=0), 'gx', swaps(1))  8.2 us
    pallas_call x1, Pallas kernels, on_device(): call(step_forward(row_count, col_count, chunk), (shape(cells, 2 * hidden)...  5.37 us
    pallas_call x1, Pallas kernels, on_device(): call(step_backward(row_count, col_count, chunk), (shape(cells, in_channel...  4.12 us
    pallas_call x1, Pallas kernels, on_device(): call(all_grads(row_count, col_count, chunk), (shape(cells, 2 * hidden), s...  3.86 us
  transfers between devices with their start and end apart: 6, of which 2 were waited for; matrix products, arithmetic and copies ran while one was open for 0% of the time, Pallas kernels for 5%

profile of v4, /device:TPU:2, one launch (start us, length us, event | category | flops | bytes accessed | tf_op | source)
XLA Modules:
  0.0 127.2 jit_solution(17531605882389207076)
XLA Ops:
  0.6 0.7 slice_bitcast_fusion
  1.4 3.3 %collective-permute-start = (bf16[16,256]{1,0:T(8,128)(2,1)S(1)}, bf16[16,256]{1,0:T(8,128)(2,1)S(1)}, u32[]{:S(2)}, u32[]{:S(2)}) collective-permute-start(bf16[16,256]{1,0:T(8,128)(2,1)S(1)} %maximum_select_fusion), channel_id=1, source_target_pairs={{0,64},{64,0},{1,65},{65,1},{2,66},{66,2},{3,67},{67,3},{4,68},{68... | collective-permute-start | bytes 24584 | tf_op jit(solution)/shard_map/ppermute | solution.py:400
  4.7 2.4 %shard_map.103 = (bf16[128,256]{1,0:T(8,128)(2,1)S(1)}, bf16[128,256]{1,0:T(8,128)(2,1)S(1)}, bf16[2048,128]{1,0:T(8,128)(2,1)S(1)}, bf16[2048,128]{1,0:T(8,128)...) custom-call(bf16[2048,128]{1,0:T(8,128)(2,1)} %bitcast.26, bf16[2048,128]{1,0:T(8,128)(2,1)} %bitcast.27, ...), custom_call_target="tpu_custom_call" | custom-call | tf_op jit(solution)/shard_map/pallas_call | solution.py:438
  7.0 0.0 collective-permute-done.row_halo
  7.1 5.2 %collective-permute-start.2 = (bf16[129,256]{1,0:T(8,128)(2,1)S(1)}, bf16[129,256]{1,0:T(8,128)(2,1)S(1)}, u32[]{:S(2)}, u32[]{:S(2)}) collective-permute-start(bf16[129,256]{1,0:T(8,128)(2,1)S(1)} %pad_maximum_fusion.1), channel_id=1, source_target_pairs={{1,2},{2,1},{3,4},{4,3},{5,6},{6,5},{7,8},{8,7},{9,10},{10,9},{11,... | collective-permute-start | bytes 198152 | tf_op jit(solution)/shard_map/ppermute | solution.py:412
  12.3 0.1 collective-permute-start.1
  12.4 3.3 %collective-permute-done.2.far = bf16[129,256]{1,0:T(8,128)(2,1)S(1)} collective-permute-done((bf16[129,256]{1,0:T(8,128)(2,1)S(1)}, bf16[129,256]{1,0:T(8,128)(2,1)S(1)}, u32[]{:S(2)}, u32[]{:S(2)}) %collective-permute-start.2) | collective-permute-done | bytes 66080 | tf_op jit(solution)/shard_map/ppermute | solution.py:412
  15.7 0.0 collective-permute-done.1.near
  15.7 5.4 %shard_map.104 = (bf16[2048,128]{1,0:T(8,128)(2,1)S(1)}, f32[2048,128]{1,0:T(8,128)S(1)}, f32[2048,128]{1,0:T(8,128)S(1)}, f32[2048,128]{1,0:T(8,128)S(1)}) custom-call(bf16[2048,128]{1,0:T(8,128)(2,1)S(1)} %get-tuple-element.20.radar, bf16[2048,128]{1,0:T(8,128)(2,1)S(1)} %get-tuple-element.21.state.refs_1_, ...), custom_call_target="tpu_custom_call" | custom-call | tf_op jit(solution)/shard_map/pallas_call | solution.py:448
  21.1 0.0 copy-start.2
  21.1 0.0 copy-start.3
  21.1 19.6 %all_to_all.10.cells = bf16[64,2,16,128]{3,2,1,0:T(8,128)(2,1)S(1)} all-to-all(bf16[64,2,16,128]{3,2,1,0:T(8,128)(2,1)S(1)} %bitcast.24), channel_id=1, replica_groups=mesh['gy'=2,'gx'=64] {'gx'}, dimensions={0} | all-to-all | bytes 1048576 | tf_op jit(solution)/shard_map/all_to_all | solution.py:464
  40.7 49.9 %shard_map.105 = bf16[64,2,16,128]{3,2,1,0:T(8,128)(2,1)S(1)} custom-call(bf16[64,2,16,128]{3,2,1,0:T(8,128)(2,1)S(1)} %all_to_all.10.cells, bf16[64,384]{1,0:T(8,128)(2,1)S(1)} %copy-done.2, bf16[64,128]{1,0:T(8,128)(2,1)S(1)} %bitcast.25), custom_call_target="tpu_custom_call" | custom-call | tf_op jit(solution)/shard_map/pallas_call | solution.py:291
  90.6 0.0 copy-start
  90.6 17.0 %all_to_all.11 = bf16[64,2,16,128]{3,2,1,0:T(8,128)(2,1)S(1)} all-to-all(bf16[64,2,16,128]{3,2,1,0:T(8,128)(2,1)S(1)} %shard_map.105), channel_id=1, replica_groups=mesh['gy'=2,'gx'=64] {'gx'}, dimensions={0} | all-to-all | bytes 1048576 | tf_op jit(solution)/shard_map/all_to_all | solution.py:466
  107.6 0.2 shard_map.107
  107.8 2.6 %collective-permute-start.3 = (bf16[16,256]{1,0:T(8,128)(2,1)S(1)}, bf16[16,256]{1,0:T(8,128)(2,1)S(1)}, u32[]{:S(2)}, u32[]{:S(2)}) collective-permute-start(bf16[16,256]{1,0:T(8,128)(2,1)S(1)} %shard_map.107), channel_id=1, source_target_pairs={{0,64},{64,0},{1,65},{65,1},{2,66},{66,2},{3,67},{67,3},{4,68},{68... | collective-permute-start | bytes 24584 | tf_op jit(solution)/shard_map/ppermute | solution.py:471
  110.4 3.9 %shard_map.106 = (bf16[2048,128]{1,0:T(8,128)(2,1)}, bf16[2048,256]{1,0:T(8,128)(2,1)S(1)}, bf16[128,256]{1,0:T(8,128)(2,1)S(1)}, bf16[128,256]{1,0:T(8,128)(2,1)S(1)}, bf16[2048,128]{1,0:T(8,128)(2,1)S(1)}) custom-call(bf16[2048,128]{1,0:T(8,128)(2,1)S(1)} %bitcast.20, bf16[2048,128]{1,0:T(8,128)(2,1)S(1)} %get-tuple-element.21.state.refs_1_, ...), custom_call_target="tpu_custom_call" | custom-call | flops 33554432 | bytes 12582912 | tf_op jit(solution)/shard_map/pallas_call | solution.py:472
  114.3 0.0 collective-permute-done.3.row_halo
  114.3 0.1 collective-permute-start.4
  114.4 3.8 %collective-permute-start.5 = (bf16[129,256]{1,0:T(8,128)(2,1)S(1)}, bf16[129,256]{1,0:T(8,128)(2,1)S(1)}, u32[]{:S(2)}, u32[]{:S(2)}) collective-permute-start(bf16[129,256]{1,0:T(8,128)(2,1)S(1)} %pad_maximum_fusion.3), channel_id=1, source_target_pairs={{1,2},{2,1},{3,4},{4,3},{5,6},{6,5},{7,8},{8,7},{9,10},{10,9},{11,... | collective-permute-start | bytes 198152 | tf_op jit(solution)/shard_map/ppermute | solution.py:412
  118.2 0.0 collective-permute-done.4.near
  118.2 4.9 %collective-permute-done.5.far = bf16[129,256]{1,0:T(8,128)(2,1)S(1)} collective-permute-done((bf16[129,256]{1,0:T(8,128)(2,1)S(1)}, bf16[129,256]{1,0:T(8,128)(2,1)S(1)}, u32[]{:S(2)}, u32[]{:S(2)}) %collective-permute-start.5) | collective-permute-done | bytes 66080 | tf_op jit(solution)/shard_map/ppermute | solution.py:412
  123.1 4.1 %shard_map.108 = (bf16[2048,128]{1,0:T(8,128)(2,1)}, bf16[2048,128]{1,0:T(8,128)(2,1)}) custom-call(bf16[2048,256]{1,0:T(8,128)(2,1)S(1)} %get-tuple-element.31.grads, bf16[16,256]{1,0:T(8,128)(2,1)S(1)} %collective-permute-done.3.row_halo, bf16[129,256]{1,0:T(8,128)(2,1)S(1)} %collective-permute-done.4.near, ...), custom_call_target="tpu_custom_call" | custom-call | tf_op jit(solution)/shard_map/pallas_call | solution.py:487
  (12 shorter events, 0.1 us)
Async XLA Ops:
  1.4 5.6 %collective-permute-start = (bf16[16,256]{1,0:T(8,128)(2,1)S(1)}, bf16[16,256]{1,0:T(8,128)(2,1)S(1)}, u32[]{:S(2)}, u32[]{:S(2)}) collective-permute-start(bf16[16,256]{1,0:T(8,128)(2,1)S(1)} %maximum_select_fusion), channel_id=1, source_target_pairs={{0,64},{64,0},{1,65},{65,1},{2,66},{66,2},{3,67},{67,3},{4,68},{68... | collective-permute-start | bytes 24584 | tf_op jit(solution)/shard_map/ppermute | solution.py:400
  7.1 8.6 %collective-permute-start.2 = (bf16[129,256]{1,0:T(8,128)(2,1)S(1)}, bf16[129,256]{1,0:T(8,128)(2,1)S(1)}, u32[]{:S(2)}, u32[]{:S(2)}) collective-permute-start(bf16[129,256]{1,0:T(8,128)(2,1)S(1)} %pad_maximum_fusion.1), channel_id=1, source_target_pairs={{1,2},{2,1},{3,4},{4,3},{5,6},{6,5},{7,8},{8,7},{9,10},{10,9},{11,... | collective-permute-start | bytes 198152 | tf_op jit(solution)/shard_map/ppermute | solution.py:412
  12.3 3.4 %collective-permute-start.1 = (bf16[129,256]{1,0:T(8,128)(2,1)S(1)}, bf16[129,256]{1,0:T(8,128)(2,1)S(1)}, u32[]{:S(2)}, u32[]{:S(2)}) collective-permute-start(bf16[129,256]{1,0:T(8,128)(2,1)S(1)} %pad_maximum_fusion), channel_id=1, source_target_pairs={{0,1},{1,0},{2,3},{3,2},{4,5},{5,4},{6,7},{7,6},{8,9},{9,8},{10,11... | collective-permute-start | bytes 198152 | tf_op jit(solution)/shard_map/ppermute | solution.py:411
  21.1 19.6 %copy-start.2 = (bf16[64,384]{1,0:T(8,128)(2,1)S(1)}, bf16[64,384]{1,0:T(8,128)(2,1)}, u32[]{:S(2)}) copy-start(bf16[64,384]{1,0:T(8,128)(2,1)} %w_qkv.1) | copy-start | bytes 147460
  21.1 19.6 %copy-start.3 = (bf16[128,64]{0,1:T(8,128)(2,1)S(1)}, bf16[128,64]{0,1:T(8,128)(2,1)}, u32[]{:S(2)}) copy-start(bf16[128,64]{0,1:T(8,128)(2,1)} %param.14) | copy-start | bytes 49156
  90.6 17.0 %copy-start = (bf16[128,16,128]{2,1,0:T(8,128)(2,1)S(1)}, bf16[128,16,128]{2,1,0:T(8,128)(2,1)}, u32[]{:S(2)}) copy-start(bf16[128,16,128]{2,1,0:T(8,128)(2,1)} %param.15) | copy-start | bytes 1572868
  107.8 6.5 %collective-permute-start.3 = (bf16[16,256]{1,0:T(8,128)(2,1)S(1)}, bf16[16,256]{1,0:T(8,128)(2,1)S(1)}, u32[]{:S(2)}, u32[]{:S(2)}) collective-permute-start(bf16[16,256]{1,0:T(8,128)(2,1)S(1)} %shard_map.107), channel_id=1, source_target_pairs={{0,64},{64,0},{1,65},{65,1},{2,66},{66,2},{3,67},{67,3},{4,68},{68... | collective-permute-start | bytes 24584 | tf_op jit(solution)/shard_map/ppermute | solution.py:471
  110.4 12.6 %copy-start.1 = (bf16[3,3,192,256]{3,2,1,0:T(8,128)(2,1)S(1)}, bf16[3,3,192,256]{3,2,1,0:T(8,128)(2,1)}, u32[]{:S(2)}) copy-start(bf16[3,3,192,256]{3,2,1,0:T(8,128)(2,1)} %weights.1) | copy-start | bytes 2654212
  114.3 3.9 %collective-permute-start.4 = (bf16[129,256]{1,0:T(8,128)(2,1)S(1)}, bf16[129,256]{1,0:T(8,128)(2,1)S(1)}, u32[]{:S(2)}, u32[]{:S(2)}) collective-permute-start(bf16[129,256]{1,0:T(8,128)(2,1)S(1)} %pad_maximum_fusion.2), channel_id=1, source_target_pairs={{0,1},{1,0},{2,3},{3,2},{4,5},{5,4},{6,7},{7,6},{8,9},{9,8},{10,11... | collective-permute-start | bytes 198152 | tf_op jit(solution)/shard_map/ppermute | solution.py:411
  114.4 8.6 %collective-permute-start.5 = (bf16[129,256]{1,0:T(8,128)(2,1)S(1)}, bf16[129,256]{1,0:T(8,128)(2,1)S(1)}, u32[]{:S(2)}, u32[]{:S(2)}) collective-permute-start(bf16[129,256]{1,0:T(8,128)(2,1)S(1)} %pad_maximum_fusion.3), channel_id=1, source_target_pairs={{1,2},{2,1},{3,4},{4,3},{5,6},{6,5},{7,8},{8,7},{9,10},{10,9},{11,... | collective-permute-start | bytes 198152 | tf_op jit(solution)/shard_map/ppermute | solution.py:412

commit v5 on v4

--- a/solution.py
+++ b/solution.py
@@ -8,7 +8,7 @@
 HEADS = 8
 EPS = 1e-05
 LOG2E = 1.4426950408889634
-VMEM_ATTEND = 28
+VMEM_ATTEND = 36
 F32 = jnp.float32
 BF16 = jnp.bfloat16
 
@@ -180,12 +180,9 @@
 
 
 def step_forward(rows, cols, chunk):
-    def body(radar, state, row_halo, near, far, weights_out, bias, gain, grad_out,
-             payload, sig_ref, mix_ref, cell_ref, taps, weights, state_grad, sems, grad_sems):
-        later = fetch(weights_out, weights, sems, 3) + fetch(grad_out, state_grad, grad_sems, 1)
+    def body(radar, state, row_halo, near, far, weights, bias, gain, state_grad,
+             payload, sig_ref, mix_ref, cell_ref, taps):
         fill_taps(taps, (radar, state), row_halo, near, far, rows, cols, chunk)
-        for copy in later:
-            copy.wait()
         count = chunk * cols
         half = state.shape[1] // 2
         for start in range(0, rows, chunk):
@@ -214,35 +211,22 @@
 def attention(length, block, group):
     def body(cells, w_qkv, w_out_t, out, w_qkv_t, rows, cols, mixed, grad_q, grad_k, grad_v,
              *per_head):
-        step = pl.program_id(1)
         size = w_out_t.shape[1]
         dim = size // HEADS
         scale = dim ** (-0.5)
         scratches = [per_head[6 * index : 6 * index + 6] for index in range(group)]
-
-        @pl.when(step == 0)
-        def _():
-            line = cells[...].reshape(length, cells.shape[-1]).astype(F32)
-            half = line.shape[1] // 2
-            normed = line[:, :half].astype(BF16)
-            given = swap_halves(line)[:, :half].astype(BF16)
-            w_qkv_t[...] = w_qkv[...].astype(F32).T.astype(BF16)
-            w_out = w_out_t[...].astype(F32).T.astype(BF16)
-            rows[...] = matmul(normed, w_qkv[:, pl.ds(size, 2 * size)]).astype(BF16)
-            cols[pl.ds(0, 3 * size), :] = matmul(w_qkv_t[...], normed, 1, 1).astype(BF16)
-            cols[pl.ds(3 * size, size), :] = matmul(w_out, given, 1, 1).astype(BF16)
-            for _, _, values, _, _, _ in scratches:
-                values[pl.ds(dim, dim), :] = jnp.ones((dim, length), BF16)
-
-        for index, scratch in enumerate(scratches):
-            query_mask, grad_mask, values, exps, probs, scores = scratch
-            at = pl.multiple_of((step * group + index) * dim, dim)
+        w_qkv_t[...] = w_qkv[...].astype(F32).T.astype(BF16)
+        for query_mask, grad_mask, values, _, _, _ in scratches:
+            query_mask[...] = jnp.zeros_like(query_mask)
+            grad_mask[...] = jnp.zeros_like(grad_mask)
+            values[pl.ds(dim, dim), :] = jnp.ones((dim, length), BF16)
+
+        def one_head(head, query_mask, grad_mask, values, exps, probs, scores):
+            at = pl.multiple_of(head * dim, dim)
             mine = pl.ds(at, dim)
             query_cols = cols[mine, :]
             key_cols = cols[pl.ds(size + at, dim), :]
             grad_cols = cols[pl.ds(3 * size + at, dim), :]
-            query_mask[...] = jnp.zeros_like(query_mask)
-            grad_mask[...] = jnp.zeros_like(grad_mask)
             query_mask[mine, :] = query_cols
             grad_mask[mine, :] = grad_cols
             values[pl.ds(0, dim), :] = cols[pl.ds(2 * size + at, dim), :]
@@ -264,17 +248,36 @@
                 grad_q[mine, part] = (matmul(key_cols, scores[:, part]) * scale).astype(BF16)
             grad_k[mine, :] = (matmul(query_cols, scores[...], 1, 1) * scale).astype(BF16)
             grad_v[mine, :] = matmul(grad_cols, probs[...], 1, 1).astype(BF16)
-
-        @pl.when(step == HEADS // group - 1)
-        def _():
+            query_mask[mine, :] = jnp.zeros_like(query_cols)
+            grad_mask[mine, :] = jnp.zeros_like(grad_cols)
+
+        def heads(step, carry):
+            for index, scratch in enumerate(scratches):
+                one_head(step * group + index, *scratch)
+            return carry
+
+        def row(index, carry):
+            here = (slice(None), pl.ds(index, 1))
+            line = cells[here].reshape(length, cells.shape[-1]).astype(F32)
+            half = line.shape[1] // 2
+            normed = line[:, :half].astype(BF16)
+            given = swap_halves(line)[:, :half].astype(BF16)
             w_out = w_out_t[...].astype(F32).T.astype(BF16)
+            rows[...] = matmul(normed, w_qkv[:, pl.ds(size, 2 * size)]).astype(BF16)
+            cols[pl.ds(0, 3 * size), :] = matmul(w_qkv_t[...], normed, 1, 1).astype(BF16)
+            cols[pl.ds(3 * size, size), :] = matmul(w_out, given, 1, 1).astype(BF16)
+            lax.fori_loop(0, HEADS // group, heads, 0)
             back = (
                 matmul(grad_q[...], w_qkv_t[pl.ds(0, size), :], 0, 0)
                 + matmul(grad_k[...], w_qkv_t[pl.ds(size, size), :], 0, 0)
                 + matmul(grad_v[...], w_qkv_t[pl.ds(2 * size, size), :], 0, 0)
             )
             result = jnp.concatenate([matmul(mixed[...], w_out, 0, 0), back], axis=1)
-            out[...] = result.astype(BF16).reshape(out.shape)
+            peers, _, cells_each, width = cells.shape
+            out[here] = result.astype(BF16).reshape(peers, 1, cells_each, width)
+            return carry
+
+        lax.fori_loop(0, cells.shape[1], row, 0)
 
     return body
 
@@ -283,18 +286,13 @@
     peers, lines, cols, width = cells.shape
     length = peers * cols
     size = w_out_t.shape[1]
-    block, group = min(512, length), 2
-    whole = lambda array: pl.BlockSpec(array.shape, lambda i, j: (0,) * array.ndim)
-    line_spec = pl.BlockSpec((peers, None, cols, width), lambda i, j: (0, i, 0, 0))
+    block, group = min(512, length), 4
     tall = pltpu.VMEM((size, length), BF16)
     square = pltpu.VMEM((length, length), BF16)
-    return pl.pallas_call(
+    return call(
         attention(length, block, group),
-        out_shape=jax.ShapeDtypeStruct(cells.shape, BF16),
-        grid=(lines, HEADS // group),
-        in_specs=[line_spec, whole(w_qkv), whole(w_out_t)],
-        out_specs=line_spec,
-        scratch_shapes=[
+        jax.ShapeDtypeStruct(cells.shape, BF16),
+        [
             pltpu.VMEM(w_qkv.shape[::-1], BF16),
             pltpu.VMEM((length, 2 * size), BF16),
             pltpu.VMEM((4 * size, length), BF16),
@@ -312,9 +310,8 @@
             square,
         ]
         * group,
-        compiler_params=pltpu.CompilerParams(
-            dimension_semantics=("arbitrary", "arbitrary"), vmem_limit_bytes=VMEM_ATTEND << 20
-        ),
+        count=3,
+        vmem=VMEM_ATTEND,
     )(cells, w_qkv, w_out_t)
 
 
@@ -419,7 +416,7 @@
     gate_dim = w_conv.shape[3]
     attn_dim = w_out.shape[0]
     cells = row_count * col_count
-    chunk = min(32, row_count)
+    chunk, long_chunk = min(16, row_count), min(64, row_count)
     lines = row_count // lax.axis_size("gx")
     shape = lambda *dims: jax.ShapeDtypeStruct(dims, BF16)
     wide = lambda *dims: jax.ShapeDtypeStruct(dims, F32)
@@ -432,11 +429,11 @@
     both = lambda row: jnp.concatenate([radar_frame[row], lstm_state[row]], axis=-1)
     row_halo = swap_border(both(0), both(-1))
     sems = pltpu.SemaphoreType.DMA
-    pieces = row_count // chunk
+    pieces = row_count // long_chunk
     in_hbm = lambda array: pltpu.with_memory_space_constraint(array, pltpu.HBM)
     bias, gain = b_gates[None], norm_gain[None]
     near, far, radar, state, bias, gain = call(
-        edges(row_count, col_count, chunk),
+        edges(row_count, col_count, long_chunk),
         (shape(row_count, depth),) * 2
         + (shape(*radar.shape), shape(*state.shape), wide(*bias.shape), wide(*gain.shape)),
         [sems((pieces,)), sems((pieces,)), sems((2,))],
@@ -448,16 +445,9 @@
     payload, sig, mix, cell = call(
         step_forward(row_count, col_count, chunk),
         (shape(cells, 2 * hidden),) + (wide(cells, 2 * hidden),) * 3,
-        [
-            vmem(((row_count + 2) * col_count, 3 * depth), BF16),
-            vmem(w_conv.shape, BF16),
-            vmem(given.shape, BF16),
-            sems((3,)),
-            sems((1,)),
-        ],
-        (5, 8),
-        9,
-    )(radar, state, *halo, in_hbm(w_conv), bias, gain, in_hbm(given))
+        [vmem(((row_count + 2) * col_count, 3 * depth), BF16)],
+        count=9,
+    )(radar, state, *halo, w_conv, bias, gain, given)
 
     peers = lax.axis_size("gx")
     send = payload.reshape(peers, lines, col_count, 2 * hidden)
@@ -470,7 +460,7 @@
     border = call(border_grads(row_count, col_count), shape(col_count, gate_dim), count=7)(*operands)
     row_halo = lax.ppermute(border, "gy", [(0, 1), (1, 0)])
     new_state, grads, near, far, c_grad = call(
-        all_grads(row_count, col_count, chunk),
+        all_grads(row_count, col_count, long_chunk),
         (
             shape(cells, 2 * hidden),
             shape(cells, gate_dim),

time: 128 us -> 124 us (0.969)
  Pallas kernels: 65.8 us -> 62.1 us
    pallas_call x3, Pallas kernels: 56.1 us -> 54.1 us  [the longest x1 48.7 us: attend(): call(attention(length, block, group), jax.ShapeDtypeStruct(cells.shape, B...]
    pallas_call x1, Pallas kernels: 5.37 us -> 3.59 us  [on_device(): call(step_forward(row_count, col_count, chunk), (shape(cells, 2 * hidden)...]
  transfers between devices with their start and end apart: 6 -> 6, of which waited for: 2 -> 2; matrix products, arithmetic and copies ran while one was open for 0% -> 0% of each run, Pallas kernels for 5% -> 4%
where the time goes in v5:
time: 124 us
  Pallas kernels  62.1 us (50%)
  blocking collectives  36.5 us (29%)
  starting transfers between devices  15.6 us (13%)
  waiting for transfers between devices  8.21 us (7%)
    pallas_call x1, Pallas kernels, attend(): call(attention(length, block, group), jax.ShapeDtypeStruct(cells.shape, B...  48.7 us
    all_to_all x1, blocking collectives, on_device(): lax.all_to_all(send, 'gx', split_axis=0, concat_axis=0, tiled=True)  19.6 us
    all_to_all x1, blocking collectives, on_device(): lax.all_to_all(lines_out, 'gx', split_axis=0, concat_axis=0, tiled=True)  16.9 us
    ppermute x2, starting transfers between devices, exchange_columns(): far = lax.ppermute(jnp.concatenate([far, far_cell], axis=0), 'gx', swaps(1))  8.94 us
    ppermute x2, waiting for transfers between devices, exchange_columns(): far = lax.ppermute(jnp.concatenate([far, far_cell], axis=0), 'gx', swaps(1))  8.2 us
    pallas_call x1, Pallas kernels, on_device(): call(step_backward(row_count, col_count, chunk), (shape(cells, in_channel...  4.16 us
    pallas_call x1, Pallas kernels, on_device(): call(step_forward(row_count, col_count, chunk), (shape(cells, 2 * hidden)...  3.59 us
    pallas_call x1, Pallas kernels, on_device(): call(all_grads(row_count, col_count, long_chunk), (shape(cells, 2 * hidde...  3.45 us
  transfers between devices with their start and end apart: 6, of which 2 were waited for; matrix products, arithmetic and copies ran while one was open for 0% of the time, Pallas kernels for 4%

profile of v5, /device:TPU:2, one launch (start us, length us, event | category | flops | bytes accessed | tf_op | source)
XLA Modules:
  0.0 124.0 jit_solution(14681361643301907371)
XLA Ops:
  0.6 0.8 slice_bitcast_fusion
  1.5 3.3 %collective-permute-start = (bf16[16,256]{1,0:T(8,128)(2,1)S(1)}, bf16[16,256]{1,0:T(8,128)(2,1)S(1)}, u32[]{:S(2)}, u32[]{:S(2)}) collective-permute-start(bf16[16,256]{1,0:T(8,128)(2,1)S(1)} %maximum_select_fusion), channel_id=1, source_target_pairs={{0,64},{64,0},{1,65},{65,1},{2,66},{66,2},{3,67},{67,3},{4,68},{68... | collective-permute-start | bytes 24584 | tf_op jit(solution)/shard_map/ppermute | solution.py:397
  4.7 2.0 %shard_map.103 = (bf16[128,256]{1,0:T(8,128)(2,1)S(1)}, bf16[128,256]{1,0:T(8,128)(2,1)S(1)}, bf16[2048,128]{1,0:T(8,128)(2,1)S(1)}, bf16[2048,128]{1,0:T(8,128)...) custom-call(bf16[2048,128]{1,0:T(8,128)(2,1)} %bitcast.26, bf16[2048,128]{1,0:T(8,128)(2,1)} %bitcast.27, ...), custom_call_target="tpu_custom_call" | custom-call | tf_op jit(solution)/shard_map/pallas_call | solution.py:435
  6.7 0.0 collective-permute-done.row_halo
  6.8 5.2 %collective-permute-start.2 = (bf16[129,256]{1,0:T(8,128)(2,1)S(1)}, bf16[129,256]{1,0:T(8,128)(2,1)S(1)}, u32[]{:S(2)}, u32[]{:S(2)}) collective-permute-start(bf16[129,256]{1,0:T(8,128)(2,1)S(1)} %pad_maximum_fusion.1), channel_id=1, source_target_pairs={{1,2},{2,1},{3,4},{4,3},{5,6},{6,5},{7,8},{8,7},{9,10},{10,9},{11,... | collective-permute-start | bytes 198152 | tf_op jit(solution)/shard_map/ppermute | solution.py:409
  12.0 0.1 collective-permute-start.1
  12.1 3.3 %collective-permute-done.2.far = bf16[129,256]{1,0:T(8,128)(2,1)S(1)} collective-permute-done((bf16[129,256]{1,0:T(8,128)(2,1)S(1)}, bf16[129,256]{1,0:T(8,128)(2,1)S(1)}, u32[]{:S(2)}, u32[]{:S(2)}) %collective-permute-start.2) | collective-permute-done | bytes 66080 | tf_op jit(solution)/shard_map/ppermute | solution.py:409
  15.4 0.0 collective-permute-done.1.near
  15.4 3.6 %shard_map.104 = (bf16[2048,128]{1,0:T(8,128)(2,1)S(1)}, f32[2048,128]{1,0:T(8,128)S(1)}, f32[2048,128]{1,0:T(8,128)S(1)}, f32[2048,128]{1,0:T(8,128)S(1)}) custom-call(bf16[2048,128]{1,0:T(8,128)(2,1)S(1)} %get-tuple-element.20.radar, bf16[2048,128]{1,0:T(8,128)(2,1)S(1)} %get-tuple-element.21.state.refs_1_, ...), custom_call_target="tpu_custom_call" | custom-call | tf_op jit(solution)/shard_map/pallas_call | solution.py:445
  19.0 0.0 copy-start.2
  19.0 0.0 copy-start.3
  19.0 19.6 %all_to_all.10.cells = bf16[64,2,16,128]{3,2,1,0:T(8,128)(2,1)S(1)} all-to-all(bf16[64,2,16,128]{3,2,1,0:T(8,128)(2,1)S(1)} %bitcast.24), channel_id=1, replica_groups=mesh['gy'=2,'gx'=64] {'gx'}, dimensions={0} | all-to-all | bytes 1048576 | tf_op jit(solution)/shard_map/all_to_all | solution.py:454
  38.6 0.0 copy-done.2
  38.6 48.7 %shard_map.105 = bf16[64,2,16,128]{3,2,1,0:T(8,128)(2,1)S(1)} custom-call(bf16[64,2,16,128]{3,2,1,0:T(8,128)(2,1)S(1)} %all_to_all.10.cells, bf16[64,384]{1,0:T(8,128)(2,1)S(1)} %copy-done.2, bf16[64,128]{1,0:T(8,128)(2,1)S(1)} %bitcast.25), custom_call_target="tpu_custom_call" | custom-call | tf_op jit(solution)/shard_map/pallas_call | solution.py:292
  87.3 16.9 %all_to_all.11 = bf16[64,2,16,128]{3,2,1,0:T(8,128)(2,1)S(1)} all-to-all(bf16[64,2,16,128]{3,2,1,0:T(8,128)(2,1)S(1)} %shard_map.105), channel_id=1, replica_groups=mesh['gy'=2,'gx'=64] {'gx'}, dimensions={0} | all-to-all | bytes 1048576 | tf_op jit(solution)/shard_map/all_to_all | solution.py:456
  104.2 0.2 shard_map.107
  104.5 3.2 %collective-permute-start.3 = (bf16[16,256]{1,0:T(8,128)(2,1)S(1)}, bf16[16,256]{1,0:T(8,128)(2,1)S(1)}, u32[]{:S(2)}, u32[]{:S(2)}) collective-permute-start(bf16[16,256]{1,0:T(8,128)(2,1)S(1)} %shard_map.107), channel_id=1, source_target_pairs={{0,64},{64,0},{1,65},{65,1},{2,66},{66,2},{3,67},{67,3},{4,68},{68... | collective-permute-start | bytes 24584 | tf_op jit(solution)/shard_map/ppermute | solution.py:461
  107.6 3.4 %shard_map.106 = (bf16[2048,128]{1,0:T(8,128)(2,1)}, bf16[2048,256]{1,0:T(8,128)(2,1)S(1)}, bf16[128,256]{1,0:T(8,128)(2,1)S(1)}, bf16[128,256]{1,0:T(8,128)(2,1)S(1)}, bf16[2048,128]{1,0:T(8,128)(2,1)S(1)}) custom-call(bf16[2048,128]{1,0:T(8,128)(2,1)S(1)} %bitcast.20, bf16[2048,128]{1,0:T(8,128)(2,1)S(1)} %get-tuple-element.21.state.refs_1_, ...), custom_call_target="tpu_custom_call" | custom-call | flops 33554432 | bytes 12582912 | tf_op jit(solution)/shard_map/pallas_call | solution.py:462
  111.1 0.0 collective-permute-done.3.row_halo
  111.1 0.1 collective-permute-start.4
  111.2 3.8 %collective-permute-start.5 = (bf16[129,256]{1,0:T(8,128)(2,1)S(1)}, bf16[129,256]{1,0:T(8,128)(2,1)S(1)}, u32[]{:S(2)}, u32[]{:S(2)}) collective-permute-start(bf16[129,256]{1,0:T(8,128)(2,1)S(1)} %pad_maximum_fusion.3), channel_id=1, source_target_pairs={{1,2},{2,1},{3,4},{4,3},{5,6},{6,5},{7,8},{8,7},{9,10},{10,9},{11,... | collective-permute-start | bytes 198152 | tf_op jit(solution)/shard_map/ppermute | solution.py:409
  115.0 0.0 collective-permute-done.4.near
  115.0 4.9 %collective-permute-done.5.far = bf16[129,256]{1,0:T(8,128)(2,1)S(1)} collective-permute-done((bf16[129,256]{1,0:T(8,128)(2,1)S(1)}, bf16[129,256]{1,0:T(8,128)(2,1)S(1)}, u32[]{:S(2)}, u32[]{:S(2)}) %collective-permute-start.5) | collective-permute-done | bytes 66080 | tf_op jit(solution)/shard_map/ppermute | solution.py:409
  119.9 4.2 %shard_map.108 = (bf16[2048,128]{1,0:T(8,128)(2,1)}, bf16[2048,128]{1,0:T(8,128)(2,1)}) custom-call(bf16[2048,256]{1,0:T(8,128)(2,1)S(1)} %get-tuple-element.31.grads, bf16[16,256]{1,0:T(8,128)(2,1)S(1)} %collective-permute-done.3.row_halo, bf16[129,256]{1,0:T(8,128)(2,1)S(1)} %collective-permute-done.4.near, ...), custom_call_target="tpu_custom_call" | custom-call | tf_op jit(solution)/shard_map/pallas_call | solution.py:477
  (12 shorter events, 0.1 us)
Async XLA Ops:
  0.6 14.8 %copy-start.1 = (bf16[3,3,192,256]{3,2,1,0:T(8,128)(2,1)S(1)}, bf16[3,3,192,256]{3,2,1,0:T(8,128)(2,1)}, u32[]{:S(2)}) copy-start(bf16[3,3,192,256]{3,2,1,0:T(8,128)(2,1)} %weights.3) | copy-start | bytes 2654212
  1.5 5.2 %collective-permute-start = (bf16[16,256]{1,0:T(8,128)(2,1)S(1)}, bf16[16,256]{1,0:T(8,128)(2,1)S(1)}, u32[]{:S(2)}, u32[]{:S(2)}) collective-permute-start(bf16[16,256]{1,0:T(8,128)(2,1)S(1)} %maximum_select_fusion), channel_id=1, source_target_pairs={{0,64},{64,0},{1,65},{65,1},{2,66},{66,2},{3,67},{67,3},{4,68},{68... | collective-permute-start | bytes 24584 | tf_op jit(solution)/shard_map/ppermute | solution.py:397
  4.7 10.7 %copy-start = (bf16[128,16,128]{2,1,0:T(8,128)(2,1)S(1)}, bf16[128,16,128]{2,1,0:T(8,128)(2,1)}, u32[]{:S(2)}) copy-start(bf16[128,16,128]{2,1,0:T(8,128)(2,1)} %param.15) | copy-start | bytes 1572868
  6.8 8.6 %collective-permute-start.2 = (bf16[129,256]{1,0:T(8,128)(2,1)S(1)}, bf16[129,256]{1,0:T(8,128)(2,1)S(1)}, u32[]{:S(2)}, u32[]{:S(2)}) collective-permute-start(bf16[129,256]{1,0:T(8,128)(2,1)S(1)} %pad_maximum_fusion.1), channel_id=1, source_target_pairs={{1,2},{2,1},{3,4},{4,3},{5,6},{6,5},{7,8},{8,7},{9,10},{10,9},{11,... | collective-permute-start | bytes 198152 | tf_op jit(solution)/shard_map/ppermute | solution.py:409
  12.0 3.4 %collective-permute-start.1 = (bf16[129,256]{1,0:T(8,128)(2,1)S(1)}, bf16[129,256]{1,0:T(8,128)(2,1)S(1)}, u32[]{:S(2)}, u32[]{:S(2)}) collective-permute-start(bf16[129,256]{1,0:T(8,128)(2,1)S(1)} %pad_maximum_fusion), channel_id=1, source_target_pairs={{0,1},{1,0},{2,3},{3,2},{4,5},{5,4},{6,7},{7,6},{8,9},{9,8},{10,11... | collective-permute-start | bytes 198152 | tf_op jit(solution)/shard_map/ppermute | solution.py:408
  19.0 19.6 %copy-start.2 = (bf16[64,384]{1,0:T(8,128)(2,1)S(1)}, bf16[64,384]{1,0:T(8,128)(2,1)}, u32[]{:S(2)}) copy-start(bf16[64,384]{1,0:T(8,128)(2,1)} %w_qkv.1) | copy-start | bytes 147460
  19.0 19.6 %copy-start.3 = (bf16[128,64]{0,1:T(8,128)(2,1)S(1)}, bf16[128,64]{0,1:T(8,128)(2,1)}, u32[]{:S(2)}) copy-start(bf16[128,64]{0,1:T(8,128)(2,1)} %param.14) | copy-start | bytes 49156
  104.5 6.6 %collective-permute-start.3 = (bf16[16,256]{1,0:T(8,128)(2,1)S(1)}, bf16[16,256]{1,0:T(8,128)(2,1)S(1)}, u32[]{:S(2)}, u32[]{:S(2)}) collective-permute-start(bf16[16,256]{1,0:T(8,128)(2,1)S(1)} %shard_map.107), channel_id=1, source_target_pairs={{0,64},{64,0},{1,65},{65,1},{2,66},{66,2},{3,67},{67,3},{4,68},{68... | collective-permute-start | bytes 24584 | tf_op jit(solution)/shard_map/ppermute | solution.py:461
  111.1 3.9 %collective-permute-start.4 = (bf16[129,256]{1,0:T(8,128)(2,1)S(1)}, bf16[129,256]{1,0:T(8,128)(2,1)S(1)}, u32[]{:S(2)}, u32[]{:S(2)}) collective-permute-start(bf16[129,256]{1,0:T(8,128)(2,1)S(1)} %pad_maximum_fusion.2), channel_id=1, source_target_pairs={{0,1},{1,0},{2,3},{3,2},{4,5},{5,4},{6,7},{7,6},{8,9},{9,8},{10,11... | collective-permute-start | bytes 198152 | tf_op jit(solution)/shard_map/ppermute | solution.py:408
  111.2 8.6 %collective-permute-start.5 = (bf16[129,256]{1,0:T(8,128)(2,1)S(1)}, bf16[129,256]{1,0:T(8,128)(2,1)S(1)}, u32[]{:S(2)}, u32[]{:S(2)}) collective-permute-start(bf16[129,256]{1,0:T(8,128)(2,1)S(1)} %pad_maximum_fusion.3), channel_id=1, source_target_pairs={{1,2},{2,1},{3,4},{4,3},{5,6},{6,5},{7,8},{8,7},{9,10},{10,9},{11,... | collective-permute-start | bytes 198152 | tf_op jit(solution)/shard_map/ppermute | solution.py:409

commit v6 on v5

--- a/solution.py
+++ b/solution.py
@@ -19,14 +19,23 @@
     )
 
 
-def call(body, out_shape, scratch=(), in_place=(), count=0, vmem=24, cost=None):
+def call(body, out_shape, scratch=(), in_place=(), count=0, vmem=24, cost=None,
+         sent=()):
     spaces = [pltpu.HBM if index in in_place else pltpu.VMEM for index in range(count)]
+    out_specs = None
+    if sent:
+        out_specs = [
+            pl.BlockSpec(memory_space=pl.ANY if index in sent else pltpu.VMEM)
+            for index in range(len(out_shape))
+        ]
+    more = {} if out_specs is None else {"out_specs": tuple(out_specs)}
     return pl.pallas_call(
         body,
         out_shape=out_shape,
         in_specs=[pl.BlockSpec(memory_space=space) for space in spaces],
         scratch_shapes=list(scratch),
         cost_estimate=cost,
+        **more,
         compiler_params=pltpu.CompilerParams(vmem_limit_bytes=vmem << 20),
     )
 
@@ -356,7 +365,8 @@
 
 def all_grads(rows, cols, chunk):
     def body(back, state, state_grad, gain, sig_ref, mix_ref, cell_ref,
-             new_state, grads, near, far, c_grad):
+             new_state, grads, near, far, c_grad, new_here, sems):
+        copies = []
         near_at, far_at = sides(cols)
         count = chunk * cols
         width = state.shape[1]
@@ -365,18 +375,28 @@
             one, two, cell, new = gate_grads(
                 part, count, back, state, state_grad, gain, sig_ref, mix_ref, cell_ref
             )
-            new_state[part, :] = new.astype(BF16)
+            new_here[part, :] = new.astype(BF16)
+            copies.append(
+                pltpu.make_async_copy(
+                    new_here.at[part], new_state.at[part], sems.at[start // chunk]
+                )
+            )
+            copies[-1].start()
             c_grad[part, :] = cell.astype(BF16)
             for lanes, value in ((pl.ds(0, width), one), (pl.ds(width, width), two)):
                 grads[part, lanes] = value
                 near[pl.ds(start, chunk), lanes] = pick_column(value, cols, near_at)
                 far[pl.ds(start, chunk), lanes] = pick_column(value, cols, far_at)
+        for copy in copies:
+            copy.wait()
 
     return body
 
 
 def step_backward(rows, cols, chunk):
-    def body(grads, row_halo, near, far, weights, c_grad, grad_frame, grad_state, taps):
+    def body(grads, row_halo, near, far, weights, c_grad, frame_out, state_out,
+             taps, grad_frame, grad_state, frame_sems, state_sems):
+        copies = []
         fill_taps(taps, (grads,), row_halo, near, far, rows, cols, chunk)
         count = chunk * cols
         wide = grad_frame.shape[1]
@@ -388,6 +408,15 @@
             grad_frame[part, :] = total[:, :wide]
             grad_state[part, pl.ds(0, rest)] = total[:, wide:]
             grad_state[part, pl.ds(rest, rest)] = c_grad[part, pl.ds(rest, rest)]
+            index = start // chunk
+            for here, out, sems in (
+                (grad_frame, frame_out, frame_sems),
+                (grad_state, state_out, state_sems),
+            ):
+                copies.append(pltpu.make_async_copy(here.at[part], out.at[part], sems.at[index]))
+                copies[-1].start()
+        for copy in copies:
+            copy.wait()
 
     return body
 
@@ -430,6 +459,7 @@
     row_halo = swap_border(both(0), both(-1))
     sems = pltpu.SemaphoreType.DMA
     pieces = row_count // long_chunk
+    send_chunk = min(32, row_count)
     in_hbm = lambda array: pltpu.with_memory_space_constraint(array, pltpu.HBM)
     bias, gain = b_gates[None], norm_gain[None]
     near, far, radar, state, bias, gain = call(
@@ -468,17 +498,26 @@
             shape(row_count, gate_dim),
             shape(cells, 2 * hidden),
         ),
+        [vmem(state.shape, BF16), sems((pieces,))],
         count=7,
+        sent=(0,),
         cost=pl.CostEstimate(
             flops=64 * cells * gate_dim, transcendentals=4 * cells * hidden, bytes_accessed=24 * cells * gate_dim
         ),
     )(*operands)
     halo = exchange_columns(near, far, row_halo)
     grad_frame, grad_state = call(
-        step_backward(row_count, col_count, chunk),
+        step_backward(row_count, col_count, send_chunk),
         (shape(cells, in_channels), shape(cells, 2 * hidden)),
-        [vmem(((row_count + 2) * col_count, 3 * gate_dim), BF16)],
+        [
+            vmem(((row_count + 2) * col_count, 3 * gate_dim), BF16),
+            vmem((cells, in_channels), BF16),
+            vmem((cells, 2 * hidden), BF16),
+            sems((row_count // send_chunk,)),
+            sems((row_count // send_chunk,)),
+        ],
         count=6,
+        sent=(0, 1),
     )(grads, *halo, w_conv, c_grad)
     whole = lambda array: array.reshape(row_count, col_count, -1)
     return whole(new_state), whole(grad_frame), whole(grad_state)

time: 124 us -> 125 us (level)
  transfers between devices with their start and end apart: 6 -> 6, of which waited for: 2 -> 2; matrix products, arithmetic and copies ran while one was open for 0% -> 0% of each run, Pallas kernels for 4% -> 5%
where the time goes in v6:
time: 125 us; the launch traced here: 124 us
  Pallas kernels  62.2 us (50%)
  blocking collectives  36.5 us (29%)
  starting transfers between devices  15.6 us (12%)
  waiting for transfers between devices  8.21 us (7%)
    pallas_call x1, Pallas kernels, attend(): call(attention(length, block, group), jax.ShapeDtypeStruct(cells.shape, B...  48.7 us
    all_to_all x1, blocking collectives, on_device(): lax.all_to_all(send, 'gx', split_axis=0, concat_axis=0, tiled=True)  19.6 us
    all_to_all x1, blocking collectives, on_device(): lax.all_to_all(lines_out, 'gx', split_axis=0, concat_axis=0, tiled=True)  16.9 us
    ppermute x2, starting transfers between devices, exchange_columns(): far = lax.ppermute(jnp.concatenate([far, far_cell], axis=0), 'gx', swaps(1))  8.94 us
    ppermute x2, waiting for transfers between devices, exchange_columns(): far = lax.ppermute(jnp.concatenate([far, far_cell], axis=0), 'gx', swaps(1))  8.2 us
    pallas_call x1, Pallas kernels, on_device(): call(step_backward(row_count, col_count, send_chunk), (shape(cells, in_ch...  4.08 us
    pallas_call x1, Pallas kernels, on_device(): call(all_grads(row_count, col_count, long_chunk), (shape(cells, 2 * hidde...  3.65 us
    pallas_call x1, Pallas kernels, on_device(): call(step_forward(row_count, col_count, chunk), (shape(cells, 2 * hidden)...  3.59 us
  transfers between devices with their start and end apart: 6, of which 2 were waited for; matrix products, arithmetic and copies ran while one was open for 0% of the time, Pallas kernels for 5%

profile of v6, /device:TPU:2, one launch (start us, length us, event | category | flops | bytes accessed | tf_op | source)
XLA Modules:
  0.0 124.3 jit_solution(13593583172141013671)
XLA Ops:
  0.6 0.8 slice_bitcast_fusion
  1.5 3.3 %collective-permute-start = (bf16[16,256]{1,0:T(8,128)(2,1)S(1)}, bf16[16,256]{1,0:T(8,128)(2,1)S(1)}, u32[]{:S(2)}, u32[]{:S(2)}) collective-permute-start(bf16[16,256]{1,0:T(8,128)(2,1)S(1)} %maximum_select_fusion), channel_id=1, source_target_pairs={{0,64},{64,0},{1,65},{65,1},{2,66},{66,2},{3,67},{67,3},{4,68},{68... | collective-permute-start | bytes 24584 | tf_op jit(solution)/shard_map/ppermute | solution.py:426
  4.7 2.0 %shard_map.103 = (bf16[128,256]{1,0:T(8,128)(2,1)S(1)}, bf16[128,256]{1,0:T(8,128)(2,1)S(1)}, bf16[2048,128]{1,0:T(8,128)(2,1)S(1)}, bf16[2048,128]{1,0:T(8,128)...) custom-call(bf16[2048,128]{1,0:T(8,128)(2,1)} %bitcast.26, bf16[2048,128]{1,0:T(8,128)(2,1)} %bitcast.27, ...), custom_call_target="tpu_custom_call" | custom-call | tf_op jit(solution)/shard_map/pallas_call | solution.py:465
  6.7 0.0 collective-permute-done.row_halo
  6.8 5.2 %collective-permute-start.2 = (bf16[129,256]{1,0:T(8,128)(2,1)S(1)}, bf16[129,256]{1,0:T(8,128)(2,1)S(1)}, u32[]{:S(2)}, u32[]{:S(2)}) collective-permute-start(bf16[129,256]{1,0:T(8,128)(2,1)S(1)} %pad_maximum_fusion.1), channel_id=1, source_target_pairs={{1,2},{2,1},{3,4},{4,3},{5,6},{6,5},{7,8},{8,7},{9,10},{10,9},{11,... | collective-permute-start | bytes 198152 | tf_op jit(solution)/shard_map/ppermute | solution.py:438
  12.0 0.1 collective-permute-start.1
  12.1 3.3 %collective-permute-done.2.far = bf16[129,256]{1,0:T(8,128)(2,1)S(1)} collective-permute-done((bf16[129,256]{1,0:T(8,128)(2,1)S(1)}, bf16[129,256]{1,0:T(8,128)(2,1)S(1)}, u32[]{:S(2)}, u32[]{:S(2)}) %collective-permute-start.2) | collective-permute-done | bytes 66080 | tf_op jit(solution)/shard_map/ppermute | solution.py:438
  15.4 0.0 collective-permute-done.1.near
  15.4 0.0 copy-done
  15.4 3.6 %shard_map.104 = (bf16[2048,128]{1,0:T(8,128)(2,1)S(1)}, f32[2048,128]{1,0:T(8,128)S(1)}, f32[2048,128]{1,0:T(8,128)S(1)}, f32[2048,128]{1,0:T(8,128)S(1)}) custom-call(bf16[2048,128]{1,0:T(8,128)(2,1)S(1)} %get-tuple-element.20.radar, bf16[2048,128]{1,0:T(8,128)(2,1)S(1)} %get-tuple-element.21.state.refs_1_, ...), custom_call_target="tpu_custom_call" | custom-call | tf_op jit(solution)/shard_map/pallas_call | solution.py:475
  19.0 0.0 copy-start.2
  19.0 0.0 copy-start.3
  19.0 19.6 %all_to_all.10.cells = bf16[64,2,16,128]{3,2,1,0:T(8,128)(2,1)S(1)} all-to-all(bf16[64,2,16,128]{3,2,1,0:T(8,128)(2,1)S(1)} %bitcast.24), channel_id=1, replica_groups=mesh['gy'=2,'gx'=64] {'gx'}, dimensions={0} | all-to-all | bytes 1048576 | tf_op jit(solution)/shard_map/all_to_all | solution.py:484
  38.6 48.7 %shard_map.105 = bf16[64,2,16,128]{3,2,1,0:T(8,128)(2,1)S(1)} custom-call(bf16[64,2,16,128]{3,2,1,0:T(8,128)(2,1)S(1)} %all_to_all.10.cells, bf16[64,384]{1,0:T(8,128)(2,1)S(1)} %copy-done.2, bf16[64,128]{1,0:T(8,128)(2,1)S(1)} %bitcast.25), custom_call_target="tpu_custom_call" | custom-call | tf_op jit(solution)/shard_map/pallas_call | solution.py:301
  87.3 16.9 %all_to_all.11 = bf16[64,2,16,128]{3,2,1,0:T(8,128)(2,1)S(1)} all-to-all(bf16[64,2,16,128]{3,2,1,0:T(8,128)(2,1)S(1)} %shard_map.105), channel_id=1, replica_groups=mesh['gy'=2,'gx'=64] {'gx'}, dimensions={0} | all-to-all | bytes 1048576 | tf_op jit(solution)/shard_map/all_to_all | solution.py:486
  104.2 0.2 shard_map.107
  104.5 3.2 %collective-permute-start.3 = (bf16[16,256]{1,0:T(8,128)(2,1)S(1)}, bf16[16,256]{1,0:T(8,128)(2,1)S(1)}, u32[]{:S(2)}, u32[]{:S(2)}) collective-permute-start(bf16[16,256]{1,0:T(8,128)(2,1)S(1)} %shard_map.107), channel_id=1, source_target_pairs={{0,64},{64,0},{1,65},{65,1},{2,66},{66,2},{3,67},{67,3},{4,68},{68... | collective-permute-start | bytes 24584 | tf_op jit(solution)/shard_map/ppermute | solution.py:491
  107.6 3.6 %shard_map.106 = (bf16[2048,128]{1,0:T(8,128)(2,1)}, bf16[2048,256]{1,0:T(8,128)(2,1)S(1)}, bf16[128,256]{1,0:T(8,128)(2,1)S(1)}, bf16[128,256]{1,0:T(8,128)(2,1)S(1)}, bf16[2048,128]{1,0:T(8,128)(2,1)S(1)}) custom-call(bf16[2048,128]{1,0:T(8,128)(2,1)S(1)} %bitcast.20, bf16[2048,128]{1,0:T(8,128)(2,1)S(1)} %get-tuple-element.21.state.refs_1_, ...), custom_call_target="tpu_custom_call" | custom-call | flops 33554432 | bytes 12582912 | tf_op jit(solution)/shard_map/pallas_call | solution.py:492
  111.3 0.0 collective-permute-done.3.row_halo
  111.3 0.1 collective-permute-start.4
  111.4 3.7 %collective-permute-start.5 = (bf16[129,256]{1,0:T(8,128)(2,1)S(1)}, bf16[129,256]{1,0:T(8,128)(2,1)S(1)}, u32[]{:S(2)}, u32[]{:S(2)}) collective-permute-start(bf16[129,256]{1,0:T(8,128)(2,1)S(1)} %pad_maximum_fusion.3), channel_id=1, source_target_pairs={{1,2},{2,1},{3,4},{4,3},{5,6},{6,5},{7,8},{8,7},{9,10},{10,9},{11,... | collective-permute-start | bytes 198152 | tf_op jit(solution)/shard_map/ppermute | solution.py:438
  115.2 0.0 collective-permute-done.4.near
  115.2 4.9 %collective-permute-done.5.far = bf16[129,256]{1,0:T(8,128)(2,1)S(1)} collective-permute-done((bf16[129,256]{1,0:T(8,128)(2,1)S(1)}, bf16[129,256]{1,0:T(8,128)(2,1)S(1)}, u32[]{:S(2)}, u32[]{:S(2)}) %collective-permute-start.5) | collective-permute-done | bytes 66080 | tf_op jit(solution)/shard_map/ppermute | solution.py:438
  120.1 4.1 %shard_map.108 = (bf16[2048,128]{1,0:T(8,128)(2,1)}, bf16[2048,128]{1,0:T(8,128)(2,1)}) custom-call(bf16[2048,256]{1,0:T(8,128)(2,1)S(1)} %get-tuple-element.31.grads, bf16[16,256]{1,0:T(8,128)(2,1)S(1)} %collective-permute-done.3.row_halo, bf16[129,256]{1,0:T(8,128)(2,1)S(1)} %collective-permute-done.4.near, ...), custom_call_target="tpu_custom_call" | custom-call | tf_op jit(solution)/shard_map/pallas_call | solution.py:509
  (12 shorter events, 0.1 us)
Async XLA Ops:
  0.6 14.8 %copy-start.1 = (bf16[3,3,192,256]{3,2,1,0:T(8,128)(2,1)S(1)}, bf16[3,3,192,256]{3,2,1,0:T(8,128)(2,1)}, u32[]{:S(2)}) copy-start(bf16[3,3,192,256]{3,2,1,0:T(8,128)(2,1)} %weights.3) | copy-start | bytes 2654212
  1.5 5.2 %collective-permute-start = (bf16[16,256]{1,0:T(8,128)(2,1)S(1)}, bf16[16,256]{1,0:T(8,128)(2,1)S(1)}, u32[]{:S(2)}, u32[]{:S(2)}) collective-permute-start(bf16[16,256]{1,0:T(8,128)(2,1)S(1)} %maximum_select_fusion), channel_id=1, source_target_pairs={{0,64},{64,0},{1,65},{65,1},{2,66},{66,2},{3,67},{67,3},{4,68},{68... | collective-permute-start | bytes 24584 | tf_op jit(solution)/shard_map/ppermute | solution.py:426
  4.7 10.7 %copy-start = (bf16[128,16,128]{2,1,0:T(8,128)(2,1)S(1)}, bf16[128,16,128]{2,1,0:T(8,128)(2,1)}, u32[]{:S(2)}) copy-start(bf16[128,16,128]{2,1,0:T(8,128)(2,1)} %param.15) | copy-start | bytes 1572868
  6.8 8.6 %collective-permute-start.2 = (bf16[129,256]{1,0:T(8,128)(2,1)S(1)}, bf16[129,256]{1,0:T(8,128)(2,1)S(1)}, u32[]{:S(2)}, u32[]{:S(2)}) collective-permute-start(bf16[129,256]{1,0:T(8,128)(2,1)S(1)} %pad_maximum_fusion.1), channel_id=1, source_target_pairs={{1,2},{2,1},{3,4},{4,3},{5,6},{6,5},{7,8},{8,7},{9,10},{10,9},{11,... | collective-permute-start | bytes 198152 | tf_op jit(solution)/shard_map/ppermute | solution.py:438
  12.0 3.4 %collective-permute-start.1 = (bf16[129,256]{1,0:T(8,128)(2,1)S(1)}, bf16[129,256]{1,0:T(8,128)(2,1)S(1)}, u32[]{:S(2)}, u32[]{:S(2)}) collective-permute-start(bf16[129,256]{1,0:T(8,128)(2,1)S(1)} %pad_maximum_fusion), channel_id=1, source_target_pairs={{0,1},{1,0},{2,3},{3,2},{4,5},{5,4},{6,7},{7,6},{8,9},{9,8},{10,11... | collective-permute-start | bytes 198152 | tf_op jit(solution)/shard_map/ppermute | solution.py:437
  19.0 19.6 %copy-start.2 = (bf16[64,384]{1,0:T(8,128)(2,1)S(1)}, bf16[64,384]{1,0:T(8,128)(2,1)}, u32[]{:S(2)}) copy-start(bf16[64,384]{1,0:T(8,128)(2,1)} %w_qkv.1) | copy-start | bytes 147460
  19.0 19.6 %copy-start.3 = (bf16[128,64]{0,1:T(8,128)(2,1)S(1)}, bf16[128,64]{0,1:T(8,128)(2,1)}, u32[]{:S(2)}) copy-start(bf16[128,64]{0,1:T(8,128)(2,1)} %param.14) | copy-start | bytes 49156
  104.5 6.8 %collective-permute-start.3 = (bf16[16,256]{1,0:T(8,128)(2,1)S(1)}, bf16[16,256]{1,0:T(8,128)(2,1)S(1)}, u32[]{:S(2)}, u32[]{:S(2)}) collective-permute-start(bf16[16,256]{1,0:T(8,128)(2,1)S(1)} %shard_map.107), channel_id=1, source_target_pairs={{0,64},{64,0},{1,65},{65,1},{2,66},{66,2},{3,67},{67,3},{4,68},{68... | collective-permute-start | bytes 24584 | tf_op jit(solution)/shard_map/ppermute | solution.py:491
  111.3 3.9 %collective-permute-start.4 = (bf16[129,256]{1,0:T(8,128)(2,1)S(1)}, bf16[129,256]{1,0:T(8,128)(2,1)S(1)}, u32[]{:S(2)}, u32[]{:S(2)}) collective-permute-start(bf16[129,256]{1,0:T(8,128)(2,1)S(1)} %pad_maximum_fusion.2), channel_id=1, source_target_pairs={{0,1},{1,0},{2,3},{3,2},{4,5},{5,4},{6,7},{7,6},{8,9},{9,8},{10,11... | collective-permute-start | bytes 198152 | tf_op jit(solution)/shard_map/ppermute | solution.py:437
  111.4 8.6 %collective-permute-start.5 = (bf16[129,256]{1,0:T(8,128)(2,1)S(1)}, bf16[129,256]{1,0:T(8,128)(2,1)S(1)}, u32[]{:S(2)}, u32[]{:S(2)}) collective-permute-start(bf16[129,256]{1,0:T(8,128)(2,1)S(1)} %pad_maximum_fusion.3), channel_id=1, source_target_pairs={{1,2},{2,1},{3,4},{4,3},{5,6},{6,5},{7,8},{8,7},{9,10},{10,9},{11,... | collective-permute-start | bytes 198152 | tf_op jit(solution)/shard_map/ppermute | solution.py:438

commit v7 on v5

--- a/solution.py
+++ b/solution.py
@@ -416,7 +416,7 @@
     gate_dim = w_conv.shape[3]
     attn_dim = w_out.shape[0]
     cells = row_count * col_count
-    chunk, long_chunk = min(16, row_count), min(64, row_count)
+    chunk, long_chunk = min(16, row_count), min(128, row_count)
     lines = row_count // lax.axis_size("gx")
     shape = lambda *dims: jax.ShapeDtypeStruct(dims, BF16)
     wide = lambda *dims: jax.ShapeDtypeStruct(dims, F32)

time: 124 us -> 125 us (level)
  transfers between devices with their start and end apart: 6 -> 6, of which waited for: 2 -> 2; matrix products, arithmetic and copies ran while one was open for 0% -> 0% of each run, Pallas kernels for 4% -> 5%
where the time goes in v7:
time: 125 us
  Pallas kernels  62.8 us (50%)
  blocking collectives  36.5 us (29%)
  starting transfers between devices  15.5 us (12%)
  waiting for transfers between devices  8.21 us (7%)
    pallas_call x1, Pallas kernels, attend(): call(attention(length, block, group), jax.ShapeDtypeStruct(cells.shape, B...  48.7 us
    all_to_all x1, blocking collectives, on_device(): lax.all_to_all(send, 'gx', split_axis=0, concat_axis=0, tiled=True)  19.6 us
    all_to_all x1, blocking collectives, on_device(): lax.all_to_all(lines_out, 'gx', split_axis=0, concat_axis=0, tiled=True)  16.9 us
    ppermute x2, starting transfers between devices, exchange_columns(): far = lax.ppermute(jnp.concatenate([far, far_cell], axis=0), 'gx', swaps(1))  8.94 us
    ppermute x2, waiting for transfers between devices, exchange_columns(): far = lax.ppermute(jnp.concatenate([far, far_cell], axis=0), 'gx', swaps(1))  8.19 us
    pallas_call x1, Pallas kernels, on_device(): call(step_backward(row_count, col_count, chunk), (shape(cells, in_channel...  4.16 us
    pallas_call x1, Pallas kernels, on_device(): call(all_grads(row_count, col_count, long_chunk), (shape(cells, 2 * hidde...  4.07 us
    pallas_call x1, Pallas kernels, on_device(): call(step_forward(row_count, col_count, chunk), (shape(cells, 2 * hidden)...  3.59 us
  transfers between devices with their start and end apart: 6, of which 2 were waited for; matrix products, arithmetic and copies ran while one was open for 0% of the time, Pallas kernels for 5%

profile of v7, /device:TPU:2, one launch (start us, length us, event | category | flops | bytes accessed | tf_op | source)
XLA Modules:
  0.0 124.6 jit_solution(15132982397120954069)
XLA Ops:
  0.6 0.8 slice_bitcast_fusion
  1.5 3.3 %collective-permute-start = (bf16[16,256]{1,0:T(8,128)(2,1)S(1)}, bf16[16,256]{1,0:T(8,128)(2,1)S(1)}, u32[]{:S(2)}, u32[]{:S(2)}) collective-permute-start(bf16[16,256]{1,0:T(8,128)(2,1)S(1)} %maximum_select_fusion), channel_id=1, source_target_pairs={{0,64},{64,0},{1,65},{65,1},{2,66},{66,2},{3,67},{67,3},{4,68},{68... | collective-permute-start | bytes 24584 | tf_op jit(solution)/shard_map/ppermute | solution.py:397
  4.7 2.0 %shard_map.103 = (bf16[128,256]{1,0:T(8,128)(2,1)S(1)}, bf16[128,256]{1,0:T(8,128)(2,1)S(1)}, bf16[2048,128]{1,0:T(8,128)(2,1)S(1)}, bf16[2048,128]{1,0:T(8,128)...) custom-call(bf16[2048,128]{1,0:T(8,128)(2,1)} %bitcast.26, bf16[2048,128]{1,0:T(8,128)(2,1)} %bitcast.27, ...), custom_call_target="tpu_custom_call" | custom-call | tf_op jit(solution)/shard_map/pallas_call | solution.py:435
  6.8 0.0 collective-permute-done.row_halo
  6.8 5.2 %collective-permute-start.2 = (bf16[129,256]{1,0:T(8,128)(2,1)S(1)}, bf16[129,256]{1,0:T(8,128)(2,1)S(1)}, u32[]{:S(2)}, u32[]{:S(2)}) collective-permute-start(bf16[129,256]{1,0:T(8,128)(2,1)S(1)} %pad_maximum_fusion.1), channel_id=1, source_target_pairs={{1,2},{2,1},{3,4},{4,3},{5,6},{6,5},{7,8},{8,7},{9,10},{10,9},{11,... | collective-permute-start | bytes 198152 | tf_op jit(solution)/shard_map/ppermute | solution.py:409
  12.1 0.1 collective-permute-start.1
  12.2 3.3 %collective-permute-done.2.far = bf16[129,256]{1,0:T(8,128)(2,1)S(1)} collective-permute-done((bf16[129,256]{1,0:T(8,128)(2,1)S(1)}, bf16[129,256]{1,0:T(8,128)(2,1)S(1)}, u32[]{:S(2)}, u32[]{:S(2)}) %collective-permute-start.2) | collective-permute-done | bytes 66080 | tf_op jit(solution)/shard_map/ppermute | solution.py:409
  15.5 0.0 collective-permute-done.1.near
  15.5 0.0 copy-done
  15.5 3.6 %shard_map.104 = (bf16[2048,128]{1,0:T(8,128)(2,1)S(1)}, f32[2048,128]{1,0:T(8,128)S(1)}, f32[2048,128]{1,0:T(8,128)S(1)}, f32[2048,128]{1,0:T(8,128)S(1)}) custom-call(bf16[2048,128]{1,0:T(8,128)(2,1)S(1)} %get-tuple-element.20.radar, bf16[2048,128]{1,0:T(8,128)(2,1)S(1)} %get-tuple-element.21.state.refs_1_, ...), custom_call_target="tpu_custom_call" | custom-call | tf_op jit(solution)/shard_map/pallas_call | solution.py:445
  19.1 0.0 copy-start.2
  19.1 0.0 copy-start.3
  19.1 19.6 %all_to_all.10.cells = bf16[64,2,16,128]{3,2,1,0:T(8,128)(2,1)S(1)} all-to-all(bf16[64,2,16,128]{3,2,1,0:T(8,128)(2,1)S(1)} %bitcast.24), channel_id=1, replica_groups=mesh['gy'=2,'gx'=64] {'gx'}, dimensions={0} | all-to-all | bytes 1048576 | tf_op jit(solution)/shard_map/all_to_all | solution.py:454
  38.7 48.7 %shard_map.105 = bf16[64,2,16,128]{3,2,1,0:T(8,128)(2,1)S(1)} custom-call(bf16[64,2,16,128]{3,2,1,0:T(8,128)(2,1)S(1)} %all_to_all.10.cells, bf16[64,384]{1,0:T(8,128)(2,1)S(1)} %copy-done.2, bf16[64,128]{1,0:T(8,128)(2,1)S(1)} %bitcast.25), custom_call_target="tpu_custom_call" | custom-call | tf_op jit(solution)/shard_map/pallas_call | solution.py:292
  87.4 16.9 %all_to_all.11 = bf16[64,2,16,128]{3,2,1,0:T(8,128)(2,1)S(1)} all-to-all(bf16[64,2,16,128]{3,2,1,0:T(8,128)(2,1)S(1)} %shard_map.105), channel_id=1, replica_groups=mesh['gy'=2,'gx'=64] {'gx'}, dimensions={0} | all-to-all | bytes 1048576 | tf_op jit(solution)/shard_map/all_to_all | solution.py:456
  104.3 0.2 shard_map.107
  104.5 3.1 %collective-permute-start.3 = (bf16[16,256]{1,0:T(8,128)(2,1)S(1)}, bf16[16,256]{1,0:T(8,128)(2,1)S(1)}, u32[]{:S(2)}, u32[]{:S(2)}) collective-permute-start(bf16[16,256]{1,0:T(8,128)(2,1)S(1)} %shard_map.107), channel_id=1, source_target_pairs={{0,64},{64,0},{1,65},{65,1},{2,66},{66,2},{3,67},{67,3},{4,68},{68... | collective-permute-start | bytes 24584 | tf_op jit(solution)/shard_map/ppermute | solution.py:461
  107.6 4.1 %shard_map.106 = (bf16[2048,128]{1,0:T(8,128)(2,1)}, bf16[2048,256]{1,0:T(8,128)(2,1)S(1)}, bf16[128,256]{1,0:T(8,128)(2,1)S(1)}, bf16[128,256]{1,0:T(8,128)(2,1)S(1)}, bf16[2048,128]{1,0:T(8,128)(2,1)S(1)}) custom-call(bf16[2048,128]{1,0:T(8,128)(2,1)S(1)} %bitcast.20, bf16[2048,128]{1,0:T(8,128)(2,1)S(1)} %get-tuple-element.21.state.refs_1_, ...), custom_call_target="tpu_custom_call" | custom-call | flops 33554432 | bytes 12582912 | tf_op jit(solution)/shard_map/pallas_call | solution.py:462
  111.7 0.0 collective-permute-done.3.row_halo
  111.7 0.1 collective-permute-start.4
  111.8 3.8 %collective-permute-start.5 = (bf16[129,256]{1,0:T(8,128)(2,1)S(1)}, bf16[129,256]{1,0:T(8,128)(2,1)S(1)}, u32[]{:S(2)}, u32[]{:S(2)}) collective-permute-start(bf16[129,256]{1,0:T(8,128)(2,1)S(1)} %pad_maximum_fusion.3), channel_id=1, source_target_pairs={{1,2},{2,1},{3,4},{4,3},{5,6},{6,5},{7,8},{8,7},{9,10},{10,9},{11,... | collective-permute-start | bytes 198152 | tf_op jit(solution)/shard_map/ppermute | solution.py:409
  115.6 0.0 collective-permute-done.4.near
  115.6 4.9 %collective-permute-done.5.far = bf16[129,256]{1,0:T(8,128)(2,1)S(1)} collective-permute-done((bf16[129,256]{1,0:T(8,128)(2,1)S(1)}, bf16[129,256]{1,0:T(8,128)(2,1)S(1)}, u32[]{:S(2)}, u32[]{:S(2)}) %collective-permute-start.5) | collective-permute-done | bytes 66080 | tf_op jit(solution)/shard_map/ppermute | solution.py:409
  120.5 4.2 %shard_map.108 = (bf16[2048,128]{1,0:T(8,128)(2,1)}, bf16[2048,128]{1,0:T(8,128)(2,1)}) custom-call(bf16[2048,256]{1,0:T(8,128)(2,1)S(1)} %get-tuple-element.31.grads, bf16[16,256]{1,0:T(8,128)(2,1)S(1)} %collective-permute-done.3.row_halo, bf16[129,256]{1,0:T(8,128)(2,1)S(1)} %collective-permute-done.4.near, ...), custom_call_target="tpu_custom_call" | custom-call | tf_op jit(solution)/shard_map/pallas_call | solution.py:477
  (12 shorter events, 0.1 us)
Async XLA Ops:
  0.6 14.9 %copy-start.1 = (bf16[3,3,192,256]{3,2,1,0:T(8,128)(2,1)S(1)}, bf16[3,3,192,256]{3,2,1,0:T(8,128)(2,1)}, u32[]{:S(2)}) copy-start(bf16[3,3,192,256]{3,2,1,0:T(8,128)(2,1)} %weights.3) | copy-start | bytes 2654212
  1.5 5.3 %collective-permute-start = (bf16[16,256]{1,0:T(8,128)(2,1)S(1)}, bf16[16,256]{1,0:T(8,128)(2,1)S(1)}, u32[]{:S(2)}, u32[]{:S(2)}) collective-permute-start(bf16[16,256]{1,0:T(8,128)(2,1)S(1)} %maximum_select_fusion), channel_id=1, source_target_pairs={{0,64},{64,0},{1,65},{65,1},{2,66},{66,2},{3,67},{67,3},{4,68},{68... | collective-permute-start | bytes 24584 | tf_op jit(solution)/shard_map/ppermute | solution.py:397
  4.7 10.7 %copy-start = (bf16[128,16,128]{2,1,0:T(8,128)(2,1)S(1)}, bf16[128,16,128]{2,1,0:T(8,128)(2,1)}, u32[]{:S(2)}) copy-start(bf16[128,16,128]{2,1,0:T(8,128)(2,1)} %param.15) | copy-start | bytes 1572868
  6.8 8.6 %collective-permute-start.2 = (bf16[129,256]{1,0:T(8,128)(2,1)S(1)}, bf16[129,256]{1,0:T(8,128)(2,1)S(1)}, u32[]{:S(2)}, u32[]{:S(2)}) collective-permute-start(bf16[129,256]{1,0:T(8,128)(2,1)S(1)} %pad_maximum_fusion.1), channel_id=1, source_target_pairs={{1,2},{2,1},{3,4},{4,3},{5,6},{6,5},{7,8},{8,7},{9,10},{10,9},{11,... | collective-permute-start | bytes 198152 | tf_op jit(solution)/shard_map/ppermute | solution.py:409
  12.1 3.4 %collective-permute-start.1 = (bf16[129,256]{1,0:T(8,128)(2,1)S(1)}, bf16[129,256]{1,0:T(8,128)(2,1)S(1)}, u32[]{:S(2)}, u32[]{:S(2)}) collective-permute-start(bf16[129,256]{1,0:T(8,128)(2,1)S(1)} %pad_maximum_fusion), channel_id=1, source_target_pairs={{0,1},{1,0},{2,3},{3,2},{4,5},{5,4},{6,7},{7,6},{8,9},{9,8},{10,11... | collective-permute-start | bytes 198152 | tf_op jit(solution)/shard_map/ppermute | solution.py:408
  19.1 19.6 %copy-start.2 = (bf16[64,384]{1,0:T(8,128)(2,1)S(1)}, bf16[64,384]{1,0:T(8,128)(2,1)}, u32[]{:S(2)}) copy-start(bf16[64,384]{1,0:T(8,128)(2,1)} %w_qkv.1) | copy-start | bytes 147460
  19.1 19.6 %copy-start.3 = (bf16[128,64]{0,1:T(8,128)(2,1)S(1)}, bf16[128,64]{0,1:T(8,128)(2,1)}, u32[]{:S(2)}) copy-start(bf16[128,64]{0,1:T(8,128)(2,1)} %param.14) | copy-start | bytes 49156
  104.5 7.2 %collective-permute-start.3 = (bf16[16,256]{1,0:T(8,128)(2,1)S(1)}, bf16[16,256]{1,0:T(8,128)(2,1)S(1)}, u32[]{:S(2)}, u32[]{:S(2)}) collective-permute-start(bf16[16,256]{1,0:T(8,128)(2,1)S(1)} %shard_map.107), channel_id=1, source_target_pairs={{0,64},{64,0},{1,65},{65,1},{2,66},{66,2},{3,67},{67,3},{4,68},{68... | collective-permute-start | bytes 24584 | tf_op jit(solution)/shard_map/ppermute | solution.py:461
  111.7 3.9 %collective-permute-start.4 = (bf16[129,256]{1,0:T(8,128)(2,1)S(1)}, bf16[129,256]{1,0:T(8,128)(2,1)S(1)}, u32[]{:S(2)}, u32[]{:S(2)}) collective-permute-start(bf16[129,256]{1,0:T(8,128)(2,1)S(1)} %pad_maximum_fusion.2), channel_id=1, source_target_pairs={{0,1},{1,0},{2,3},{3,2},{4,5},{5,4},{6,7},{7,6},{8,9},{9,8},{10,11... | collective-permute-start | bytes 198152 | tf_op jit(solution)/shard_map/ppermute | solution.py:408
  111.8 8.6 %collective-permute-start.5 = (bf16[129,256]{1,0:T(8,128)(2,1)S(1)}, bf16[129,256]{1,0:T(8,128)(2,1)S(1)}, u32[]{:S(2)}, u32[]{:S(2)}) collective-permute-start(bf16[129,256]{1,0:T(8,128)(2,1)S(1)} %pad_maximum_fusion.3), channel_id=1, source_target_pairs={{1,2},{2,1},{3,4},{4,3},{5,6},{6,5},{7,8},{8,7},{9,10},{10,9},{11,... | collective-permute-start | bytes 198152 | tf_op jit(solution)/shard_map/ppermute | solution.py:409
